TPU v7x, 32 devices: a whole 2x2x4 slice. The times are simulated.
32 devices in a mesh: dp: 4 (over y, x), section: 4 (over z), mp: 2 (over core).
Axes of the slice: x: 2, y: 2, z: 4, core: 2. Of those that a mesh axis runs over, the one named last changes fastest.
Arguments:
- enc_rows: bfloat16 [4, 1024, 4096], P('dp', ('section', 'mp')), may hold values from -6 to 6
- pack_index: int32 [4, 1024], P('dp'), may hold values from 0 to 1023, each once within a row
- enc_segments: int32 [4, 1024], P('dp'), may hold values from 0 to 3, never falling along the last dimension, each value on 1 to 512 neighbouring positions
- dec_segments: int32 [4, 256], P('dp'), may hold values from 0 to 3, never falling along the last dimension, each value on 1 to 128 neighbouring positions
- dec_inputs: bfloat16 [4, 4, 256, 4096], P('dp', 'section', 'mp'), may hold values from -6 to 6
- norm_gain: bfloat16 [4, 4096], P('section'), may hold values from 0.099609375 to 1.8984375
- w_query: bfloat16 [4, 4096, 2048], P('section', None, 'mp'), may hold values from -0.09375 to 0.09375
- w_key: bfloat16 [4, 4096, 2048], P('section', None, 'mp'), may hold values from -0.09375 to 0.09375
- w_value: bfloat16 [4, 4096, 2048], P('section', None, 'mp'), may hold values from -0.09375 to 0.09375
- w_out: bfloat16 [4, 2048, 4096], P('section', 'mp'), may hold values from -0.125 to 0.125
- cotangent: bfloat16 [4, 256, 4096], P('dp', 'mp'), may hold values from -6 to 6
Outputs:
- dec_grads: bfloat16 [4, 4, 256, 4096], P('dp', 'section', 'mp')
- enc_grads: float32 [4, 1024, 4096], P('dp', ('section', 'mp'))
Inputs may be any that keep to these rules, and one draw needn't show every extreme that they name: `dec_segments`: every sequence id of a group occurs among both its decoder tokens and its packed encoder positions.
All inputs are finite; a program needn't handle non-finite values.
Results may differ from a plain program's by a relative error of at most 0.024.
Values may be sent and summed in bfloat16 or wider, within the bound.
No kernel may reach another device: no remote copies, remote signals or barrier semaphores. Data moves between devices by JAX's collectives and lax.ppermute only.
A program may use at most 192 MiB of HBM per device.

v0:
```python
import jax
import jax.numpy as jnp
from jax import lax
from jax.sharding import PartitionSpec as P

HD = 64
MICRO = 4


epsilon = 1e-06
masked_value = -1e30


def passed_along(x, axis, by):
    count = lax.axis_size(axis)
    pairs = [(i, i + by) for i in range(count) if 0 <= i + by < count]
    return lax.ppermute(x, axis, pairs)


def on_device(
    enc_rows,
    pack_index,
    enc_segments,
    dec_segments,
    dec_inputs,
    norm_gain,
    w_query,
    w_key,
    w_value,
    w_out,
    cotangent,
):
    query_weight = w_query[0]
    key_weight = w_key[0]
    value_weight = w_value[0]
    out_weight = w_out[0]
    norm_scale = norm_gain[0].astype(jnp.float32)
    width = query_weight.shape[1]
    heads_here = width // HD
    scale_factor = HD ** (-0.5)
    mp_parts = lax.axis_size("mp")
    phase_count = lax.axis_size("section")
    mp_place = lax.axis_index("mp")
    phase_place = lax.axis_index("section")
    rows_here = lax.all_gather(enc_rows, ("section", "mp"), axis=1, tiled=True)[0]
    key_part = jnp.dot(rows_here, key_weight, preferred_element_type=jnp.float32).astype(
        jnp.bfloat16
    )
    value_part = jnp.dot(rows_here, value_weight, preferred_element_type=jnp.float32).astype(
        jnp.bfloat16
    )
    projected = jnp.concatenate([key_part, value_part], axis=1)[None][0]
    packing = pack_index[0]
    projected = jnp.take(projected, packing, axis=0)
    enc_count = projected.shape[0]
    key_heads = projected[:, :width].reshape(enc_count, heads_here, HD)
    value_heads = projected[:, width:].reshape(enc_count, heads_here, HD)
    enc_ids = enc_segments[0]
    inputs = lax.all_gather(dec_inputs, "mp", axis=2, tiled=True)[0, 0].astype(jnp.float32)
    token_count = inputs.shape[0]
    model_width = inputs.shape[1]
    recip = lax.rsqrt(jnp.mean(inputs * inputs, axis=-1, keepdims=True) + epsilon)
    unit = inputs * recip
    normed = (unit * norm_scale).astype(jnp.bfloat16)
    queries = jnp.dot(normed, query_weight, preferred_element_type=jnp.float32).astype(jnp.bfloat16)
    micro_count = MICRO
    share_rows = token_count // (mp_parts * micro_count)
    row_count = share_rows * mp_parts

    def split_blocks(array):
        return array.reshape((mp_parts, micro_count, share_rows) + array.shape[1:])

    query_blocks = split_blocks(queries)
    unit_blocks = split_blocks(unit)
    recip_blocks = split_blocks(recip)
    segment_blocks = split_blocks(dec_segments[0])
    upstream_blocks = split_blocks(lax.all_gather(cotangent, "mp", axis=1, tiled=True)[0])

    def select_block(blocks_in, block_index):
        picked = lax.dynamic_index_in_dim(blocks_in, block_index, 1, keepdims=False)
        return picked.reshape((row_count,) + blocks_in.shape[3:])

    def norm_back(upstream, summed, unit_rows, recip_rows):
        scaled = summed * norm_scale
        result = upstream.astype(jnp.float32) + recip_rows * (
            scaled - unit_rows * jnp.mean(scaled * unit_rows, axis=-1, keepdims=True)
        )
        return result.astype(jnp.bfloat16)

    def advance(turn_index, current_state):
        incoming, key_grad, value_grad, layer_grads = current_state
        micro_index = turn_index - (phase_count - 1 - phase_place)
        is_valid = (micro_index >= 0) & (micro_index < micro_count)
        block_index = jnp.clip(micro_index, 0, micro_count - 1)
        is_last = phase_place == phase_count - 1
        upstream = jnp.where(is_last, select_block(upstream_blocks, block_index), incoming)
        attn_grad = jnp.einsum(
            "rd,cd->rc", upstream, out_weight, preferred_element_type=jnp.float32
        ).astype(jnp.bfloat16)
        attn_grad = attn_grad.reshape(row_count, heads_here, HD)
        query_rows = select_block(query_blocks, block_index).reshape(row_count, heads_here, HD)
        allowed = select_block(segment_blocks, block_index)[:, None] == enc_ids[None, :]
        scores = (
            jnp.einsum("qhd,khd->hqk", query_rows, key_heads, preferred_element_type=jnp.float32)
            * scale_factor
        )
        scores = jnp.where(allowed[None], scores, masked_value)
        attention = jax.nn.softmax(scores, axis=-1)
        attention_low = attention.astype(jnp.bfloat16)
        prob_grad = jnp.einsum(
            "qhd,khd->hqk", attn_grad, value_heads, preferred_element_type=jnp.float32
        )
        score_grad = (
            attention
            * (prob_grad - jnp.sum(prob_grad * attention, axis=-1, keepdims=True))
            * scale_factor
        ).astype(jnp.bfloat16)
        query_grad = jnp.einsum(
            "hqk,khd->qhd", score_grad, key_heads, preferred_element_type=jnp.float32
        ).astype(jnp.bfloat16)
        query_grad = query_grad.reshape(row_count, width)
        keep_mask = is_valid.astype(jnp.float32)
        key_grad = key_grad + keep_mask * jnp.einsum(
            "hqk,qhd->khd", score_grad, query_rows, preferred_element_type=jnp.float32
        )
        value_grad = value_grad + keep_mask * jnp.einsum(
            "hqk,qhd->khd", attention_low, attn_grad, preferred_element_type=jnp.float32
        )
        partial_grad = jnp.einsum(
            "rc,dc->rd", query_grad, query_weight, preferred_element_type=jnp.float32
        )
        summed = lax.psum(partial_grad.astype(jnp.bfloat16), "mp").astype(jnp.float32)
        whole = norm_back(
            upstream,
            summed,
            select_block(unit_blocks, block_index),
            select_block(recip_blocks, block_index),
        )
        mine = lax.dynamic_index_in_dim(
            whole.reshape(mp_parts, share_rows, model_width), mp_place, 0, keepdims=False
        )
        passed = passed_along(whole, "section", -1)
        previous = lax.dynamic_index_in_dim(layer_grads, block_index, 0, keepdims=False)
        layer_grads = lax.dynamic_update_index_in_dim(
            layer_grads, jnp.where(is_valid, mine, previous), block_index, 0
        )
        return (passed, key_grad, value_grad, layer_grads)

    start_rows = jnp.zeros((row_count, model_width), jnp.bfloat16)
    initial = (
        start_rows,
        jnp.zeros((enc_count, heads_here, HD), jnp.float32),
        jnp.zeros((enc_count, heads_here, HD), jnp.float32),
        jnp.zeros((micro_count, share_rows, model_width), jnp.bfloat16),
    )
    final_state = lax.fori_loop(0, phase_count + micro_count - 1, advance, initial)
    key_low = final_state[1].astype(jnp.bfloat16).reshape(enc_count, width)
    value_low = final_state[2].astype(jnp.bfloat16).reshape(enc_count, width)
    layer_grads = final_state[3]
    inverse = (
        jnp.zeros((enc_count,), jnp.int32).at[packing].set(jnp.arange(enc_count, dtype=jnp.int32))
    )
    picked = inverse
    key_part = jnp.take(key_low, picked, axis=0)
    value_part = jnp.take(value_low, picked, axis=0)
    result = jnp.einsum("rc,dc->rd", key_part, key_weight, preferred_element_type=jnp.float32)
    enc_share = lax.psum_scatter(
        (
            result
            + jnp.einsum("rc,dc->rd", value_part, value_weight, preferred_element_type=jnp.float32)
        ).astype(jnp.bfloat16),
        ("section", "mp"),
        scatter_dimension=0,
        tiled=True,
    ).astype(jnp.float32)
    return (layer_grads.reshape(1, 1, micro_count * share_rows, model_width), enc_share[None])


def solution(mesh):
    in_specs = (
        P("dp", ("section", "mp"), None),
        P("dp", None),
        P("dp", None),
        P("dp", None),
        P("dp", "section", "mp", None),
        P("section", None),
        P("section", None, "mp"),
        P("section", None, "mp"),
        P("section", None, "mp"),
        P("section", "mp", None),
        P("dp", "mp", None),
    )
    out_specs = (P("dp", "section", "mp", None), P("dp", ("section", "mp"), None))
    return jax.shard_map(
        on_device, mesh=mesh, in_specs=in_specs, out_specs=out_specs, check_vma=False
    )
```

profile of v0, /device:TPU:0, one launch (start us, length us, event | category | flops | bytes accessed | tf_op | source)
XLA Modules:
  0.0 884.4 jit_solution(1912103485543909097)
XLA Ops:
  35.4 72.3 %all-gather.8.cloned.1.call-done = bf16[1,1024,4096]{2,1,0:T(8,128)(2,1)} async-done(((bf16[1,128,4096]{2,1,0:T(8,128)(2,1)}), bf16[1,1024,4096]{2,1,0:T(8,128)(2,1)}) %all-gather.8.cloned.1.call-update) | async-done | bytes 8388624 | tf_op jit(solution)/shard_map/all_gather | solution.py:45
  107.7 14.1 %fusion.61 = bf16[1024,1024]{0,1:T(8,128)(2,1)S(1)} fusion(bf16[1,4096,1024]{2,1,0:T(8,128)(2,1)} %param.22, bf16[1,1024,4096]{2,1,0:T(8,128)(2,1)} %all-gather.8.cloned.1.call-done), kind=kOutput, calls=%fused_computation.76 | convolution fusion | flops 8590983168 | bytes 18874368 | tf_op jit(solution)/shard_map/dot_general | solution.py:46
  121.8 13.8 %fusion.66 = bf16[1024,1024]{0,1:T(8,128)(2,1)S(1)} fusion(bf16[1,4096,1024]{2,1,0:T(8,128)(2,1)} %param.23, bf16[1,1024,4096]{2,1,0:T(8,128)(2,1)} %all-gather.8.cloned.1.call-done), kind=kOutput, calls=%fused_computation.77 | convolution fusion | flops 8590983168 | bytes 18874368 | tf_op jit(solution)/shard_map/dot_general | solution.py:49
  144.5 11.6 %gather_fusion = bf16[1024,2048]{1,0:T(8,128)(2,1)} fusion(bf16[1024,2048]{1,0:T(8,128)(2,1)} %copy.26, s32[1024]{0:T(1024)S(1)} %broadcast_clamp_fusion), kind=kCustom, calls=%fused_computation.2 | custom fusion | bytes 8392704 | tf_op jit(solution)/shard_map/jit(_take)/gather | solution.py:54
  168.1 556.1 %while.22 = (s32[]{:T(128)}, bf16[64,4096]{1,0:T(8,128)(2,1)S(1)}, f32[1024,16,64]{0,2,1:T(8,128)}, f32[1024,16,64]{0,2,1:T(8,128)}, bf16[4,32,4096]{2,1,0:T(8,1...) while((s32[]{:T(128)}, bf16[64,4096]{1,0:T(8,128)(2,1)S(1)}, ...), condition=%wide.region_7.8_spmd.clone, body=%wide.region_1.7_spmd.clone.sunk | while | flops 1776358400 | bytes 87875976 | solution.py:156
  195.4 12.0 %fusion.133 = bf16[64,16,64]{2,0,1:T(8,128)(2,1)S(1)} fusion(bf16[1024,16,64]{0,2,1:T(8,128)(2,1)} %get-tuple-element.735, f32[16,64,1024]{2,1,0:T(8,128)} %fusion.131, f32[16,64,1024]{2,1,0:T(8,128)} %get-tuple-element.675, f32[16,64]{1,0:T(8,128)S(1)} %get-tuple-element.676), kind=kOutput, calls=%fused_computation.25.clone.1 | convolution fusion | flops 141625344 | bytes 10620928 | tf_op jit(solution)/shard_map/while/body/eval_jaxpr/hqk,khd->qhd/dot_general | solution.py:118
  207.8 6.9 convolution_convert_fusion.5
  221.3 10.7 %all-reduce.2.cloned.1.call-done = bf16[64,4096]{1,0:T(8,128)(2,1)} async-done(((bf16[64,4096]{1,0:T(8,128)(2,1)}), bf16[64,4096]{1,0:T(8,128)(2,1)}) %all-reduce.2.cloned.1.call-update) | async-done | bytes 524304 | tf_op jit(solution)/shard_map/while/body/eval_jaxpr/psum | solution.py:132
  236.1 13.7 %bitcast_add_fusion.4 = f32[1024,16,64]{0,2,1:T(8,128)} fusion(f32[1024,16,64]{0,2,1:T(8,128)} %get-tuple-element.702, f32[]{:T(128)S(6)} %convert_element_type.208, pred[]{:T(512)S(6)} %compare.3, bf16[64,16,64]{0,2,1:T(8,128)(2,1)S(1)} %copy.46, f32[16,64,1024]{2,1,0:T(8,128)} %fusion.131, f32[16,64,1024]{2,1,0:T(8,128)} %get-tuple-element.675, ...), kind=kOutput, calls=%fused_computation.8.clone.1 | convolution fusion | flops 144705536 | bytes 16912388 | tf_op jit(solution)/shard_map/while/body/eval_jaxpr/hqk,qhd->khd/dot_general | solution.py:123
  269.1 12.0 %fusion.133 = bf16[64,16,64]{2,0,1:T(8,128)(2,1)S(1)} fusion(bf16[1024,16,64]{0,2,1:T(8,128)(2,1)} %get-tuple-element.735, f32[16,64,1024]{2,1,0:T(8,128)} %fusion.131, f32[16,64,1024]{2,1,0:T(8,128)} %get-tuple-element.675, f32[16,64]{1,0:T(8,128)S(1)} %get-tuple-element.676), kind=kOutput, calls=%fused_computation.25.clone.1 | convolution fusion | flops 141625344 | bytes 10620928 | tf_op jit(solution)/shard_map/while/body/eval_jaxpr/hqk,khd->qhd/dot_general | solution.py:118
  296.1 13.4 %all-reduce.2.cloned.1.call-done = bf16[64,4096]{1,0:T(8,128)(2,1)} async-done(((bf16[64,4096]{1,0:T(8,128)(2,1)}), bf16[64,4096]{1,0:T(8,128)(2,1)}) %all-reduce.2.cloned.1.call-update) | async-done | bytes 524304 | tf_op jit(solution)/shard_map/while/body/eval_jaxpr/psum | solution.py:132
  313.7 14.8 %bitcast_add_fusion.4 = f32[1024,16,64]{0,2,1:T(8,128)} fusion(f32[1024,16,64]{0,2,1:T(8,128)} %get-tuple-element.702, f32[]{:T(128)S(6)} %convert_element_type.208, pred[]{:T(512)S(6)} %compare.3, bf16[64,16,64]{0,2,1:T(8,128)(2,1)S(1)} %copy.46, f32[16,64,1024]{2,1,0:T(8,128)} %fusion.131, f32[16,64,1024]{2,1,0:T(8,128)} %get-tuple-element.675, ...), kind=kOutput, calls=%fused_computation.8.clone.1 | convolution fusion | flops 144705536 | bytes 16912388 | tf_op jit(solution)/shard_map/while/body/eval_jaxpr/hqk,qhd->khd/dot_general | solution.py:123
  347.8 12.0 %fusion.133 = bf16[64,16,64]{2,0,1:T(8,128)(2,1)S(1)} fusion(bf16[1024,16,64]{0,2,1:T(8,128)(2,1)} %get-tuple-element.735, f32[16,64,1024]{2,1,0:T(8,128)} %fusion.131, f32[16,64,1024]{2,1,0:T(8,128)} %get-tuple-element.675, f32[16,64]{1,0:T(8,128)S(1)} %get-tuple-element.676), kind=kOutput, calls=%fused_computation.25.clone.1 | convolution fusion | flops 141625344 | bytes 10620928 | tf_op jit(solution)/shard_map/while/body/eval_jaxpr/hqk,khd->qhd/dot_general | solution.py:118
  360.2 6.9 convolution_convert_fusion.5
  374.9 13.4 %all-reduce.2.cloned.1.call-done = bf16[64,4096]{1,0:T(8,128)(2,1)} async-done(((bf16[64,4096]{1,0:T(8,128)(2,1)}), bf16[64,4096]{1,0:T(8,128)(2,1)}) %all-reduce.2.cloned.1.call-update) | async-done | bytes 524304 | tf_op jit(solution)/shard_map/while/body/eval_jaxpr/psum | solution.py:132
  392.5 14.8 %bitcast_add_fusion.4 = f32[1024,16,64]{0,2,1:T(8,128)} fusion(f32[1024,16,64]{0,2,1:T(8,128)} %get-tuple-element.702, f32[]{:T(128)S(6)} %convert_element_type.208, pred[]{:T(512)S(6)} %compare.3, bf16[64,16,64]{0,2,1:T(8,128)(2,1)S(1)} %copy.46, f32[16,64,1024]{2,1,0:T(8,128)} %fusion.131, f32[16,64,1024]{2,1,0:T(8,128)} %get-tuple-element.675, ...), kind=kOutput, calls=%fused_computation.8.clone.1 | convolution fusion | flops 144705536 | bytes 16912388 | tf_op jit(solution)/shard_map/while/body/eval_jaxpr/hqk,qhd->khd/dot_general | solution.py:123
  426.6 12.0 %fusion.133 = bf16[64,16,64]{2,0,1:T(8,128)(2,1)S(1)} fusion(bf16[1024,16,64]{0,2,1:T(8,128)(2,1)} %get-tuple-element.735, f32[16,64,1024]{2,1,0:T(8,128)} %fusion.131, f32[16,64,1024]{2,1,0:T(8,128)} %get-tuple-element.675, f32[16,64]{1,0:T(8,128)S(1)} %get-tuple-element.676), kind=kOutput, calls=%fused_computation.25.clone.1 | convolution fusion | flops 141625344 | bytes 10620928 | tf_op jit(solution)/shard_map/while/body/eval_jaxpr/hqk,khd->qhd/dot_general | solution.py:118
  439.0 6.9 convolution_convert_fusion.5
  453.7 13.4 %all-reduce.2.cloned.1.call-done = bf16[64,4096]{1,0:T(8,128)(2,1)} async-done(((bf16[64,4096]{1,0:T(8,128)(2,1)}), bf16[64,4096]{1,0:T(8,128)(2,1)}) %all-reduce.2.cloned.1.call-update) | async-done | bytes 524304 | tf_op jit(solution)/shard_map/while/body/eval_jaxpr/psum | solution.py:132
  471.3 14.8 %bitcast_add_fusion.4 = f32[1024,16,64]{0,2,1:T(8,128)} fusion(f32[1024,16,64]{0,2,1:T(8,128)} %get-tuple-element.702, f32[]{:T(128)S(6)} %convert_element_type.208, pred[]{:T(512)S(6)} %compare.3, bf16[64,16,64]{0,2,1:T(8,128)(2,1)S(1)} %copy.46, f32[16,64,1024]{2,1,0:T(8,128)} %fusion.131, f32[16,64,1024]{2,1,0:T(8,128)} %get-tuple-element.675, ...), kind=kOutput, calls=%fused_computation.8.clone.1 | convolution fusion | flops 144705536 | bytes 16912388 | tf_op jit(solution)/shard_map/while/body/eval_jaxpr/hqk,qhd->khd/dot_general | solution.py:123
  505.4 12.0 %fusion.133 = bf16[64,16,64]{2,0,1:T(8,128)(2,1)S(1)} fusion(bf16[1024,16,64]{0,2,1:T(8,128)(2,1)} %get-tuple-element.735, f32[16,64,1024]{2,1,0:T(8,128)} %fusion.131, f32[16,64,1024]{2,1,0:T(8,128)} %get-tuple-element.675, f32[16,64]{1,0:T(8,128)S(1)} %get-tuple-element.676), kind=kOutput, calls=%fused_computation.25.clone.1 | convolution fusion | flops 141625344 | bytes 10620928 | tf_op jit(solution)/shard_map/while/body/eval_jaxpr/hqk,khd->qhd/dot_general | solution.py:118
  532.5 13.4 %all-reduce.2.cloned.1.call-done = bf16[64,4096]{1,0:T(8,128)(2,1)} async-done(((bf16[64,4096]{1,0:T(8,128)(2,1)}), bf16[64,4096]{1,0:T(8,128)(2,1)}) %all-reduce.2.cloned.1.call-update) | async-done | bytes 524304 | tf_op jit(solution)/shard_map/while/body/eval_jaxpr/psum | solution.py:132
  550.0 14.8 %bitcast_add_fusion.4 = f32[1024,16,64]{0,2,1:T(8,128)} fusion(f32[1024,16,64]{0,2,1:T(8,128)} %get-tuple-element.702, f32[]{:T(128)S(6)} %convert_element_type.208, pred[]{:T(512)S(6)} %compare.3, bf16[64,16,64]{0,2,1:T(8,128)(2,1)S(1)} %copy.46, f32[16,64,1024]{2,1,0:T(8,128)} %fusion.131, f32[16,64,1024]{2,1,0:T(8,128)} %get-tuple-element.675, ...), kind=kOutput, calls=%fused_computation.8.clone.1 | convolution fusion | flops 144705536 | bytes 16912388 | tf_op jit(solution)/shard_map/while/body/eval_jaxpr/hqk,qhd->khd/dot_general | solution.py:123
  584.2 12.0 %fusion.133 = bf16[64,16,64]{2,0,1:T(8,128)(2,1)S(1)} fusion(bf16[1024,16,64]{0,2,1:T(8,128)(2,1)} %get-tuple-element.735, f32[16,64,1024]{2,1,0:T(8,128)} %fusion.131, f32[16,64,1024]{2,1,0:T(8,128)} %get-tuple-element.675, f32[16,64]{1,0:T(8,128)S(1)} %get-tuple-element.676), kind=kOutput, calls=%fused_computation.25.clone.1 | convolution fusion | flops 141625344 | bytes 10620928 | tf_op jit(solution)/shard_map/while/body/eval_jaxpr/hqk,khd->qhd/dot_general | solution.py:118
  611.3 13.4 %all-reduce.2.cloned.1.call-done = bf16[64,4096]{1,0:T(8,128)(2,1)} async-done(((bf16[64,4096]{1,0:T(8,128)(2,1)}), bf16[64,4096]{1,0:T(8,128)(2,1)}) %all-reduce.2.cloned.1.call-update) | async-done | bytes 524304 | tf_op jit(solution)/shard_map/while/body/eval_jaxpr/psum | solution.py:132
  628.8 14.8 %bitcast_add_fusion.4 = f32[1024,16,64]{0,2,1:T(8,128)} fusion(f32[1024,16,64]{0,2,1:T(8,128)} %get-tuple-element.702, f32[]{:T(128)S(6)} %convert_element_type.208, pred[]{:T(512)S(6)} %compare.3, bf16[64,16,64]{0,2,1:T(8,128)(2,1)S(1)} %copy.46, f32[16,64,1024]{2,1,0:T(8,128)} %fusion.131, f32[16,64,1024]{2,1,0:T(8,128)} %get-tuple-element.675, ...), kind=kOutput, calls=%fused_computation.8.clone.1 | convolution fusion | flops 144705536 | bytes 16912388 | tf_op jit(solution)/shard_map/while/body/eval_jaxpr/hqk,qhd->khd/dot_general | solution.py:123
  663.0 12.0 %fusion.133 = bf16[64,16,64]{2,0,1:T(8,128)(2,1)S(1)} fusion(bf16[1024,16,64]{0,2,1:T(8,128)(2,1)} %get-tuple-element.735, f32[16,64,1024]{2,1,0:T(8,128)} %fusion.131, f32[16,64,1024]{2,1,0:T(8,128)} %get-tuple-element.675, f32[16,64]{1,0:T(8,128)S(1)} %get-tuple-element.676), kind=kOutput, calls=%fused_computation.25.clone.1 | convolution fusion | flops 141625344 | bytes 10620928 | tf_op jit(solution)/shard_map/while/body/eval_jaxpr/hqk,khd->qhd/dot_general | solution.py:118
  690.1 13.4 %all-reduce.2.cloned.1.call-done = bf16[64,4096]{1,0:T(8,128)(2,1)} async-done(((bf16[64,4096]{1,0:T(8,128)(2,1)}), bf16[64,4096]{1,0:T(8,128)(2,1)}) %all-reduce.2.cloned.1.call-update) | async-done | bytes 524304 | tf_op jit(solution)/shard_map/while/body/eval_jaxpr/psum | solution.py:132
  707.6 14.8 %bitcast_add_fusion.4 = f32[1024,16,64]{0,2,1:T(8,128)} fusion(f32[1024,16,64]{0,2,1:T(8,128)} %get-tuple-element.702, f32[]{:T(128)S(6)} %convert_element_type.208, pred[]{:T(512)S(6)} %compare.3, bf16[64,16,64]{0,2,1:T(8,128)(2,1)S(1)} %copy.46, f32[16,64,1024]{2,1,0:T(8,128)} %fusion.131, f32[16,64,1024]{2,1,0:T(8,128)} %get-tuple-element.675, ...), kind=kOutput, calls=%fused_computation.8.clone.1 | convolution fusion | flops 144705536 | bytes 16912388 | tf_op jit(solution)/shard_map/while/body/eval_jaxpr/hqk,qhd->khd/dot_general | solution.py:123
  750.9 15.2 %fusion.39 = f32[1024,4096]{1,0:T(8,128)} fusion(bf16[1,4096,1024]{2,1,0:T(8,128)(2,1)} %param.23, bf16[1024,1024]{1,0:T(8,128)(2,1)} %gather_fusion.2, pred[1024]{0:T(1024)(128)(4,1)S(1)} %copy-done.5), kind=kOutput, calls=%fused_computation.52 | convolution fusion | flops 8590983168 | bytes 27264000 | tf_op jit(solution)/shard_map/rc,dc->rd/dot_general | solution.py:170
  766.1 16.6 %add_convert_fusion = bf16[1024,4096]{1,0:T(8,128)(2,1)} fusion(f32[1024,4096]{1,0:T(8,128)} %fusion.39, bf16[1,4096,1024]{2,1,0:T(8,128)(2,1)} %param.22, bf16[1024,1024]{1,0:T(8,128)(2,1)S(1)} %gather_fusion.1, pred[1024]{0:T(1024)(128)(4,1)S(1)} %copy-done.5), kind=kOutput, calls=%fused_computation.51 | convolution fusion | flops 8599371776 | bytes 35652608 | tf_op jit(solution)/shard_map/rc,dc->rd/dot_general | solution.py:166
  782.8 92.1 %reduce-scatter.2.cloned.1.call-done = bf16[128,4096]{1,0:T(8,128)(2,1)} async-done(((bf16[1024,4096]{1,0:T(8,128)(2,1)}), bf16[128,4096]{1,0:T(8,128)(2,1)}) %reduce-scatter.2.cloned.1.call-update) | async-done | bytes 1048592 | tf_op jit(solution)/shard_map/reduce_scatter | solution.py:167
  (242 shorter events, 325.2 us)
Async XLA Ops:
  7.2 15.7 %all-gather.6.cloned.1.call-start = ((), (), s32[]{:S(2)}) async-start(), calls=%async_computation.2 | async-start | bytes 3145728 | tf_op jit(solution)/shard_map/all_gather | solution.py:59
  7.9 99.8 %all-gather.8.cloned.1.call-start = ((), (), s32[]{:S(2)}) async-start(), calls=%async_computation.3 | async-start | bytes 9437184 | tf_op jit(solution)/shard_map/all_gather | solution.py:45
  8.6 158.3 %all-gather.4.cloned.1.call-start = ((), (), s32[]{:S(2)}) async-start(), calls=%async_computation.1 | async-start | bytes 3145728 | tf_op jit(solution)/shard_map/all_gather | solution.py:77
  16.4 13.0 %copy-start.1 = (f32[1,4096]{1,0:T(1,128)}, f32[1,4096]{1,0:T(1,128)S(1)}, u32[]{:S(2)}) copy-start(f32[1,4096]{1,0:T(1,128)S(1)} %mul.200) | copy-start | bytes 49156
  22.8 6.5 copy-start
  160.5 7.6 copy-start.2
  160.5 7.6 copy-start.3
  177.7 54.3 %all-reduce.2.cloned.1.call-start = ((), (), s32[]{:S(2)}) async-start(), calls=%async_computation.5 | async-start | bytes 1048576 | tf_op jit(solution)/shard_map/while/body/eval_jaxpr/psum | solution.py:132
  234.8 16.7 %collective-permute-start = (bf16[64,4096]{1,0:T(8,128)(2,1)S(1)}, bf16[64,4096]{1,0:T(8,128)(2,1)S(1)}, u32[]{:S(2)}, u32[]{:S(2)}) collective-permute-start(bf16[64,4096]{1,0:T(8,128)(2,1)S(1)} %fusion.135), channel_id=1, source_target_pairs={{2,0},{4,2},{6,4},{3,1},{5,3},{7,5},{10,8},{12,10},{14,12},{11,9},... | collective-permute-start | bytes 1572872 | tf_op jit(solution)/shard_map/while/body/eval_jaxpr/ppermute | solution.py:17
  251.4 58.1 %all-reduce.2.cloned.1.call-start = ((), (), s32[]{:S(2)}) async-start(), calls=%async_computation.5 | async-start | bytes 1048576 | tf_op jit(solution)/shard_map/while/body/eval_jaxpr/psum | solution.py:132
  312.4 17.9 %collective-permute-start = (bf16[64,4096]{1,0:T(8,128)(2,1)S(1)}, bf16[64,4096]{1,0:T(8,128)(2,1)S(1)}, u32[]{:S(2)}, u32[]{:S(2)}) collective-permute-start(bf16[64,4096]{1,0:T(8,128)(2,1)S(1)} %fusion.135), channel_id=1, source_target_pairs={{2,0},{4,2},{6,4},{3,1},{5,3},{7,5},{10,8},{12,10},{14,12},{11,9},... | collective-permute-start | bytes 1572872 | tf_op jit(solution)/shard_map/while/body/eval_jaxpr/ppermute | solution.py:17
  330.2 58.2 %all-reduce.2.cloned.1.call-start = ((), (), s32[]{:S(2)}) async-start(), calls=%async_computation.5 | async-start | bytes 1048576 | tf_op jit(solution)/shard_map/while/body/eval_jaxpr/psum | solution.py:132
  391.2 17.9 %collective-permute-start = (bf16[64,4096]{1,0:T(8,128)(2,1)S(1)}, bf16[64,4096]{1,0:T(8,128)(2,1)S(1)}, u32[]{:S(2)}, u32[]{:S(2)}) collective-permute-start(bf16[64,4096]{1,0:T(8,128)(2,1)S(1)} %fusion.135), channel_id=1, source_target_pairs={{2,0},{4,2},{6,4},{3,1},{5,3},{7,5},{10,8},{12,10},{14,12},{11,9},... | collective-permute-start | bytes 1572872 | tf_op jit(solution)/shard_map/while/body/eval_jaxpr/ppermute | solution.py:17
  409.0 58.2 %all-reduce.2.cloned.1.call-start = ((), (), s32[]{:S(2)}) async-start(), calls=%async_computation.5 | async-start | bytes 1048576 | tf_op jit(solution)/shard_map/while/body/eval_jaxpr/psum | solution.py:132
  470.0 17.9 %collective-permute-start = (bf16[64,4096]{1,0:T(8,128)(2,1)S(1)}, bf16[64,4096]{1,0:T(8,128)(2,1)S(1)}, u32[]{:S(2)}, u32[]{:S(2)}) collective-permute-start(bf16[64,4096]{1,0:T(8,128)(2,1)S(1)} %fusion.135), channel_id=1, source_target_pairs={{2,0},{4,2},{6,4},{3,1},{5,3},{7,5},{10,8},{12,10},{14,12},{11,9},... | collective-permute-start | bytes 1572872 | tf_op jit(solution)/shard_map/while/body/eval_jaxpr/ppermute | solution.py:17
  487.8 58.2 %all-reduce.2.cloned.1.call-start = ((), (), s32[]{:S(2)}) async-start(), calls=%async_computation.5 | async-start | bytes 1048576 | tf_op jit(solution)/shard_map/while/body/eval_jaxpr/psum | solution.py:132
  548.7 17.9 %collective-permute-start = (bf16[64,4096]{1,0:T(8,128)(2,1)S(1)}, bf16[64,4096]{1,0:T(8,128)(2,1)S(1)}, u32[]{:S(2)}, u32[]{:S(2)}) collective-permute-start(bf16[64,4096]{1,0:T(8,128)(2,1)S(1)} %fusion.135), channel_id=1, source_target_pairs={{2,0},{4,2},{6,4},{3,1},{5,3},{7,5},{10,8},{12,10},{14,12},{11,9},... | collective-permute-start | bytes 1572872 | tf_op jit(solution)/shard_map/while/body/eval_jaxpr/ppermute | solution.py:17
  566.6 58.2 %all-reduce.2.cloned.1.call-start = ((), (), s32[]{:S(2)}) async-start(), calls=%async_computation.5 | async-start | bytes 1048576 | tf_op jit(solution)/shard_map/while/body/eval_jaxpr/psum | solution.py:132
  627.5 17.9 %collective-permute-start = (bf16[64,4096]{1,0:T(8,128)(2,1)S(1)}, bf16[64,4096]{1,0:T(8,128)(2,1)S(1)}, u32[]{:S(2)}, u32[]{:S(2)}) collective-permute-start(bf16[64,4096]{1,0:T(8,128)(2,1)S(1)} %fusion.135), channel_id=1, source_target_pairs={{2,0},{4,2},{6,4},{3,1},{5,3},{7,5},{10,8},{12,10},{14,12},{11,9},... | collective-permute-start | bytes 1572872 | tf_op jit(solution)/shard_map/while/body/eval_jaxpr/ppermute | solution.py:17
  645.4 58.2 %all-reduce.2.cloned.1.call-start = ((), (), s32[]{:S(2)}) async-start(), calls=%async_computation.5 | async-start | bytes 1048576 | tf_op jit(solution)/shard_map/while/body/eval_jaxpr/psum | solution.py:132
  706.3 17.9 %collective-permute-start = (bf16[64,4096]{1,0:T(8,128)(2,1)S(1)}, bf16[64,4096]{1,0:T(8,128)(2,1)S(1)}, u32[]{:S(2)}, u32[]{:S(2)}) collective-permute-start(bf16[64,4096]{1,0:T(8,128)(2,1)S(1)} %fusion.135), channel_id=1, source_target_pairs={{2,0},{4,2},{6,4},{3,1},{5,3},{7,5},{10,8},{12,10},{14,12},{11,9},... | collective-permute-start | bytes 1572872 | tf_op jit(solution)/shard_map/while/body/eval_jaxpr/ppermute | solution.py:17
  724.2 150.6 %reduce-scatter.2.cloned.1.call-start = ((), (), s32[]{:S(2)}) async-start(), calls=%async_computation.4 | async-start | bytes 9437184 | tf_op jit(solution)/shard_map/reduce_scatter | solution.py:167
  730.9 7.8 copy-start.4
  744.0 6.8 copy-start.5
Sparse Core Ops, SparseCore 0:
  9.5 13.2 all-gather.5
  24.4 83.1 all-gather.7
  109.2 9.0 all-gather.3
  214.9 17.0 all-reduce.1
  288.5 21.0 all-reduce.1
  367.3 21.0 all-reduce.1
  446.1 21.0 all-reduce.1
  524.9 21.0 all-reduce.1
  603.7 21.0 all-reduce.1
  682.5 21.0 all-reduce.1
  782.9 91.9 reduce-scatter.1
where the time goes:
time: 891 us; the launch traced here: 884 us
  matrix products  453 us (51%)
  waiting for transfers between devices  262 us (29%)
  local copies, waits for them, and re-layouts  76.6 us (9%)
  other arithmetic  59.3 us (7%)
  between operations  14.1 us (2%)
  loops' own time  10.5 us (1%)
  starting transfers between devices  9.22 us (1%)
    dot_general x7, matrix products, advance(): jnp.einsum('hqk,qhd->khd', score_grad, query_rows, preferred_element_type...  103 us
    reduce_scatter x1, waiting for transfers between devices, on_device(): lax.psum_scatter((result + jnp.einsum('rc,dc->rd', value_part, value_weig...  92.1 us
    psum x7, waiting for transfers between devices, advance(): lax.psum(partial_grad.astype(jnp.bfloat16), 'mp').astype(jnp.float32)  91.4 us
    dot_general x7, matrix products, advance(): jnp.einsum('hqk,khd->qhd', score_grad, key_heads, preferred_element_type=...  84 us
    all_gather x1, waiting for transfers between devices, on_device(): lax.all_gather(enc_rows, ('section', 'mp'), axis=1, tiled=True)[0]  72.3 us
    dot_general x7, matrix products, advance(): jnp.einsum('rc,dc->rd', query_grad, query_weight, preferred_element_type=...  48.4 us
    dot_general x7, matrix products, advance(): jnp.einsum('hqk,qhd->khd', attention_low, attn_grad, preferred_element_ty...  43.2 us
    dot_general x7, matrix products, advance(): jnp.einsum('rd,cd->rc', upstream, out_weight, preferred_element_type=jnp....  42.3 us
  transfers between devices with their start and end apart: 18, of which 10 were waited for; matrix products, arithmetic and copies ran while one was open for 28% of the time, Pallas kernels for 0%

commit v1 on v0

v1 whole, which is shorter than its diff:
```python
import functools

import jax
import jax.numpy as jnp
from jax import lax
from jax.experimental import pallas as pl
from jax.experimental.pallas import tpu as pltpu
from jax.sharding import PartitionSpec as P

HD = 64
PAIR = 2 * HD
MICRO = 4
SKEW = 2
PIECES = 2
BLOCK = 512
OUT_BLOCK = 512
SLOTS = ((0, 1, 2, 3), (1, 2, 1, 2), (2, 3, 0, 1), (3, 0, 3, 0))

epsilon = 1e-06
masked_value = -1e30
f32 = jnp.float32
bf16 = jnp.bfloat16
NT = (((1,), (1,)), ((), ()))
NN = (((1,), (0,)), ((), ()))


def dot(a, b, dims):
    return lax.dot_general(a, b, dims, preferred_element_type=f32)


def stacked(x):
    lane = lax.broadcasted_iota(jnp.int32, x.shape, 1)
    zero = jnp.zeros_like(x)
    return jnp.concatenate(
        [jnp.where(lane < HD, x, zero), jnp.where(lane >= HD, x, zero)], axis=0
    )


def probs_kernel(q_ref, k_ref, tok_ref, key_ref, p_ref):
    q = stacked(q_ref[...].astype(f32) * (HD**-0.5)).astype(bf16)
    s = dot(q, k_ref[...], NT)
    s = jnp.where(tok_ref[0] == key_ref[...], s, masked_value)
    e = jnp.exp(s - jnp.max(s, axis=-1, keepdims=True))
    total = jnp.sum(e, axis=-1, keepdims=True)
    p_ref[0, 0] = (e * (1.0 / total)).astype(bf16)


def load_kernel(count, *refs):
    sems = refs[-1]
    copies = [
        pltpu.make_async_copy(refs[i], refs[count + i], sems.at[i]) for i in range(count)
    ]
    for copy in copies:
        copy.start()
    for copy in copies:
        copy.wait()


def project_kernel(count, *refs):
    x_refs = refs[:count]
    wk_ref, wv_ref = refs[count : count + 2]
    k_ref, v_ref, x_all = refs[-3:]

    @pl.when(pl.program_id(0) == 0)
    def _():
        start = 0
        for x in x_refs:
            x_all[start : start + x.shape[0]] = x[...]
            start += x.shape[0]

    block = k_ref.shape[1]
    cols = pl.ds(pl.multiple_of(pl.program_id(0) * block, block), block)
    k_ref[...] = dot(x_all[...], wk_ref[:, cols], NN).astype(bf16)
    v_ref[...] = dot(x_all[...], wv_ref[:, cols], NN).astype(bf16)


def back_kernel(kg_ref, vg_ref, wk_ref, wv_ref, own_ref, other_ref):
    block = own_ref.shape[1]
    place = pl.ds(pl.multiple_of(pl.program_id(0) * block, block), block)
    out = dot(kg_ref[...], wk_ref[place, :], NT) + dot(vg_ref[...], wv_ref[place, :], NT)
    rows = own_ref.shape[0]
    own_ref[...] = out[:rows].astype(bf16)
    other_ref[...] = out[rows:].astype(bf16)


def turn_kernel(parts, own_rows, slots, *refs):
    del slots
    up_refs = refs[:parts]
    wo_ref, wq_ref, k_ref, v_ref, p_ref = refs[parts : parts + 5]
    own_ref, other_ref, ds_ref, ag_ref, acc_ref = refs[-5:]
    step = pl.program_id(0)
    block = ag_ref.shape[2]
    start = pl.multiple_of(step * block, block)
    up = up_refs[0][...] if parts == 1 else jnp.concatenate([r[...] for r in up_refs], axis=0)
    rows = up.shape[0]
    grads = dot(up, wo_ref[pl.ds(start, block), :], NT).astype(bf16)
    ag_ref[0] = grads
    wide = grads.astype(f32)
    lane = lax.broadcasted_iota(jnp.int32, (rows, PAIR), 1)
    pieces = []
    for pair in range(grads.shape[1] // PAIR):
        cols = pl.ds(pl.multiple_of(start + pair * PAIR, PAIR), PAIR)
        here = wide[:, pair * PAIR : (pair + 1) * PAIR]
        pg = dot(stacked(here).astype(bf16), v_ref[:, cols], NT)
        p = p_ref[0, pair].astype(f32)
        mean = jnp.sum(pg * p, axis=-1, keepdims=True)
        ds = (p * (pg - mean)).astype(bf16)
        ds_ref[0, pair] = ds
        both = dot(ds, k_ref[:, cols], NN)
        mine = jnp.where(lane < HD, both[:rows], both[rows:]) * (HD**-0.5)
        pieces.append(mine.astype(bf16))
    qg = pieces[0] if len(pieces) == 1 else jnp.concatenate(pieces, axis=1)
    partial = dot(qg, wq_ref[:, pl.ds(start, block)], NT)

    @pl.when(step == 0)
    def _():
        acc_ref[...] = partial

    @pl.when(step > 0)
    def _():
        acc_ref[...] += partial

    @pl.when(step == pl.num_programs(0) - 1)
    def _():
        own_ref[...] = acc_ref[:own_rows].astype(bf16)
        other_ref[...] = acc_ref[own_rows:].astype(bf16)


def norm_kernel(received, slots, *refs):
    del slots
    got_refs = refs[:received]
    own_ref, up_ref, x_ref, gain_ref = refs[received : received + 4]
    mine_ref, all_ref = refs[-2:]
    x = x_ref[...].astype(f32)
    recip = lax.rsqrt(jnp.mean(x * x, axis=-1, keepdims=True) + epsilon)
    unit = x * recip
    summed = own_ref[...].astype(f32)
    for got in got_refs:
        summed = summed + got[...].astype(f32)
    scaled = summed * gain_ref[...]
    out = up_ref[...].astype(f32) + recip * (
        scaled - unit * jnp.mean(scaled * unit, axis=-1, keepdims=True)
    )
    out = out.astype(bf16)
    mine_ref[...] = out
    all_ref[...] = out


def grads_kernel(micro, ds_ref, p_ref, q_ref, ag_ref, kg_ref, vg_ref):
    rows = ag_ref.shape[1]
    enc = ds_ref.shape[-1]
    q = jnp.concatenate(
        [stacked(q_ref[i * rows : (i + 1) * rows, :].astype(f32)) for i in range(micro)], axis=0
    )
    ag = jnp.concatenate([stacked(ag_ref[i].astype(f32)) for i in range(micro)], axis=0)
    ds = ds_ref[:, 0].reshape(micro * 2 * rows, enc)
    p = p_ref[:, 0].reshape(micro * 2 * rows, enc)
    kg = dot(q.T.astype(bf16), ds, NN) * (HD**-0.5)
    vg = dot(ag.T.astype(bf16), p, NN)
    kg_ref[...] = kg.T.astype(bf16)
    vg_ref[...] = vg.T.astype(bf16)


def all_of_it(
    enc_rows,
    pack_index,
    enc_segments,
    dec_segments,
    dec_inputs,
    norm_gain,
    w_query,
    w_key,
    w_value,
    w_out,
    cotangent,
):
    wq, wk, wv, wo = w_query[0], w_key[0], w_value[0], w_out[0]
    gain = norm_gain.astype(f32)
    model, width = wq.shape
    pairs = width // PAIR
    n = lax.axis_size("mp")
    sections = lax.axis_size("section")
    me = lax.axis_index("mp")
    section = lax.axis_index("section")
    assert sections == len(SLOTS)
    share = enc_rows.shape[1]
    enc = share * n * sections
    own = dec_inputs.shape[2]
    r = own // MICRO
    m = r * n
    tokens = own * n
    params = pltpu.CompilerParams(vmem_limit_bytes=24 * 1024 * 1024)
    small = pltpu.CompilerParams(vmem_limit_bytes=14 * 1024 * 1024)

    def shifted(x, by):
        return lax.ppermute(x, "mp", [((i + by) % n, i) for i in range(n)])

    def along(x, *pairs):
        return lax.ppermute(x, "section", pairs)

    low = section < 2
    block = min(BLOCK, width)
    bp = block // PAIR
    parts = 2 if n == 2 else 1
    any_spec = pl.BlockSpec(memory_space=pl.ANY)
    resident = pl.BlockSpec(memory_space=pltpu.MemorySpace.VMEM)

    def in_hbm(x):
        return pltpu.with_memory_space_constraint(x, pltpu.MemorySpace.HBM)

    def loaded(*xs):
        return pl.pallas_call(
            functools.partial(load_kernel, len(xs)),
            in_specs=[any_spec] * len(xs),
            out_specs=[resident] * len(xs),
            out_shape=[pltpu.MemorySpace.VMEM(x.shape, x.dtype) for x in xs],
            scratch_shapes=[pltpu.SemaphoreType.DMA((len(xs),))],
            compiler_params=small,
            name="load",
        )(*map(in_hbm, xs))

    def all_parts(x):
        return [x] + [shifted(x, k) for k in range(1, n)]

    x_own = dec_inputs[0, 0]
    x_all = jnp.stack([v.reshape(MICRO, r, model) for v in all_parts(x_own)], axis=1)
    x_all = x_all.reshape(tokens, model).astype(f32)
    recip = lax.rsqrt(jnp.mean(x_all * x_all, axis=-1, keepdims=True) + epsilon)
    normed = (x_all * recip * gain).astype(bf16)
    queries = dot(normed, wq, NN).astype(bf16)
    token_ids = dec_segments[0].reshape(n, MICRO, r)
    order = jnp.remainder(me + jnp.arange(n), n)
    token_ids = jnp.take(token_ids, order, axis=0).transpose(1, 0, 2).reshape(MICRO, m)
    token_ids = jnp.concatenate([token_ids, token_ids], axis=1)[:, :, None]

    blocks = jnp.asarray(SLOTS, jnp.int32)[:, section]
    stored = (blocks[:, None] * n + order[None, :])[:, :, None] * share
    stored = (stored + jnp.arange(share)).reshape(1, enc)
    key_ids = jnp.sum(
        jnp.where(pack_index[0][:, None] == stored, enc_segments[0][:, None], 0),
        axis=0,
        keepdims=True,
    )
    size = share // PIECES
    mine = [enc_rows[0, i * size : (i + 1) * size] for i in range(PIECES)]

    def ring(values, *pairs):
        out = []
        for v in values:
            out.append(along(v, *pairs))
        return out

    up1 = ring(mine, (0, 1), (1, 2), (2, 3))
    down1 = ring(mine, (3, 2), (2, 1), (1, 0))
    up2 = ring(up1, (1, 2), (2, 3))
    down2 = ring(down1, (2, 1), (1, 0))
    third = [jnp.where(low, d, u) for u, d in zip(up2, down2)]
    third = ring(third, (2, 3), (1, 0))
    outer = (section == 0) | (section == 3)
    near_in = [jnp.where(low, d, u) for u, d in zip(up1, down1)]
    far_in = lax.optimization_barrier([jnp.where(low, u, d) for u, d in zip(up1, down1)])
    mid_in = [jnp.where(low, d, u) for u, d in zip(up2, down2)]
    last_in = [jnp.where(outer, t, f) for t, f in zip(third, far_in)]
    slots_in = [mine, near_in, mid_in, last_in]
    keys_values = []
    rows = share * n
    for slot, held in enumerate(slots_in):
        xs = [all_parts(v) for v in held]
        xs = [x[k] for k in range(n) for x in xs]
        if n > 2:
            xs = [jnp.concatenate(xs, axis=0)]
        project = pl.pallas_call(
            functools.partial(project_kernel, len(xs)),
            grid=(width // block,),
            in_specs=[pl.BlockSpec(x.shape, lambda i: (0, 0)) for x in xs]
            + [resident] * 2
            + [any_spec] * len(keys_values),
            out_specs=[pl.BlockSpec((rows, block), lambda i, slot=slot: (slot, i))] * 2,
            out_shape=[jax.ShapeDtypeStruct((enc, width), bf16)] * 2,
            scratch_shapes=[pltpu.VMEM((rows, model), bf16)],
            input_output_aliases={len(xs) + 2 + i: i for i in range(len(keys_values))},
            compiler_params=params,
            name="project",
        )
        keys_values = project(*xs, wk, wv, *keys_values)
    keys, values = keys_values

    probs = pl.pallas_call(
        probs_kernel,
        grid=(pairs, MICRO),
        in_specs=[
            pl.BlockSpec((m, PAIR), lambda p, i: (i, p)),
            pl.BlockSpec((enc, PAIR), lambda p, i: (0, p)),
            pl.BlockSpec((1, 2 * m, 1), lambda p, i: (i, 0, 0)),
            pl.BlockSpec((1, enc), lambda p, i: (0, 0)),
        ],
        out_specs=pl.BlockSpec((1, 1, 2 * m, enc), lambda p, i: (i, p, 0, 0)),
        out_shape=pltpu.MemorySpace.HBM((MICRO, pairs, 2 * m, enc), bf16),
        compiler_params=params,
        name="probs",
    )(queries, keys, token_ids, key_ids)

    weights = loaded(wo, wq, keys, values)

    def turn(t, ups, held, after):
        if parts == 1:
            ups = [jnp.concatenate(ups, axis=0)] if n > 1 else ups
        up_specs = [pl.BlockSpec(u.shape, lambda i, s: (0, 0)) for u in ups]
        return pl.pallas_call(
            functools.partial(turn_kernel, parts, r),
            grid_spec=pltpu.PrefetchScalarGridSpec(
                num_scalar_prefetch=1,
                grid=(width // block,),
                in_specs=up_specs
                + [resident] * 4
                + [
                    pl.BlockSpec((1, bp, 2 * m, enc), lambda i, s: (s[t, 0], i, 0, 0)),
                ]
                + [any_spec] * (len(held) + len(after)),
                out_specs=[
                    pl.BlockSpec((r, model), lambda i, s: (0, 0)),
                    pl.BlockSpec((m - r, model), lambda i, s: (0, 0)),
                    pl.BlockSpec((1, bp, 2 * m, enc), lambda i, s: (s[t, 1], i, 0, 0)),
                    pl.BlockSpec((1, m, block), lambda i, s: (s[t, 1], 0, i)),
                ],
                scratch_shapes=[pltpu.VMEM((m, model), f32)],
            ),
            out_shape=[
                jax.ShapeDtypeStruct((r, model), bf16),
                jax.ShapeDtypeStruct((m - r, model), bf16),
                pltpu.MemorySpace.HBM((MICRO + 1, pairs, 2 * m, enc), bf16),
                pltpu.MemorySpace.HBM((MICRO + 1, m, width), bf16),
            ],
            input_output_aliases={parts + 6 + i: 2 + i for i in range(len(held))},
            compiler_params=small,
            name="turn",
        )(slots, *ups, *weights, in_hbm(probs), *map(in_hbm, held), *map(in_hbm, after))

    def norm_back(t, got, own_part, up_own, held):
        row_spec = pl.BlockSpec((r, model), lambda i, s: (0, 0))
        k = len(got)
        return pl.pallas_call(
            functools.partial(norm_kernel, k),
            grid_spec=pltpu.PrefetchScalarGridSpec(
                num_scalar_prefetch=1,
                grid=(1,),
                in_specs=[row_spec] * (k + 2)
                + [
                    pl.BlockSpec((r, model), lambda i, s: (s[t, 0], 0)),
                    pl.BlockSpec((1, model), lambda i, s: (0, 0)),
                ]
                + [any_spec] * len(held),
                out_specs=[row_spec, pl.BlockSpec((r, model), lambda i, s: (s[t, 1], 0))],
            ),
            out_shape=[
                jax.ShapeDtypeStruct((r, model), bf16),
                pltpu.MemorySpace.HBM(((MICRO + 1) * r, model), bf16),
            ],
            input_output_aliases={k + 5: 1} if held else {},
            compiler_params=small,
            name="norm",
        )(slots, *got, own_part, up_own, in_hbm(x_own), gain, *map(in_hbm, held))

    held, dec_held = [], []
    is_last = section == sections - 1
    hops = {}
    turns = MICRO + SKEW * (sections - 1)
    micro = jnp.arange(turns, dtype=jnp.int32) - SKEW * (sections - 1 - section)
    read = jnp.clip(micro, 0, MICRO - 1)
    slots = jnp.stack([read, jnp.where(micro == read, read, MICRO)], axis=1)
    for t in range(turns):
        if t < MICRO:
            up_own = cotangent[0, t * r : (t + 1) * r]
            if t >= SKEW:
                up_own, _ = lax.optimization_barrier((up_own, own_part))
                up_own = jnp.where(is_last, up_own, hops[t - SKEW])
        else:
            up_own = hops[t - SKEW]
        ups = all_parts(up_own)
        own_part, other, *held = turn(t, ups, held, dec_held)
        got = [
            shifted(other if n == 2 else other[(k - 1) * r : k * r], -k) for k in range(1, n)
        ]
        mine, *dec_held = norm_back(t, got, own_part, up_own, dec_held)
        if t + SKEW < turns:
            hops[t] = along(mine, (3, 2), (2, 1), (1, 0))

    kg, vg = pl.pallas_call(
        functools.partial(grads_kernel, MICRO),
        grid=(pairs,),
        in_specs=[
            pl.BlockSpec((MICRO, 1, 2 * m, enc), lambda p: (0, p, 0, 0)),
            pl.BlockSpec((MICRO, 1, 2 * m, enc), lambda p: (0, p, 0, 0)),
            pl.BlockSpec((tokens, PAIR), lambda p: (0, p)),
            pl.BlockSpec((MICRO, m, PAIR), lambda p: (0, 0, p)),
        ],
        out_specs=[pl.BlockSpec((enc, PAIR), lambda p: (0, p))] * 2,
        out_shape=[jax.ShapeDtypeStruct((enc, width), bf16)] * 2,
        compiler_params=params,
        name="grads",
    )(*map(in_hbm, (held[0], probs, queries, held[1])))

    out_block = min(OUT_BLOCK, model)

    def back(slot):
        own_part, other = back_call(slot)
        return summed_parts(own_part, other)

    def back_call(slot):
        return pl.pallas_call(
            back_kernel,
            grid=(model // out_block,),
            in_specs=[pl.BlockSpec((rows, width), lambda i: (slot, 0))] * 2
            + [resident] * 2,
            out_specs=[
                pl.BlockSpec((share, out_block), lambda i: (0, i)),
                pl.BlockSpec((rows - share, out_block), lambda i: (0, i)),
            ],
            out_shape=[
                jax.ShapeDtypeStruct((share, model), bf16),
                jax.ShapeDtypeStruct((rows - share, model), bf16),
            ],
            compiler_params=params,
            name="back",
        )(kg, vg, wk, wv)

    def summed_parts(own_part, other):
        totals = []
        for i in range(PIECES):
            total = own_part[i * size : (i + 1) * size].astype(f32)
            for k in range(1, n):
                first = (k - 1) * share + i * size
                got = shifted(other[first : first + size], -k)
                total = total + got.astype(f32)
            totals.append(total)
        return totals

    far, mid = back(3), back(2)
    got = []
    for v in far:
        got.append(along(v.astype(bf16), (0, 1), (3, 2)))
    near = back(1)
    up2, down2 = [], []
    for v, g in zip(mid, got):
        v = (v + g.astype(f32)).astype(bf16)
        up2.append(along(v, (0, 1), (1, 2)))
        down2.append(along(v, (3, 2), (2, 1)))
    here = back(0)
    enc_share = []
    for i in range(PIECES):
        up3 = jnp.where(section == 2, far[i], near[i]) + up2[i].astype(f32)
        down3 = jnp.where(section == 1, far[i], near[i]) + down2[i].astype(f32)
        up3 = along(up3.astype(bf16), (0, 1), (1, 2), (2, 3))
        down3 = along(down3.astype(bf16), (3, 2), (2, 1), (1, 0))
        enc_share.append(here[i] + up3.astype(f32) + down3.astype(f32))
    enc_share = jnp.concatenate(enc_share, axis=0)
    return dec_held[0][:own][None, None], enc_share[None]


def solution(mesh):
    in_specs = (
        P("dp", ("section", "mp"), None),
        P("dp", None),
        P("dp", None),
        P("dp", None),
        P("dp", "section", "mp", None),
        P("section", None),
        P("section", None, "mp"),
        P("section", None, "mp"),
        P("section", None, "mp"),
        P("section", "mp", None),
        P("dp", "mp", None),
    )
    out_specs = (P("dp", "section", "mp", None), P("dp", ("section", "mp"), None))
    return jax.shard_map(
        all_of_it, mesh=mesh, in_specs=in_specs, out_specs=out_specs, check_vma=False
    )
```

time: 891 us -> 473 us (0.53)
  matrix products: 453 us -> 2.38 us
  Pallas kernels: 0 us -> 227 us
  waiting for transfers between devices: 262 us -> 108 us
  starting transfers between devices: 9.22 us -> 80.5 us
  local copies, waits for them, and re-layouts: 76.6 us -> 31.8 us
  other arithmetic: 59.3 us -> 15.1 us
  between operations: 14.1 us -> 1.92 us
  loops' own time: 10.5 us -> 0 us
    dot_general x47 -> x1, matrix products: 416 us -> 2.38 us  [dot(): return lax.dot_general(a, b, dims, preferred_element_type=f32)]
    pallas_call x0 -> x31, Pallas kernels: none -> 227 us  [the longest x10 115 us: turn(): pl.pallas_call(functools.partial(turn_kernel, parts, r), grid_spec=pltpu....]
    ppermute x7 -> x65, waiting for transfers between devices: 0.02 us -> 108 us  [the longest x28 99.2 us: along(): return lax.ppermute(x, 'section', pairs)]
    reduce_scatter x1 -> x0, waiting for transfers between devices: 92.1 us -> none  [on_device(): lax.psum_scatter((result + jnp.einsum('rc,dc->rd', value_part, value_weig...]
    psum x7 -> x0, waiting for transfers between devices: 91.4 us -> none  [advance(): lax.psum(partial_grad.astype(jnp.bfloat16), 'mp').astype(jnp.float32)]
    all_gather x3 -> x0, waiting for transfers between devices: 76.1 us -> none  [the longest x1 72.3 us: on_device(): lax.all_gather(enc_rows, ('section', 'mp'), axis=1, tiled=True)[0]]
    ppermute x7 -> x65, starting transfers between devices: 9.04 us -> 80.5 us  [the longest x28 72.1 us: along(): return lax.ppermute(x, 'section', pairs)]
    sub x7 -> x0, matrix products: 36.6 us -> none  [advance(): attention = jax.nn.softmax(scores, axis=-1)]
  transfers between devices with their start and end apart: 18 -> 65, of which waited for: 10 -> 26; matrix products, arithmetic and copies ran while one was open for 28% -> 4% of each run, Pallas kernels for 0% -> 36%
where the time goes in v1:
time: 473 us; the launch traced here: 467 us
  Pallas kernels  227 us (48%)
  waiting for transfers between devices  108 us (23%)
  starting transfers between devices  80.5 us (17%)
  local copies, waits for them, and re-layouts  31.8 us (7%)
  other arithmetic  15.1 us (3%)
    pallas_call x10, Pallas kernels, turn(): pl.pallas_call(functools.partial(turn_kernel, parts, r), grid_spec=pltpu....  115 us
    ppermute x28, waiting for transfers between devices, along(): return lax.ppermute(x, 'section', pairs)  99.2 us
    ppermute x28, starting transfers between devices, along(): return lax.ppermute(x, 'section', pairs)  72.1 us
    pallas_call x10, Pallas kernels, norm_back(): pl.pallas_call(functools.partial(norm_kernel, k), grid_spec=pltpu.Prefetc...  27.5 us
    unnamed x79, local copies, waits for them, and re-layouts  27.2 us
    pallas_call x4, Pallas kernels, back_call(): pl.pallas_call(back_kernel, grid=(model // out_block,), in_specs=[pl.Bloc...  24.3 us
    pallas_call x1, Pallas kernels, all_of_it(): pl.pallas_call(probs_kernel, grid=(pairs, MICRO), in_specs=[pl.BlockSpec(...  22 us
    pallas_call x4, Pallas kernels, all_of_it(): keys_values = project(*xs, wk, wv, *keys_values)  19.7 us
  transfers between devices with their start and end apart: 65, of which 26 were waited for; matrix products, arithmetic and copies ran while one was open for 4% of the time, Pallas kernels for 36%

profile of v1, /device:TPU:0, one launch (start us, length us, event | category | flops | bytes accessed | tf_op | source)
XLA Modules:
  0.0 466.8 jit_solution(4650196705253987175)
XLA Ops:
  3.3 6.4 %collective-permute-start.3 = (bf16[64,4096]{1,0:T(8,128)(2,1)S(1)}, bf16[64,4096]{1,0:T(8,128)(2,1)}, u32[]{:S(2)}, u32[]{:S(2)}) collective-permute-start(bf16[64,4096]{1,0:T(8,128)(2,1)S(1)} %get-tuple-element.199.refs_0_), channel_id=1, source_target_pairs={{0,2},{2,4},{4,6},{1,3},{3,5},{5,7},{8,10},{10,12},{12,14},{9,11},... | collective-permute-start | bytes 1572872 | tf_op jit(solution)/shard_map/ppermute | solution.py:199
  11.0 5.4 %collective-permute-start.6 = (bf16[64,4096]{1,0:T(8,128)(2,1)S(1)}, bf16[64,4096]{1,0:T(8,128)(2,1)}, u32[]{:S(2)}, u32[]{:S(2)}) collective-permute-start(bf16[64,4096]{1,0:T(8,128)(2,1)S(1)} %get-tuple-element.198.refs_1_), channel_id=1, source_target_pairs={{0,2},{2,4},{4,6},{1,3},{3,5},{5,7},{8,10},{10,12},{12,14},{9,11},... | collective-permute-start | bytes 1572872 | tf_op jit(solution)/shard_map/ppermute | solution.py:199
  23.2 7.0 %collective-permute-done.7 = bf16[64,4096]{1,0:T(8,128)(2,1)} collective-permute-done((bf16[64,4096]{1,0:T(8,128)(2,1)S(1)}, bf16[64,4096]{1,0:T(8,128)(2,1)}, u32[]{:S(2)}, u32[]{:S(2)}) %collective-permute-start.7) | collective-permute-done | bytes 524320 | tf_op jit(solution)/shard_map/ppermute | solution.py:199
  55.0 17.4 %collective-permute-done.8 = bf16[64,4096]{1,0:T(8,128)(2,1)S(1)} collective-permute-done((bf16[64,4096]{1,0:T(8,128)(2,1)}, bf16[64,4096]{1,0:T(8,128)(2,1)S(1)}, u32[]{:S(2)}, u32[]{:S(2)}) %collective-permute-start.8) | collective-permute-done | bytes 524320 | tf_op jit(solution)/shard_map/ppermute | solution.py:199
  73.9 13.2 %collective-permute-done.5 = bf16[64,4096]{1,0:T(8,128)(2,1)S(1)} collective-permute-done((bf16[64,4096]{1,0:T(8,128)(2,1)S(1)}, bf16[64,4096]{1,0:T(8,128)(2,1)S(1)}, u32[]{:S(2)}, u32[]{:S(2)}) %collective-permute-start.5) | collective-permute-done | bytes 524320 | tf_op jit(solution)/shard_map/ppermute | solution.py:199
  88.6 12.3 %collective-permute-done.10 = bf16[64,4096]{1,0:T(8,128)(2,1)S(1)} collective-permute-done((bf16[64,4096]{1,0:T(8,128)(2,1)S(1)}, bf16[64,4096]{1,0:T(8,128)(2,1)S(1)}, u32[]{:S(2)}, u32[]{:S(2)}) %collective-permute-start.10) | collective-permute-done | bytes 524320 | tf_op jit(solution)/shard_map/ppermute | solution.py:199
  115.6 4.9 %project.6 = (bf16[1024,1024]{1,0:T(8,128)(2,1)S(1)}, bf16[1024,1024]{1,0:T(8,128)(2,1)S(1)}) custom-call(bf16[64,4096]{1,0:T(8,128)(2,1)S(1)} %broadcast_select_fusion.5.refs_0_, bf16[64,4096]{1,0:T(8,128)(2,1)S(1)} %broadcast_select_fusion.2.refs_1_, ...), custom_call_target="tpu_custom_call", output_to_operand_aliasing={{0}: (6, {}), {1}: (7, {})} | custom-call | tf_op jit(solution)/shard_map/project/pallas_call | solution.py:285
  120.6 4.9 %project.7 = (bf16[1024,1024]{1,0:T(8,128)(2,1)S(1)}, bf16[1024,1024]{1,0:T(8,128)(2,1)S(1)}) custom-call(bf16[64,4096]{1,0:T(8,128)(2,1)S(1)} %broadcast_select_fusion.7.refs_0_, bf16[64,4096]{1,0:T(8,128)(2,1)S(1)} %broadcast_select_fusion.6.refs_1_, ...), custom_call_target="tpu_custom_call", output_to_operand_aliasing={{0}: (6, {}), {1}: (7, {})} | custom-call | tf_op jit(solution)/shard_map/project/pallas_call | solution.py:285
  128.2 7.1 %load.1 = (bf16[1024,4096]{1,0:T(8,128)(2,1)S(1)}, bf16[4096,1024]{1,0:T(8,128)(2,1)S(1)}, bf16[1024,1024]{1,0:T(8,128)(2,1)S(1)}, bf16[1024,1024]{1,0:T(8,128)(2,1)S(1)}) custom-call(bf16[1024,4096]{1,0:T(8,128)(2,1)} %bitcast.66, bf16[4096,1024]{1,0:T(8,128)(2,1)} %bitcast.67, bf16[1024,1024]{1,0:T(8,128)(2,1)} %copy-done.11, bf16[1024,1024]{1,0:T(8,128)(2,1)} %copy-done.15), custom_call_target="tpu_custom_call" | custom-call | tf_op jit(solution)/shard_map/load/pallas_call | solution.py:212
  135.7 22.0 %probs.1.refs_6_.p_ref = bf16[4,8,128,1024]{3,2,1,0:T(8,128)(2,1)} custom-call(bf16[256,1024]{1,0:T(8,128)(2,1)S(1)} %convolution_convert_fusion.q_ref, bf16[1024,1024]{1,0:T(8,128)(2,1)S(1)} %copy-done.12, s32[4,128,1]{2,1,0:T(8,128)S(1)} %copy.77.tok_ref, s32[1,1024]{1,0:T(1,128)S(1)} %bitcast.65), custom_call_target="tpu_custom_call" | custom-call | tf_op jit(solution)/shard_map/probs/pallas_call | solution.py:288
  157.7 11.5 %turn.10 = (bf16[32,4096]{1,0:T(8,128)(2,1)S(1)}, bf16[32,4096]{1,0:T(8,128)(2,1)S(1)}, bf16[5,8,128,1024]{3,2,1,0:T(8,128)(2,1)}, bf16[5,64,1024]{2,1,0:T(8,128)(2,1)}) custom-call(s32[10,2]{1,0:T(8,128)S(1)} %copy.97.slots, bf16[32,4096]{1,0:T(8,128)(2,1)S(1)} %get-tuple-element.190.refs_0_.refs_2_, bf16[32,4096]{1,0:T(8,128)(2,1)} %collective-permute-done.20.refs_1_, ...), custom_call_target="tpu_custom_call" | custom-call | tf_op jit(solution)/shard_map/turn/pallas_call | solution.py:309
  175.3 11.5 %turn.11 = (bf16[32,4096]{1,0:T(8,128)(2,1)S(1)}, bf16[32,4096]{1,0:T(8,128)(2,1)S(1)}, bf16[5,8,128,1024]{3,2,1,0:T(8,128)(2,1)}, bf16[5,64,1024]{2,1,0:T(8,128)(2,1)}) custom-call(s32[10,2]{1,0:T(8,128)S(1)} %copy.97.slots, bf16[32,4096]{1,0:T(8,128)(2,1)S(1)} %get-tuple-element.193.refs_0_.refs_2_, ...), custom_call_target="tpu_custom_call", output_to_operand_aliasing={{2}: (8, {}), {3}: (9, {})} | custom-call | tf_op jit(solution)/shard_map/turn/pallas_call | solution.py:309
  192.4 11.5 %turn.12 = (bf16[32,4096]{1,0:T(8,128)(2,1)S(1)}, bf16[32,4096]{1,0:T(8,128)(2,1)S(1)}, bf16[5,8,128,1024]{3,2,1,0:T(8,128)(2,1)}, bf16[5,64,1024]{2,1,0:T(8,128)(2,1)}) custom-call(s32[10,2]{1,0:T(8,128)S(1)} %copy.97.slots, bf16[32,4096]{1,0:T(8,128)(2,1)S(1)} %broadcast_select_fusion.9.refs_0_.refs_2_, ...), custom_call_target="tpu_custom_call", output_to_operand_aliasing={{2}: (8, {}), {3}: (9, {})} | custom-call | tf_op jit(solution)/shard_map/turn/pallas_call | solution.py:309
  209.5 11.5 %turn.13 = (bf16[32,4096]{1,0:T(8,128)(2,1)S(1)}, bf16[32,4096]{1,0:T(8,128)(2,1)S(1)}, bf16[5,8,128,1024]{3,2,1,0:T(8,128)(2,1)}, bf16[5,64,1024]{2,1,0:T(8,128)(2,1)}) custom-call(s32[10,2]{1,0:T(8,128)S(1)} %copy.97.slots, bf16[32,4096]{1,0:T(8,128)(2,1)S(1)} %broadcast_select_fusion.8.refs_0_.refs_2_, ...), custom_call_target="tpu_custom_call", output_to_operand_aliasing={{2}: (8, {}), {3}: (9, {})} | custom-call | tf_op jit(solution)/shard_map/turn/pallas_call | solution.py:309
  226.7 11.5 %turn.14 = (bf16[32,4096]{1,0:T(8,128)(2,1)S(1)}, bf16[32,4096]{1,0:T(8,128)(2,1)S(1)}, bf16[5,8,128,1024]{3,2,1,0:T(8,128)(2,1)}, bf16[5,64,1024]{2,1,0:T(8,128)(2,1)}) custom-call(s32[10,2]{1,0:T(8,128)S(1)} %copy.97.slots, bf16[32,4096]{1,0:T(8,128)(2,1)S(1)} %collective-permute-done.31.refs_0_.refs_2_, ...), custom_call_target="tpu_custom_call", output_to_operand_aliasing={{2}: (8, {}), {3}: (9, {})} | custom-call | tf_op jit(solution)/shard_map/turn/pallas_call | solution.py:309
  243.8 11.5 %turn.15 = (bf16[32,4096]{1,0:T(8,128)(2,1)S(1)}, bf16[32,4096]{1,0:T(8,128)(2,1)S(1)}, bf16[5,8,128,1024]{3,2,1,0:T(8,128)(2,1)}, bf16[5,64,1024]{2,1,0:T(8,128)(2,1)}) custom-call(s32[10,2]{1,0:T(8,128)S(1)} %copy.97.slots, bf16[32,4096]{1,0:T(8,128)(2,1)S(1)} %collective-permute-done.29.refs_0_.refs_2_, ...), custom_call_target="tpu_custom_call", output_to_operand_aliasing={{2}: (8, {}), {3}: (9, {})} | custom-call | tf_op jit(solution)/shard_map/turn/pallas_call | solution.py:309
  260.8 11.5 %turn.16 = (bf16[32,4096]{1,0:T(8,128)(2,1)S(1)}, bf16[32,4096]{1,0:T(8,128)(2,1)S(1)}, bf16[5,8,128,1024]{3,2,1,0:T(8,128)(2,1)}, bf16[5,64,1024]{2,1,0:T(8,128)(2,1)}) custom-call(s32[10,2]{1,0:T(8,128)S(1)} %copy.97.slots, bf16[32,4096]{1,0:T(8,128)(2,1)S(1)} %collective-permute-done.37.refs_0_.refs_2_, ...), custom_call_target="tpu_custom_call", output_to_operand_aliasing={{2}: (8, {}), {3}: (9, {})} | custom-call | tf_op jit(solution)/shard_map/turn/pallas_call | solution.py:309
  277.9 11.5 %turn.17 = (bf16[32,4096]{1,0:T(8,128)(2,1)S(1)}, bf16[32,4096]{1,0:T(8,128)(2,1)S(1)}, bf16[5,8,128,1024]{3,2,1,0:T(8,128)(2,1)}, bf16[5,64,1024]{2,1,0:T(8,128)(2,1)}) custom-call(s32[10,2]{1,0:T(8,128)S(1)} %copy.97.slots, bf16[32,4096]{1,0:T(8,128)(2,1)S(1)} %collective-permute-done.35.refs_0_.refs_2_, ...), custom_call_target="tpu_custom_call", output_to_operand_aliasing={{2}: (8, {}), {3}: (9, {})} | custom-call | tf_op jit(solution)/shard_map/turn/pallas_call | solution.py:309
  295.2 11.6 %turn.18 = (bf16[32,4096]{1,0:T(8,128)(2,1)S(1)}, bf16[32,4096]{1,0:T(8,128)(2,1)}, bf16[5,8,128,1024]{3,2,1,0:T(8,128)(2,1)}, bf16[5,64,1024]{2,1,0:T(8,128)(2,1)}) custom-call(s32[10,2]{1,0:T(8,128)S(1)} %copy.97.slots, bf16[32,4096]{1,0:T(8,128)(2,1)S(1)} %collective-permute-done.43.refs_0_.refs_2_, ...), custom_call_target="tpu_custom_call", output_to_operand_aliasing={{2}: (8, {}), {3}: (9, {})} | custom-call | tf_op jit(solution)/shard_map/turn/pallas_call | solution.py:309
  318.3 11.5 %turn.19 = (bf16[32,4096]{1,0:T(8,128)(2,1)S(1)}, bf16[32,4096]{1,0:T(8,128)(2,1)S(1)}, bf16[5,8,128,1024]{3,2,1,0:T(8,128)(2,1)}, bf16[5,64,1024]{2,1,0:T(8,128)(2,1)}) custom-call(s32[10,2]{1,0:T(8,128)S(1)} %copy.97.slots, bf16[32,4096]{1,0:T(8,128)(2,1)S(1)} %collective-permute-done.41.refs_0_.refs_2_, ...), custom_call_target="tpu_custom_call", output_to_operand_aliasing={{2}: (8, {}), {3}: (9, {})} | custom-call | tf_op jit(solution)/shard_map/turn/pallas_call | solution.py:309
  329.8 11.6 %grads.1 = (bf16[1024,1024]{1,0:T(8,128)(2,1)S(1)}, bf16[1024,1024]{1,0:T(8,128)(2,1)S(1)}) custom-call(bf16[5,8,128,1024]{3,2,1,0:T(8,128)(2,1)} %get-tuple-element.158.ds_ref, bf16[4,8,128,1024]{3,2,1,0:T(8,128)(2,1)} %probs.1.refs_6_.p_ref, bf16[256,1024]{1,0:T(8,128)(2,1)} %copy-done.16, bf16[5,64,1024]{2,1,0:T(8,128)(2,1)} %get-tuple-element.159.ag_ref), custom_call_target="tpu_custom_call" | custom-call | tf_op jit(solution)/shard_map/grads/pallas_call | solution.py:388
  344.8 6.1 %back.5 = (bf16[128,4096]{1,0:T(8,128)(2,1)S(1)}, bf16[128,4096]{1,0:T(8,128)(2,1)S(1)}) custom-call(bf16[1024,1024]{1,0:T(8,128)(2,1)S(1)} %get-tuple-element.160.kg_ref, bf16[1024,1024]{1,0:T(8,128)(2,1)S(1)} %get-tuple-element.161.vg_ref, bf16[4096,1024]{1,0:T(8,128)(2,1)S(1)} %bitcast.50, bf16[4096,1024]{1,0:T(8,128)(2,1)S(1)} %bitcast.60), custom_call_target="tpu_custom_call" | custom-call | tf_op jit(solution)/shard_map/back/pallas_call | solution.py:410
  350.9 6.1 %back.7 = (bf16[128,4096]{1,0:T(8,128)(2,1)S(1)}, bf16[128,4096]{1,0:T(8,128)(2,1)S(1)}) custom-call(bf16[1024,1024]{1,0:T(8,128)(2,1)S(1)} %get-tuple-element.160.kg_ref, bf16[1024,1024]{1,0:T(8,128)(2,1)S(1)} %get-tuple-element.161.vg_ref, bf16[4096,1024]{1,0:T(8,128)(2,1)S(1)} %bitcast.51, bf16[4096,1024]{1,0:T(8,128)(2,1)S(1)} %bitcast.61), custom_call_target="tpu_custom_call" | custom-call | tf_op jit(solution)/shard_map/back/pallas_call | solution.py:410
  357.0 6.1 %back.6 = (bf16[128,4096]{1,0:T(8,128)(2,1)S(1)}, bf16[128,4096]{1,0:T(8,128)(2,1)S(1)}) custom-call(bf16[1024,1024]{1,0:T(8,128)(2,1)S(1)} %get-tuple-element.160.kg_ref, bf16[1024,1024]{1,0:T(8,128)(2,1)S(1)} %get-tuple-element.161.vg_ref, bf16[4096,1024]{1,0:T(8,128)(2,1)S(1)} %bitcast.52, bf16[4096,1024]{1,0:T(8,128)(2,1)S(1)} %bitcast.62), custom_call_target="tpu_custom_call" | custom-call | tf_op jit(solution)/shard_map/back/pallas_call | solution.py:410
  363.1 6.1 %back.4 = (bf16[128,4096]{1,0:T(8,128)(2,1)S(1)}, bf16[128,4096]{1,0:T(8,128)(2,1)S(1)}) custom-call(bf16[1024,1024]{1,0:T(8,128)(2,1)S(1)} %get-tuple-element.160.kg_ref, bf16[1024,1024]{1,0:T(8,128)(2,1)S(1)} %get-tuple-element.161.vg_ref, bf16[4096,1024]{1,0:T(8,128)(2,1)S(1)} %bitcast.53, bf16[4096,1024]{1,0:T(8,128)(2,1)S(1)} %bitcast.63), custom_call_target="tpu_custom_call" | custom-call | tf_op jit(solution)/shard_map/back/pallas_call | solution.py:410
  372.7 8.6 %collective-permute-start.51 = (bf16[64,4096]{1,0:T(8,128)(2,1)S(1)}, bf16[64,4096]{1,0:T(8,128)(2,1)S(1)}, u32[]{:S(2)}, u32[]{:S(2)}) collective-permute-start(bf16[64,4096]{1,0:T(8,128)(2,1)S(1)} %get-tuple-element.186), channel_id=1, source_target_pairs={{0,2},{6,4},{1,3},{7,5},{8,10},{14,12},{9,11},{15,13},{16,18},{22,... | collective-permute-start | bytes 1572872 | tf_op jit(solution)/shard_map/ppermute | solution.py:199
  383.4 10.2 %collective-permute-done.51 = bf16[64,4096]{1,0:T(8,128)(2,1)S(1)} collective-permute-done((bf16[64,4096]{1,0:T(8,128)(2,1)S(1)}, bf16[64,4096]{1,0:T(8,128)(2,1)S(1)}, u32[]{:S(2)}, u32[]{:S(2)}) %collective-permute-start.51) | collective-permute-done | bytes 524320 | tf_op jit(solution)/shard_map/ppermute | solution.py:199
  393.6 10.6 %collective-permute-done.60 = bf16[64,4096]{1,0:T(8,128)(2,1)S(1)} collective-permute-done((bf16[64,4096]{1,0:T(8,128)(2,1)S(1)}, bf16[64,4096]{1,0:T(8,128)(2,1)S(1)}, u32[]{:S(2)}, u32[]{:S(2)}) %collective-permute-start.60) | collective-permute-done | bytes 524320 | tf_op jit(solution)/shard_map/ppermute | solution.py:199
  410.5 6.9 %collective-permute-start.61 = (bf16[64,4096]{1,0:T(8,128)(2,1)S(1)}, bf16[64,4096]{1,0:T(8,128)(2,1)S(1)}, u32[]{:S(2)}, u32[]{:S(2)}) collective-permute-start(bf16[64,4096]{1,0:T(8,128)(2,1)S(1)} %get-tuple-element.183), channel_id=1, source_target_pairs={{0,2},{2,4},{1,3},{3,5},{8,10},{10,12},{9,11},{11,13},{16,18},{18,... | collective-permute-start | bytes 1572872 | tf_op jit(solution)/shard_map/ppermute | solution.py:199
  421.4 9.7 %collective-permute-done.61 = bf16[64,4096]{1,0:T(8,128)(2,1)S(1)} collective-permute-done((bf16[64,4096]{1,0:T(8,128)(2,1)S(1)}, bf16[64,4096]{1,0:T(8,128)(2,1)S(1)}, u32[]{:S(2)}, u32[]{:S(2)}) %collective-permute-start.61) | collective-permute-done | bytes 524320 | tf_op jit(solution)/shard_map/ppermute | solution.py:199
  433.5 10.1 %collective-permute-start.53 = (bf16[64,4096]{1,0:T(8,128)(2,1)S(1)}, bf16[64,4096]{1,0:T(8,128)(2,1)S(1)}, u32[]{:S(2)}, u32[]{:S(2)}) collective-permute-start(bf16[64,4096]{1,0:T(8,128)(2,1)S(1)} %get-tuple-element.170), channel_id=1, source_target_pairs={{0,2},{2,4},{4,6},{1,3},{3,5},{5,7},{8,10},{10,12},{12,14},{9,11},... | collective-permute-start | bytes 1572872 | tf_op jit(solution)/shard_map/ppermute | solution.py:199
  455.9 7.3 %collective-permute-done.64 = bf16[64,4096]{1,0:T(8,128)(2,1)S(1)} collective-permute-done((bf16[64,4096]{1,0:T(8,128)(2,1)S(1)}, bf16[64,4096]{1,0:T(8,128)(2,1)S(1)}, u32[]{:S(2)}, u32[]{:S(2)}) %collective-permute-start.64) | collective-permute-done | bytes 524320 | tf_op jit(solution)/shard_map/ppermute | solution.py:199
  (255 shorter events, 149.6 us)
Async XLA Ops:
  2.0 19.2 %collective-permute-start.1 = (bf16[64,4096]{1,0:T(8,128)(2,1)S(1)}, bf16[64,4096]{1,0:T(8,128)(2,1)}, u32[]{:S(2)}, u32[]{:S(2)}) collective-permute-start(bf16[64,4096]{1,0:T(8,128)(2,1)S(1)} %get-tuple-element.199.refs_0_), channel_id=1, source_target_pairs={{6,4},{4,2},{2,0},{7,5},{5,3},{3,1},{14,12},{12,10},{10,8},{15,13}... | collective-permute-start | bytes 1572872 | tf_op jit(solution)/shard_map/ppermute | solution.py:199
  3.3 18.5 %collective-permute-start.3 = (bf16[64,4096]{1,0:T(8,128)(2,1)S(1)}, bf16[64,4096]{1,0:T(8,128)(2,1)}, u32[]{:S(2)}, u32[]{:S(2)}) collective-permute-start(bf16[64,4096]{1,0:T(8,128)(2,1)S(1)} %get-tuple-element.199.refs_0_), channel_id=1, source_target_pairs={{0,2},{2,4},{4,6},{1,3},{3,5},{5,7},{8,10},{10,12},{12,14},{9,11},... | collective-permute-start | bytes 1572872 | tf_op jit(solution)/shard_map/ppermute | solution.py:199
  9.7 20.5 %collective-permute-start.7 = (bf16[64,4096]{1,0:T(8,128)(2,1)S(1)}, bf16[64,4096]{1,0:T(8,128)(2,1)}, u32[]{:S(2)}, u32[]{:S(2)}) collective-permute-start(bf16[64,4096]{1,0:T(8,128)(2,1)S(1)} %get-tuple-element.198.refs_1_), channel_id=1, source_target_pairs={{6,4},{4,2},{2,0},{7,5},{5,3},{3,1},{14,12},{12,10},{10,8},{15,13}... | collective-permute-start | bytes 1572872 | tf_op jit(solution)/shard_map/ppermute | solution.py:199
  11.0 20.3 %collective-permute-start.6 = (bf16[64,4096]{1,0:T(8,128)(2,1)S(1)}, bf16[64,4096]{1,0:T(8,128)(2,1)}, u32[]{:S(2)}, u32[]{:S(2)}) collective-permute-start(bf16[64,4096]{1,0:T(8,128)(2,1)S(1)} %get-tuple-element.198.refs_1_), channel_id=1, source_target_pairs={{0,2},{2,4},{4,6},{1,3},{3,5},{5,7},{8,10},{10,12},{12,14},{9,11},... | collective-permute-start | bytes 1572872 | tf_op jit(solution)/shard_map/ppermute | solution.py:199
  16.4 16.3 %collective-permute-start.17 = (bf16[64,4096]{1,0:T(8,128)(2,1)S(1)}, bf16[64,4096]{1,0:T(8,128)(2,1)S(1)}, u32[]{:S(2)}, u32[]{:S(2)}) collective-permute-start(bf16[64,4096]{1,0:T(8,128)(2,1)S(1)} %get-tuple-element.199.refs_0_), channel_id=1, source_target_pairs={{1,0},{0,1},{3,2},{2,3},{5,4},{4,5},{7,6},{6,7},{9,8},{8,9},{11,10... | collective-permute-start | bytes 1572872 | tf_op jit(solution)/shard_map/ppermute | solution.py:196
  21.8 24.4 %collective-permute-start.19 = (bf16[128,4096]{1,0:T(8,128)(2,1)}, bf16[128,4096]{1,0:T(8,128)(2,1)S(1)}, u32[]{:S(2)}, u32[]{:S(2)}) collective-permute-start(bf16[128,4096]{1,0:T(8,128)(2,1)} %bitcast.10.refs_3_), channel_id=1, source_target_pairs={{1,0},{0,1},{3,2},{2,3},{5,4},{4,5},{7,6},{6,7},{9,8},{8,9},{11,10... | collective-permute-start | bytes 3145736 | tf_op jit(solution)/shard_map/ppermute | solution.py:196
  30.3 127.4 %collective-permute-start.20 = (bf16[32,4096]{1,0:T(8,128)(2,1)S(1)}, bf16[32,4096]{1,0:T(8,128)(2,1)}, u32[]{:S(2)}, u32[]{:S(2)}) collective-permute-start(bf16[32,4096]{1,0:T(8,128)(2,1)S(1)} %get-tuple-element.190.refs_0_.refs_2_), channel_id=1, source_target_pairs={{1,0},{0,1},{3,2},{2,3},{5,4},{4,5},{7,6},{6,7},{9,8},{8,9},{11,10... | collective-permute-start | bytes 786440 | tf_op jit(solution)/shard_map/ppermute | solution.py:196
  32.6 68.3 %collective-permute-start.15 = (bf16[64,4096]{1,0:T(8,128)(2,1)S(1)}, bf16[64,4096]{1,0:T(8,128)(2,1)S(1)}, u32[]{:S(2)}, u32[]{:S(2)}) collective-permute-start(bf16[64,4096]{1,0:T(8,128)(2,1)S(1)} %get-tuple-element.196.refs_0_), channel_id=1, source_target_pairs={{1,0},{0,1},{3,2},{2,3},{5,4},{4,5},{7,6},{6,7},{9,8},{8,9},{11,10... | collective-permute-start | bytes 1572872 | tf_op jit(solution)/shard_map/ppermute | solution.py:196
  32.7 69.6 %collective-permute-start.16 = (bf16[64,4096]{1,0:T(8,128)(2,1)S(1)}, bf16[64,4096]{1,0:T(8,128)(2,1)S(1)}, u32[]{:S(2)}, u32[]{:S(2)}) collective-permute-start(bf16[64,4096]{1,0:T(8,128)(2,1)S(1)} %get-tuple-element.194.refs_1_), channel_id=1, source_target_pairs={{1,0},{0,1},{3,2},{2,3},{5,4},{4,5},{7,6},{6,7},{9,8},{8,9},{11,10... | collective-permute-start | bytes 1572872 | tf_op jit(solution)/shard_map/ppermute | solution.py:196
  33.2 19.6 %collective-permute-start.2 = (bf16[64,4096]{1,0:T(8,128)(2,1)}, bf16[64,4096]{1,0:T(8,128)(2,1)S(1)}, u32[]{:S(2)}, u32[]{:S(2)}) collective-permute-start(bf16[64,4096]{1,0:T(8,128)(2,1)} %collective-permute-done.1), channel_id=1, source_target_pairs={{4,2},{2,0},{5,3},{3,1},{12,10},{10,8},{13,11},{11,9},{20,18},{18,... | collective-permute-start | bytes 1572872 | tf_op jit(solution)/shard_map/ppermute | solution.py:199
  52.8 19.6 %collective-permute-start.8 = (bf16[64,4096]{1,0:T(8,128)(2,1)}, bf16[64,4096]{1,0:T(8,128)(2,1)S(1)}, u32[]{:S(2)}, u32[]{:S(2)}) collective-permute-start(bf16[64,4096]{1,0:T(8,128)(2,1)} %collective-permute-done.7), channel_id=1, source_target_pairs={{4,2},{2,0},{5,3},{3,1},{12,10},{10,8},{13,11},{11,9},{20,18},{18,... | collective-permute-start | bytes 1572872 | tf_op jit(solution)/shard_map/ppermute | solution.py:199
  54.2 19.5 %collective-permute-start.9 = (bf16[64,4096]{1,0:T(8,128)(2,1)}, bf16[64,4096]{1,0:T(8,128)(2,1)S(1)}, u32[]{:S(2)}, u32[]{:S(2)}) collective-permute-start(bf16[64,4096]{1,0:T(8,128)(2,1)} %collective-permute-done.6), channel_id=1, source_target_pairs={{2,4},{4,6},{3,5},{5,7},{10,12},{12,14},{11,13},{13,15},{18,20},{2... | collective-permute-start | bytes 1572872 | tf_op jit(solution)/shard_map/ppermute | solution.py:199
  72.4 14.7 %collective-permute-start.5 = (bf16[64,4096]{1,0:T(8,128)(2,1)S(1)}, bf16[64,4096]{1,0:T(8,128)(2,1)S(1)}, u32[]{:S(2)}, u32[]{:S(2)}) collective-permute-start(bf16[64,4096]{1,0:T(8,128)(2,1)S(1)} %broadcast_select_fusion.5.refs_0_), channel_id=1, source_target_pairs={{4,6},{2,0},{5,7},{3,1},{12,14},{10,8},{13,15},{11,9},{20,22},{18,... | collective-permute-start | bytes 1572872 | tf_op jit(solution)/shard_map/ppermute | solution.py:199
  73.7 41.9 %collective-permute-start.13 = (bf16[64,4096]{1,0:T(8,128)(2,1)S(1)}, bf16[64,4096]{1,0:T(8,128)(2,1)S(1)}, u32[]{:S(2)}, u32[]{:S(2)}) collective-permute-start(bf16[64,4096]{1,0:T(8,128)(2,1)S(1)} %broadcast_select_fusion.5.refs_0_), channel_id=1, source_target_pairs={{1,0},{0,1},{3,2},{2,3},{5,4},{4,5},{7,6},{6,7},{9,8},{8,9},{11,10... | collective-permute-start | bytes 1572872 | tf_op jit(solution)/shard_map/ppermute | solution.py:196
  100.9 14.7 %collective-permute-start.14 = (bf16[64,4096]{1,0:T(8,128)(2,1)S(1)}, bf16[64,4096]{1,0:T(8,128)(2,1)S(1)}, u32[]{:S(2)}, u32[]{:S(2)}) collective-permute-start(bf16[64,4096]{1,0:T(8,128)(2,1)S(1)} %broadcast_select_fusion.2.refs_1_), channel_id=1, source_target_pairs={{1,0},{0,1},{3,2},{2,3},{5,4},{4,5},{7,6},{6,7},{9,8},{8,9},{11,10... | collective-permute-start | bytes 1572872 | tf_op jit(solution)/shard_map/ppermute | solution.py:196
  101.8 18.8 %collective-permute-start.11 = (bf16[64,4096]{1,0:T(8,128)(2,1)S(1)}, bf16[64,4096]{1,0:T(8,128)(2,1)S(1)}, u32[]{:S(2)}, u32[]{:S(2)}) collective-permute-start(bf16[64,4096]{1,0:T(8,128)(2,1)S(1)} %broadcast_select_fusion.7.refs_0_), channel_id=1, source_target_pairs={{1,0},{0,1},{3,2},{2,3},{5,4},{4,5},{7,6},{6,7},{9,8},{8,9},{11,10... | collective-permute-start | bytes 1572872 | tf_op jit(solution)/shard_map/ppermute | solution.py:196
  103.1 17.5 %collective-permute-start.12 = (bf16[64,4096]{1,0:T(8,128)(2,1)S(1)}, bf16[64,4096]{1,0:T(8,128)(2,1)S(1)}, u32[]{:S(2)}, u32[]{:S(2)}) collective-permute-start(bf16[64,4096]{1,0:T(8,128)(2,1)S(1)} %broadcast_select_fusion.6.refs_1_), channel_id=1, source_target_pairs={{1,0},{0,1},{3,2},{2,3},{5,4},{4,5},{7,6},{6,7},{9,8},{8,9},{11,10... | collective-permute-start | bytes 1572872 | tf_op jit(solution)/shard_map/ppermute | solution.py:196
  276.6 14.3 %collective-permute-start.43 = (bf16[32,4096]{1,0:T(8,128)(2,1)S(1)}, bf16[32,4096]{1,0:T(8,128)(2,1)S(1)}, u32[]{:S(2)}, u32[]{:S(2)}) collective-permute-start(bf16[32,4096]{1,0:T(8,128)(2,1)S(1)} %get-tuple-element.146), channel_id=1, source_target_pairs={{6,4},{4,2},{2,0},{7,5},{5,3},{3,1},{14,12},{12,10},{10,8},{15,13}... | collective-permute-start | bytes 786440 | tf_op jit(solution)/shard_map/ppermute | solution.py:199
  293.7 14.9 %collective-permute-start.41 = (bf16[32,4096]{1,0:T(8,128)(2,1)S(1)}, bf16[32,4096]{1,0:T(8,128)(2,1)S(1)}, u32[]{:S(2)}, u32[]{:S(2)}) collective-permute-start(bf16[32,4096]{1,0:T(8,128)(2,1)S(1)} %get-tuple-element.145), channel_id=1, source_target_pairs={{6,4},{4,2},{2,0},{7,5},{5,3},{3,1},{14,12},{12,10},{10,8},{15,13}... | collective-permute-start | bytes 786440 | tf_op jit(solution)/shard_map/ppermute | solution.py:199
  369.2 40.6 %collective-permute-start.46 = (bf16[32,4096]{1,0:T(8,128)(2,1)S(1)}, bf16[32,4096]{1,0:T(8,128)(2,1)S(1)}, u32[]{:S(2)}, u32[]{:S(2)}) collective-permute-start(bf16[32,4096]{1,0:T(8,128)(2,1)S(1)} %get-tuple-element.155), channel_id=1, source_target_pairs={{1,0},{0,1},{3,2},{2,3},{5,4},{4,5},{7,6},{6,7},{9,8},{8,9},{11,10... | collective-permute-start | bytes 786440 | tf_op jit(solution)/shard_map/ppermute | solution.py:196
  372.7 20.9 %collective-permute-start.51 = (bf16[64,4096]{1,0:T(8,128)(2,1)S(1)}, bf16[64,4096]{1,0:T(8,128)(2,1)S(1)}, u32[]{:S(2)}, u32[]{:S(2)}) collective-permute-start(bf16[64,4096]{1,0:T(8,128)(2,1)S(1)} %get-tuple-element.186), channel_id=1, source_target_pairs={{0,2},{6,4},{1,3},{7,5},{8,10},{14,12},{9,11},{15,13},{16,18},{22,... | collective-permute-start | bytes 1572872 | tf_op jit(solution)/shard_map/ppermute | solution.py:199
  381.4 22.8 %collective-permute-start.60 = (bf16[64,4096]{1,0:T(8,128)(2,1)S(1)}, bf16[64,4096]{1,0:T(8,128)(2,1)S(1)}, u32[]{:S(2)}, u32[]{:S(2)}) collective-permute-start(bf16[64,4096]{1,0:T(8,128)(2,1)S(1)} %get-tuple-element.187), channel_id=1, source_target_pairs={{0,2},{6,4},{1,3},{7,5},{8,10},{14,12},{9,11},{15,13},{16,18},{22,... | collective-permute-start | bytes 1572872 | tf_op jit(solution)/shard_map/ppermute | solution.py:199
  382.8 27.7 %collective-permute-start.49 = (bf16[64,4096]{1,0:T(8,128)(2,1)S(1)}, bf16[64,4096]{1,0:T(8,128)(2,1)S(1)}, u32[]{:S(2)}, u32[]{:S(2)}) collective-permute-start(bf16[64,4096]{1,0:T(8,128)(2,1)S(1)} %get-tuple-element.180), channel_id=1, source_target_pairs={{1,0},{0,1},{3,2},{2,3},{5,4},{4,5},{7,6},{6,7},{9,8},{8,9},{11,10... | collective-permute-start | bytes 1572872 | tf_op jit(solution)/shard_map/ppermute | solution.py:196
  382.9 37.4 %collective-permute-start.58 = (bf16[64,4096]{1,0:T(8,128)(2,1)S(1)}, bf16[64,4096]{1,0:T(8,128)(2,1)S(1)}, u32[]{:S(2)}, u32[]{:S(2)}) collective-permute-start(bf16[64,4096]{1,0:T(8,128)(2,1)S(1)} %get-tuple-element.181), channel_id=1, source_target_pairs={{1,0},{0,1},{3,2},{2,3},{5,4},{4,5},{7,6},{6,7},{9,8},{8,9},{11,10... | collective-permute-start | bytes 1572872 | tf_op jit(solution)/shard_map/ppermute | solution.py:196
  404.7 16.7 %collective-permute-start.52 = (bf16[64,4096]{1,0:T(8,128)(2,1)S(1)}, bf16[64,4096]{1,0:T(8,128)(2,1)S(1)}, u32[]{:S(2)}, u32[]{:S(2)}) collective-permute-start(bf16[64,4096]{1,0:T(8,128)(2,1)S(1)} %get-tuple-element.182), channel_id=1, source_target_pairs={{0,2},{2,4},{1,3},{3,5},{8,10},{10,12},{9,11},{11,13},{16,18},{18,... | collective-permute-start | bytes 1572872 | tf_op jit(solution)/shard_map/ppermute | solution.py:199
  410.5 20.5 %collective-permute-start.61 = (bf16[64,4096]{1,0:T(8,128)(2,1)S(1)}, bf16[64,4096]{1,0:T(8,128)(2,1)S(1)}, u32[]{:S(2)}, u32[]{:S(2)}) collective-permute-start(bf16[64,4096]{1,0:T(8,128)(2,1)S(1)} %get-tuple-element.183), channel_id=1, source_target_pairs={{0,2},{2,4},{1,3},{3,5},{8,10},{10,12},{9,11},{11,13},{16,18},{18,... | collective-permute-start | bytes 1572872 | tf_op jit(solution)/shard_map/ppermute | solution.py:199
  420.3 24.6 %collective-permute-start.47 = (bf16[64,4096]{1,0:T(8,128)(2,1)S(1)}, bf16[64,4096]{1,0:T(8,128)(2,1)S(1)}, u32[]{:S(2)}, u32[]{:S(2)}) collective-permute-start(bf16[64,4096]{1,0:T(8,128)(2,1)S(1)} %get-tuple-element.178), channel_id=1, source_target_pairs={{1,0},{0,1},{3,2},{2,3},{5,4},{4,5},{7,6},{6,7},{9,8},{8,9},{11,10... | collective-permute-start | bytes 1572872 | tf_op jit(solution)/shard_map/ppermute | solution.py:196
  421.4 29.3 %collective-permute-start.56 = (bf16[64,4096]{1,0:T(8,128)(2,1)S(1)}, bf16[64,4096]{1,0:T(8,128)(2,1)S(1)}, u32[]{:S(2)}, u32[]{:S(2)}) collective-permute-start(bf16[64,4096]{1,0:T(8,128)(2,1)S(1)} %get-tuple-element.179), channel_id=1, source_target_pairs={{1,0},{0,1},{3,2},{2,3},{5,4},{4,5},{7,6},{6,7},{9,8},{8,9},{11,10... | collective-permute-start | bytes 1572872 | tf_op jit(solution)/shard_map/ppermute | solution.py:196
  432.2 22.2 %collective-permute-start.55 = (bf16[64,4096]{1,0:T(8,128)(2,1)S(1)}, bf16[64,4096]{1,0:T(8,128)(2,1)S(1)}, u32[]{:S(2)}, u32[]{:S(2)}) collective-permute-start(bf16[64,4096]{1,0:T(8,128)(2,1)S(1)} %get-tuple-element.171), channel_id=1, source_target_pairs={{6,4},{4,2},{2,0},{7,5},{5,3},{3,1},{14,12},{12,10},{10,8},{15,13}... | collective-permute-start | bytes 1572872 | tf_op jit(solution)/shard_map/ppermute | solution.py:199
  433.5 22.4 %collective-permute-start.53 = (bf16[64,4096]{1,0:T(8,128)(2,1)S(1)}, bf16[64,4096]{1,0:T(8,128)(2,1)S(1)}, u32[]{:S(2)}, u32[]{:S(2)}) collective-permute-start(bf16[64,4096]{1,0:T(8,128)(2,1)S(1)} %get-tuple-element.170), channel_id=1, source_target_pairs={{0,2},{2,4},{4,6},{1,3},{3,5},{5,7},{8,10},{10,12},{12,14},{9,11},... | collective-permute-start | bytes 1572872 | tf_op jit(solution)/shard_map/ppermute | solution.py:199
  443.6 19.6 %collective-permute-start.64 = (bf16[64,4096]{1,0:T(8,128)(2,1)S(1)}, bf16[64,4096]{1,0:T(8,128)(2,1)S(1)}, u32[]{:S(2)}, u32[]{:S(2)}) collective-permute-start(bf16[64,4096]{1,0:T(8,128)(2,1)S(1)} %get-tuple-element.174), channel_id=1, source_target_pairs={{6,4},{4,2},{2,0},{7,5},{5,3},{3,1},{14,12},{12,10},{10,8},{15,13}... | collective-permute-start | bytes 1572872 | tf_op jit(solution)/shard_map/ppermute | solution.py:199
  444.9 19.4 %collective-permute-start.62 = (bf16[64,4096]{1,0:T(8,128)(2,1)S(1)}, bf16[64,4096]{1,0:T(8,128)(2,1)S(1)}, u32[]{:S(2)}, u32[]{:S(2)}) collective-permute-start(bf16[64,4096]{1,0:T(8,128)(2,1)S(1)} %get-tuple-element.175), channel_id=1, source_target_pairs={{0,2},{2,4},{4,6},{1,3},{3,5},{5,7},{8,10},{10,12},{12,14},{9,11},... | collective-permute-start | bytes 1572872 | tf_op jit(solution)/shard_map/ppermute | solution.py:199
  (72 other events, 1102.5 us)

commit v2 on v1

--- a/solution.py
+++ b/solution.py
@@ -11,7 +11,7 @@
 PAIR = 2 * HD
 MICRO = 4
 SKEW = 2
-PIECES = 2
+PIECES = 1
 BLOCK = 512
 OUT_BLOCK = 512
 SLOTS = ((0, 1, 2, 3), (1, 2, 1, 2), (2, 3, 0, 1), (3, 0, 3, 0))
@@ -36,27 +36,34 @@
     )
 
 
-def probs_kernel(q_ref, k_ref, tok_ref, key_ref, p_ref):
+def probs_kernel(q_ref, k_ref, tok_ref, key_ref, wo_ref, wq_ref, p_ref, wo_out, wq_out, sems):
+    first = (pl.program_id(0) == 0) & (pl.program_id(1) == 0)
+    last = pl.program_id(0) == pl.num_programs(0) - 1
+    last = last & (pl.program_id(1) == pl.num_programs(1) - 1)
+    copies = [
+        pltpu.make_async_copy(wo_ref, wo_out, sems.at[0]),
+        pltpu.make_async_copy(wq_ref, wq_out, sems.at[1]),
+    ]
+
+    @pl.when(first)
+    def _():
+        for copy in copies:
+            copy.start()
+
     q = stacked(q_ref[...].astype(f32) * (HD**-0.5)).astype(bf16)
     s = dot(q, k_ref[...], NT)
     s = jnp.where(tok_ref[0] == key_ref[...], s, masked_value)
     e = jnp.exp(s - jnp.max(s, axis=-1, keepdims=True))
     total = jnp.sum(e, axis=-1, keepdims=True)
-    p_ref[0, 0] = (e * (1.0 / total)).astype(bf16)
-
-
-def load_kernel(count, *refs):
-    sems = refs[-1]
-    copies = [
-        pltpu.make_async_copy(refs[i], refs[count + i], sems.at[i]) for i in range(count)
-    ]
-    for copy in copies:
-        copy.start()
-    for copy in copies:
-        copy.wait()
-
-
-def project_kernel(count, *refs):
+    p_ref[pl.program_id(1), pl.program_id(0)] = (e * (1.0 / total)).astype(bf16)
+
+    @pl.when(last)
+    def _():
+        for copy in copies:
+            copy.wait()
+
+
+def project_kernel(count, slot, block, *refs):
     x_refs = refs[:count]
     wk_ref, wv_ref = refs[count : count + 2]
     k_ref, v_ref, x_all = refs[-3:]
@@ -68,33 +75,30 @@
             x_all[start : start + x.shape[0]] = x[...]
             start += x.shape[0]
 
-    block = k_ref.shape[1]
     cols = pl.ds(pl.multiple_of(pl.program_id(0) * block, block), block)
-    k_ref[...] = dot(x_all[...], wk_ref[:, cols], NN).astype(bf16)
-    v_ref[...] = dot(x_all[...], wv_ref[:, cols], NN).astype(bf16)
+    rows = slice(slot * x_all.shape[0], (slot + 1) * x_all.shape[0])
+    k_ref[rows, cols] = dot(x_all[...], wk_ref[:, cols], NN).astype(bf16)
+    v_ref[rows, cols] = dot(x_all[...], wv_ref[:, cols], NN).astype(bf16)
 
 
 def back_kernel(kg_ref, vg_ref, wk_ref, wv_ref, own_ref, other_ref):
-    block = own_ref.shape[1]
-    place = pl.ds(pl.multiple_of(pl.program_id(0) * block, block), block)
-    out = dot(kg_ref[...], wk_ref[place, :], NT) + dot(vg_ref[...], wv_ref[place, :], NT)
+    out = dot(kg_ref[...], wk_ref[...], NT) + dot(vg_ref[...], wv_ref[...], NT)
     rows = own_ref.shape[0]
     own_ref[...] = out[:rows].astype(bf16)
     other_ref[...] = out[rows:].astype(bf16)
 
 
-def turn_kernel(parts, own_rows, slots, *refs):
-    del slots
+def turn_kernel(parts, own_rows, t, block, slots, *refs):
+    read, write = slots[t, 0], slots[t, 1]
     up_refs = refs[:parts]
     wo_ref, wq_ref, k_ref, v_ref, p_ref = refs[parts : parts + 5]
     own_ref, other_ref, ds_ref, ag_ref, acc_ref = refs[-5:]
     step = pl.program_id(0)
-    block = ag_ref.shape[2]
     start = pl.multiple_of(step * block, block)
     up = up_refs[0][...] if parts == 1 else jnp.concatenate([r[...] for r in up_refs], axis=0)
     rows = up.shape[0]
     grads = dot(up, wo_ref[pl.ds(start, block), :], NT).astype(bf16)
-    ag_ref[0] = grads
+    ag_ref[write, :, pl.ds(start, block)] = grads
     wide = grads.astype(f32)
     lane = lax.broadcasted_iota(jnp.int32, (rows, PAIR), 1)
     pieces = []
@@ -102,10 +106,11 @@
         cols = pl.ds(pl.multiple_of(start + pair * PAIR, PAIR), PAIR)
         here = wide[:, pair * PAIR : (pair + 1) * PAIR]
         pg = dot(stacked(here).astype(bf16), v_ref[:, cols], NT)
-        p = p_ref[0, pair].astype(f32)
+        place = step * (block // PAIR) + pair
+        p = p_ref[read, place].astype(f32)
         mean = jnp.sum(pg * p, axis=-1, keepdims=True)
         ds = (p * (pg - mean)).astype(bf16)
-        ds_ref[0, pair] = ds
+        ds_ref[write, place] = ds
         both = dot(ds, k_ref[:, cols], NN)
         mine = jnp.where(lane < HD, both[:rows], both[rows:]) * (HD**-0.5)
         pieces.append(mine.astype(bf16))
@@ -126,12 +131,12 @@
         other_ref[...] = acc_ref[own_rows:].astype(bf16)
 
 
-def norm_kernel(received, slots, *refs):
-    del slots
+def norm_kernel(received, t, slots, *refs):
     got_refs = refs[:received]
     own_ref, up_ref, x_ref, gain_ref = refs[received : received + 4]
     mine_ref, all_ref = refs[-2:]
-    x = x_ref[...].astype(f32)
+    rows = mine_ref.shape[0]
+    x = x_ref[pl.ds(pl.multiple_of(slots[t, 0] * rows, rows), rows), :].astype(f32)
     recip = lax.rsqrt(jnp.mean(x * x, axis=-1, keepdims=True) + epsilon)
     unit = x * recip
     summed = own_ref[...].astype(f32)
@@ -143,18 +148,21 @@
     )
     out = out.astype(bf16)
     mine_ref[...] = out
-    all_ref[...] = out
+    all_ref[pl.ds(pl.multiple_of(slots[t, 1] * rows, rows), rows), :] = out
 
 
 def grads_kernel(micro, ds_ref, p_ref, q_ref, ag_ref, kg_ref, vg_ref):
     rows = ag_ref.shape[1]
-    enc = ds_ref.shape[-1]
+    pair = pl.program_id(0)
+    cols = pl.ds(pl.multiple_of(pair * PAIR, PAIR), PAIR)
     q = jnp.concatenate(
         [stacked(q_ref[i * rows : (i + 1) * rows, :].astype(f32)) for i in range(micro)], axis=0
     )
-    ag = jnp.concatenate([stacked(ag_ref[i].astype(f32)) for i in range(micro)], axis=0)
-    ds = ds_ref[:, 0].reshape(micro * 2 * rows, enc)
-    p = p_ref[:, 0].reshape(micro * 2 * rows, enc)
+    ag = jnp.concatenate(
+        [stacked(ag_ref[i, :, cols].astype(f32)) for i in range(micro)], axis=0
+    )
+    ds = jnp.concatenate([ds_ref[i, pair] for i in range(micro)], axis=0)
+    p = jnp.concatenate([p_ref[i, pair] for i in range(micro)], axis=0)
     kg = dot(q.T.astype(bf16), ds, NN) * (HD**-0.5)
     vg = dot(ag.T.astype(bf16), p, NN)
     kg_ref[...] = kg.T.astype(bf16)
@@ -190,7 +198,8 @@
     m = r * n
     tokens = own * n
     params = pltpu.CompilerParams(vmem_limit_bytes=24 * 1024 * 1024)
-    small = pltpu.CompilerParams(vmem_limit_bytes=14 * 1024 * 1024)
+    small = pltpu.CompilerParams(vmem_limit_bytes=12 * 1024 * 1024)
+    least = pltpu.CompilerParams(vmem_limit_bytes=8 * 1024 * 1024)
 
     def shifted(x, by):
         return lax.ppermute(x, "mp", [((i + by) % n, i) for i in range(n)])
@@ -200,7 +209,6 @@
 
     low = section < 2
     block = min(BLOCK, width)
-    bp = block // PAIR
     parts = 2 if n == 2 else 1
     any_spec = pl.BlockSpec(memory_space=pl.ANY)
     resident = pl.BlockSpec(memory_space=pltpu.MemorySpace.VMEM)
@@ -208,16 +216,8 @@
     def in_hbm(x):
         return pltpu.with_memory_space_constraint(x, pltpu.MemorySpace.HBM)
 
-    def loaded(*xs):
-        return pl.pallas_call(
-            functools.partial(load_kernel, len(xs)),
-            in_specs=[any_spec] * len(xs),
-            out_specs=[resident] * len(xs),
-            out_shape=[pltpu.MemorySpace.VMEM(x.shape, x.dtype) for x in xs],
-            scratch_shapes=[pltpu.SemaphoreType.DMA((len(xs),))],
-            compiler_params=small,
-            name="load",
-        )(*map(in_hbm, xs))
+    def in_vmem(shape):
+        return pltpu.MemorySpace.VMEM(shape, bf16)
 
     def all_parts(x):
         return [x] + [shifted(x, k) for k in range(1, n)]
@@ -241,6 +241,15 @@
         axis=0,
         keepdims=True,
     )
+    turns = MICRO + SKEW * (sections - 1)
+    micro = jnp.arange(turns, dtype=jnp.int32) - SKEW * (sections - 1 - section)
+    read = jnp.clip(micro, 0, MICRO - 1)
+    slots = jnp.stack([read, jnp.where(micro == read, read, MICRO)], axis=1)
+    outer = (section == 0) | (section == 3)
+    is_last = section == sections - 1
+    wk, wv, low, outer, is_last, slots = lax.optimization_barrier(
+        (wk, wv, low, outer, is_last, slots)
+    )
     size = share // PIECES
     mine = [enc_rows[0, i * size : (i + 1) * size] for i in range(PIECES)]
 
@@ -256,7 +265,6 @@
     down2 = ring(down1, (2, 1), (1, 0))
     third = [jnp.where(low, d, u) for u, d in zip(up2, down2)]
     third = ring(third, (2, 3), (1, 0))
-    outer = (section == 0) | (section == 3)
     near_in = [jnp.where(low, d, u) for u, d in zip(up1, down1)]
     far_in = lax.optimization_barrier([jnp.where(low, u, d) for u, d in zip(up1, down1)])
     mid_in = [jnp.where(low, d, u) for u, d in zip(up2, down2)]
@@ -267,25 +275,26 @@
     for slot, held in enumerate(slots_in):
         xs = [all_parts(v) for v in held]
         xs = [x[k] for k in range(n) for x in xs]
+        early = [] if slot else [slots, key_ids, token_ids]
         if n > 2:
             xs = [jnp.concatenate(xs, axis=0)]
         project = pl.pallas_call(
-            functools.partial(project_kernel, len(xs)),
+            functools.partial(project_kernel, len(xs), slot, block),
             grid=(width // block,),
             in_specs=[pl.BlockSpec(x.shape, lambda i: (0, 0)) for x in xs]
-            + [resident] * 2
-            + [any_spec] * len(keys_values),
-            out_specs=[pl.BlockSpec((rows, block), lambda i, slot=slot: (slot, i))] * 2,
-            out_shape=[jax.ShapeDtypeStruct((enc, width), bf16)] * 2,
+            + [resident] * (2 + len(keys_values))
+            + [any_spec] * len(early),
+            out_specs=[resident] * 2,
+            out_shape=[in_vmem((enc, width))] * 2,
             scratch_shapes=[pltpu.VMEM((rows, model), bf16)],
             input_output_aliases={len(xs) + 2 + i: i for i in range(len(keys_values))},
-            compiler_params=params,
+            compiler_params=small,
             name="project",
         )
-        keys_values = project(*xs, wk, wv, *keys_values)
+        keys_values = project(*xs, wk, wv, *keys_values, *early)
     keys, values = keys_values
 
-    probs = pl.pallas_call(
+    probs, *weights = pl.pallas_call(
         probs_kernel,
         grid=(pairs, MICRO),
         in_specs=[
@@ -293,81 +302,62 @@
             pl.BlockSpec((enc, PAIR), lambda p, i: (0, p)),
             pl.BlockSpec((1, 2 * m, 1), lambda p, i: (i, 0, 0)),
             pl.BlockSpec((1, enc), lambda p, i: (0, 0)),
+            any_spec,
+            any_spec,
         ],
-        out_specs=pl.BlockSpec((1, 1, 2 * m, enc), lambda p, i: (i, p, 0, 0)),
-        out_shape=pltpu.MemorySpace.HBM((MICRO, pairs, 2 * m, enc), bf16),
-        compiler_params=params,
+        out_specs=[resident] * 3,
+        out_shape=[
+            in_vmem((MICRO, pairs, 2 * m, enc)),
+            in_vmem(wo.shape),
+            in_vmem(wq.shape),
+        ],
+        scratch_shapes=[pltpu.SemaphoreType.DMA((2,))],
+        compiler_params=small,
         name="probs",
-    )(queries, keys, token_ids, key_ids)
-
-    weights = loaded(wo, wq, keys, values)
+    )(queries, keys, token_ids, key_ids, in_hbm(wo), in_hbm(wq))
+
 
     def turn(t, ups, held, after):
         if parts == 1:
             ups = [jnp.concatenate(ups, axis=0)] if n > 1 else ups
-        up_specs = [pl.BlockSpec(u.shape, lambda i, s: (0, 0)) for u in ups]
         return pl.pallas_call(
-            functools.partial(turn_kernel, parts, r),
+            functools.partial(turn_kernel, parts, r, t, block),
             grid_spec=pltpu.PrefetchScalarGridSpec(
                 num_scalar_prefetch=1,
                 grid=(width // block,),
-                in_specs=up_specs
-                + [resident] * 4
-                + [
-                    pl.BlockSpec((1, bp, 2 * m, enc), lambda i, s: (s[t, 0], i, 0, 0)),
-                ]
-                + [any_spec] * (len(held) + len(after)),
-                out_specs=[
-                    pl.BlockSpec((r, model), lambda i, s: (0, 0)),
-                    pl.BlockSpec((m - r, model), lambda i, s: (0, 0)),
-                    pl.BlockSpec((1, bp, 2 * m, enc), lambda i, s: (s[t, 1], i, 0, 0)),
-                    pl.BlockSpec((1, m, block), lambda i, s: (s[t, 1], 0, i)),
-                ],
+                in_specs=[resident] * (parts + 5 + len(held)) + [any_spec] * len(after),
+                out_specs=[resident] * 4,
                 scratch_shapes=[pltpu.VMEM((m, model), f32)],
             ),
             out_shape=[
-                jax.ShapeDtypeStruct((r, model), bf16),
-                jax.ShapeDtypeStruct((m - r, model), bf16),
-                pltpu.MemorySpace.HBM((MICRO + 1, pairs, 2 * m, enc), bf16),
-                pltpu.MemorySpace.HBM((MICRO + 1, m, width), bf16),
+                in_vmem((r, model)),
+                in_vmem((m - r, model)),
+                in_vmem((MICRO + 1, pairs, 2 * m, enc)),
+                in_vmem((MICRO + 1, m, width)),
             ],
             input_output_aliases={parts + 6 + i: 2 + i for i in range(len(held))},
-            compiler_params=small,
+            compiler_params=least,
             name="turn",
-        )(slots, *ups, *weights, in_hbm(probs), *map(in_hbm, held), *map(in_hbm, after))
+        )(slots, *ups, *weights, keys, values, probs, *held, *after)
 
     def norm_back(t, got, own_part, up_own, held):
-        row_spec = pl.BlockSpec((r, model), lambda i, s: (0, 0))
         k = len(got)
         return pl.pallas_call(
-            functools.partial(norm_kernel, k),
+            functools.partial(norm_kernel, k, t),
             grid_spec=pltpu.PrefetchScalarGridSpec(
                 num_scalar_prefetch=1,
                 grid=(1,),
-                in_specs=[row_spec] * (k + 2)
-                + [
-                    pl.BlockSpec((r, model), lambda i, s: (s[t, 0], 0)),
-                    pl.BlockSpec((1, model), lambda i, s: (0, 0)),
-                ]
-                + [any_spec] * len(held),
-                out_specs=[row_spec, pl.BlockSpec((r, model), lambda i, s: (s[t, 1], 0))],
+                in_specs=[resident] * (k + 4 + len(held)),
+                out_specs=[resident] * 2,
             ),
-            out_shape=[
-                jax.ShapeDtypeStruct((r, model), bf16),
-                pltpu.MemorySpace.HBM(((MICRO + 1) * r, model), bf16),
-            ],
+            out_shape=[in_vmem((r, model)), in_vmem(((MICRO + 1) * r, model))],
             input_output_aliases={k + 5: 1} if held else {},
-            compiler_params=small,
+            compiler_params=least,
             name="norm",
-        )(slots, *got, own_part, up_own, in_hbm(x_own), gain, *map(in_hbm, held))
+        )(slots, *got, own_part, up_own, x_own, gain, *held)
 
     held, dec_held = [], []
-    is_last = section == sections - 1
     hops = {}
-    turns = MICRO + SKEW * (sections - 1)
-    micro = jnp.arange(turns, dtype=jnp.int32) - SKEW * (sections - 1 - section)
-    read = jnp.clip(micro, 0, MICRO - 1)
-    slots = jnp.stack([read, jnp.where(micro == read, read, MICRO)], axis=1)
     for t in range(turns):
         if t < MICRO:
             up_own = cotangent[0, t * r : (t + 1) * r]
@@ -389,16 +379,16 @@
         functools.partial(grads_kernel, MICRO),
         grid=(pairs,),
         in_specs=[
-            pl.BlockSpec((MICRO, 1, 2 * m, enc), lambda p: (0, p, 0, 0)),
-            pl.BlockSpec((MICRO, 1, 2 * m, enc), lambda p: (0, p, 0, 0)),
+            resident,
+            resident,
             pl.BlockSpec((tokens, PAIR), lambda p: (0, p)),
-            pl.BlockSpec((MICRO, m, PAIR), lambda p: (0, 0, p)),
+            resident,
         ],
         out_specs=[pl.BlockSpec((enc, PAIR), lambda p: (0, p))] * 2,
         out_shape=[jax.ShapeDtypeStruct((enc, width), bf16)] * 2,
-        compiler_params=params,
+        compiler_params=small,
         name="grads",
-    )(*map(in_hbm, (held[0], probs, queries, held[1])))
+    )(held[0], probs, in_hbm(queries), held[1])
 
     out_block = min(OUT_BLOCK, model)
 
@@ -411,7 +401,7 @@
             back_kernel,
             grid=(model // out_block,),
             in_specs=[pl.BlockSpec((rows, width), lambda i: (slot, 0))] * 2
-            + [resident] * 2,
+            + [pl.BlockSpec((out_block, width), lambda i: (i, 0))] * 2,
             out_specs=[
                 pl.BlockSpec((share, out_block), lambda i: (0, i)),
                 pl.BlockSpec((rows - share, out_block), lambda i: (0, i)),
@@ -420,9 +410,9 @@
                 jax.ShapeDtypeStruct((share, model), bf16),
                 jax.ShapeDtypeStruct((rows - share, model), bf16),
             ],
-            compiler_params=params,
+            compiler_params=small,
             name="back",
-        )(kg, vg, wk, wv)
+        )(kg, vg, in_hbm(w_key[0]), in_hbm(w_value[0]))
 
     def summed_parts(own_part, other):
         totals = []

time: 473 us -> 407 us (0.86)
  Pallas kernels: 227 us -> 195 us
  starting transfers between devices: 80.5 us -> 53.1 us
  local copies, waits for them, and re-layouts: 31.8 us -> 25.1 us
    pallas_call x25 -> x24, Pallas kernels: 169 us -> 128 us  [the longest x10 95.3 us: turn(): pl.pallas_call(functools.partial(turn_kernel, parts, r, t, block), grid_s...]
    ppermute x28 -> x18, starting transfers between devices: 72.1 us -> 45.6 us  [along(): return lax.ppermute(x, 'section', pairs)]
    pallas_call x4, Pallas kernels: 24.3 us -> 43.6 us  [back_call(): pl.pallas_call(back_kernel, grid=(model // out_block,), in_specs=[pl.Bloc...]
    pallas_call x1, Pallas kernels: 22 us -> 15.8 us  [all_of_it(): pl.pallas_call(probs_kernel, grid=(pairs, MICRO), in_specs=[pl.BlockSpec(...]
    unnamed x79 -> x91, local copies, waits for them, and re-layouts: 27.2 us -> 21 us
    ppermute x37 -> x29, waiting for transfers between devices: 8.44 us -> 3.41 us  [shifted(): return lax.ppermute(x, 'mp', [((i + by) % n, i) for i in range(n)])]
    ppermute x28 -> x18, waiting for transfers between devices: 99.2 us -> 104 us  [along(): return lax.ppermute(x, 'section', pairs)]
  transfers between devices with their start and end apart: 65 -> 47, of which waited for: 26 -> 19; matrix products, arithmetic and copies ran while one was open for 4% -> 5% of each run, Pallas kernels for 36% -> 39%
where the time goes in v2:
time: 407 us; the launch traced here: 401 us
  Pallas kernels  195 us (48%)
  waiting for transfers between devices  107 us (26%)
  starting transfers between devices  53.1 us (13%)
  local copies, waits for them, and re-layouts  25.1 us (6%)
  other arithmetic  14.8 us (4%)
  matrix products  4.15 us (1%)
    ppermute x18, waiting for transfers between devices, along(): return lax.ppermute(x, 'section', pairs)  104 us
    pallas_call x10, Pallas kernels, turn(): pl.pallas_call(functools.partial(turn_kernel, parts, r, t, block), grid_s...  95.3 us
    ppermute x18, starting transfers between devices, along(): return lax.ppermute(x, 'section', pairs)  45.6 us
    pallas_call x4, Pallas kernels, back_call(): pl.pallas_call(back_kernel, grid=(model // out_block,), in_specs=[pl.Bloc...  43.6 us
    unnamed x91, local copies, waits for them, and re-layouts  21 us
    pallas_call x4, Pallas kernels, all_of_it(): keys_values = project(*xs, wk, wv, *keys_values, *early)  19.9 us
    pallas_call x1, Pallas kernels, all_of_it(): pl.pallas_call(probs_kernel, grid=(pairs, MICRO), in_specs=[pl.BlockSpec(...  15.8 us
    pallas_call x10, Pallas kernels, norm_back(): pl.pallas_call(functools.partial(norm_kernel, k, t), grid_spec=pltpu.Pref...  13.1 us
  transfers between devices with their start and end apart: 47, of which 19 were waited for; matrix products, arithmetic and copies ran while one was open for 5% of the time, Pallas kernels for 39%

profile of v2, /device:TPU:0, one launch (start us, length us, event | category | flops | bytes accessed | tf_op | source)
XLA Modules:
  0.0 400.9 jit_solution(3014473446824807631)
XLA Ops:
  2.1 6.6 %collective-permute-start.4 = (bf16[128,4096]{1,0:T(8,128)(2,1)}, bf16[128,4096]{1,0:T(8,128)(2,1)}, u32[]{:S(2)}, u32[]{:S(2)}) collective-permute-start(bf16[128,4096]{1,0:T(8,128)(2,1)} %bitcast.74), channel_id=1, source_target_pairs={{0,2},{2,4},{4,6},{1,3},{3,5},{5,7},{8,10},{10,12},{12,14},{9,11},... | collective-permute-start | bytes 3145736 | tf_op jit(solution)/shard_map/ppermute | solution.py:208
  13.3 15.9 %collective-permute-done.2 = bf16[128,4096]{1,0:T(8,128)(2,1)} collective-permute-done((bf16[128,4096]{1,0:T(8,128)(2,1)}, bf16[128,4096]{1,0:T(8,128)(2,1)}, u32[]{:S(2)}, u32[]{:S(2)}) %collective-permute-start.2) | collective-permute-done | bytes 1048608 | tf_op jit(solution)/shard_map/ppermute | solution.py:208
  34.2 21.6 %collective-permute-done.3 = bf16[128,4096]{1,0:T(8,128)(2,1)} collective-permute-done((bf16[128,4096]{1,0:T(8,128)(2,1)}, bf16[128,4096]{1,0:T(8,128)(2,1)}, u32[]{:S(2)}, u32[]{:S(2)}) %collective-permute-start.3) | collective-permute-done | bytes 1048608 | tf_op jit(solution)/shard_map/ppermute | solution.py:208
  61.4 21.9 %collective-permute-done.6 = bf16[128,4096]{1,0:T(8,128)(2,1)S(1)} collective-permute-done((bf16[128,4096]{1,0:T(8,128)(2,1)S(1)}, bf16[128,4096]{1,0:T(8,128)(2,1)S(1)}, u32[]{:S(2)}, u32[]{:S(2)}) %collective-permute-start.6) | collective-permute-done | bytes 1048608 | tf_op jit(solution)/shard_map/ppermute | solution.py:208
  85.5 4.2 %convolution_convert_fusion.q_ref = bf16[256,1024]{1,0:T(8,128)(2,1)S(1)} fusion(bf16[256,4096]{1,0:T(8,128)(2,1)} %bitcast.83, bf16[1,4096,1024]{2,1,0:T(8,128)(2,1)S(1)} %copy-done.32), kind=kOutput, calls=%fused_computation.15 | convolution fusion | flops 2147745792 | bytes 11010048 | tf_op jit(solution)/shard_map/dot_general | solution.py:28
  94.0 5.1 %project.4 = (bf16[1024,1024]{1,0:T(8,128)(2,1)S(1)}, bf16[1024,1024]{1,0:T(8,128)(2,1)S(1)}) custom-call(bf16[128,4096]{1,0:T(8,128)(2,1)S(1)} %bitcast.76, bf16[128,4096]{1,0:T(8,128)(2,1)S(1)} %copy-done.25, bf16[4096,1024]{1,0:T(8,128)(2,1)S(1)} %bitcast.45, bf16[4096,1024]{1,0:T(8,128)(2,1)S(1)} %bitcast.55, s32[10,2]{1,0:T(8,128)S(1)} %copy.103.refs_4_.slots, ...), custom_call_target="tpu_custom_call" | custom-call | tf_op jit(solution)/shard_map/project/pallas_call | solution.py:294
  99.1 4.9 %project.5 = (bf16[1024,1024]{1,0:T(8,128)(2,1)S(1)}, bf16[1024,1024]{1,0:T(8,128)(2,1)S(1)}) custom-call(bf16[128,4096]{1,0:T(8,128)(2,1)S(1)} %get-tuple-element.178.refs_0_, bf16[128,4096]{1,0:T(8,128)(2,1)S(1)} %collective-permute-done.9.refs_1_, bf16[4096,1024]{1,0:T(8,128)(2,1)S(1)} %bitcast.46, ...), custom_call_target="tpu_custom_call", output_to_operand_aliasing={{0}: (4, {}), {1}: (5, {})} | custom-call | tf_op jit(solution)/shard_map/project/pallas_call | solution.py:294
  104.0 4.9 %project.6 = (bf16[1024,1024]{1,0:T(8,128)(2,1)S(1)}, bf16[1024,1024]{1,0:T(8,128)(2,1)S(1)}) custom-call(bf16[128,4096]{1,0:T(8,128)(2,1)S(1)} %broadcast_select_fusion.2.refs_0_, bf16[128,4096]{1,0:T(8,128)(2,1)S(1)} %collective-permute-done.8.refs_1_, bf16[4096,1024]{1,0:T(8,128)(2,1)S(1)} %bitcast.47, ...), custom_call_target="tpu_custom_call", output_to_operand_aliasing={{0}: (4, {}), {1}: (5, {})} | custom-call | tf_op jit(solution)/shard_map/project/pallas_call | solution.py:294
  109.0 4.9 %project.7 = (bf16[1024,1024]{1,0:T(8,128)(2,1)S(1)}, bf16[1024,1024]{1,0:T(8,128)(2,1)S(1)}) custom-call(bf16[128,4096]{1,0:T(8,128)(2,1)S(1)} %broadcast_select_fusion.3.refs_0_, bf16[128,4096]{1,0:T(8,128)(2,1)S(1)} %collective-permute-done.7.refs_1_, bf16[4096,1024]{1,0:T(8,128)(2,1)S(1)} %bitcast.48, ...), custom_call_target="tpu_custom_call", output_to_operand_aliasing={{0}: (4, {}), {1}: (5, {})} | custom-call | tf_op jit(solution)/shard_map/project/pallas_call | solution.py:294
  114.0 15.8 %probs.1 = (bf16[4,8,128,1024]{3,2,1,0:T(8,128)(2,1)S(1)}, bf16[1024,4096]{1,0:T(8,128)(2,1)S(1)}, bf16[4096,1024]{1,0:T(8,128)(2,1)S(1)}) custom-call(bf16[256,1024]{1,0:T(8,128)(2,1)S(1)} %convolution_convert_fusion.q_ref, bf16[1024,1024]{1,0:T(8,128)(2,1)S(1)} %get-tuple-element.101.k_ref.refs_4_, s32[4,128,1]{2,1,0:T(8,128)S(1)} %copy.82.refs_6_.tok_ref, ...), custom_call_target="tpu_custom_call" | custom-call | tf_op jit(solution)/shard_map/probs/pallas_call | solution.py:297
  129.8 10.4 %turn.10 = (bf16[32,4096]{1,0:T(8,128)(2,1)S(1)}, bf16[32,4096]{1,0:T(8,128)(2,1)S(1)}, bf16[5,8,128,1024]{3,2,1,0:T(8,128)(2,1)S(1)}, bf16[5,64,1024]{2,1,0:T(8,128)(2,1)S(1)}) custom-call(s32[10,2]{1,0:T(8,128)S(1)} %copy.103.refs_4_.slots, bf16[32,4096]{1,0:T(8,128)(2,1)S(1)} %get-tuple-element.180.refs_0_.refs_2_, ...), custom_call_target="tpu_custom_call" | custom-call | tf_op jit(solution)/shard_map/turn/pallas_call | solution.py:323
  148.7 3.4 copy-done.4
  157.0 10.8 %turn.11 = (bf16[32,4096]{1,0:T(8,128)(2,1)S(1)}, bf16[32,4096]{1,0:T(8,128)(2,1)S(1)}, bf16[5,8,128,1024]{3,2,1,0:T(8,128)(2,1)S(1)}, bf16[5,64,1024]{2,1,0:T(8,128)(2,1)S(1)}) custom-call(s32[10,2]{1,0:T(8,128)S(1)} %copy.103.refs_4_.slots, bf16[32,4096]{1,0:T(8,128)(2,1)} %get-tuple-element.183.refs_0_.refs_2_, ...), custom_call_target="tpu_custom_call", output_to_operand_aliasing={{2}: (8, {}), {3}: (9, {})} | custom-call | tf_op jit(solution)/shard_map/turn/pallas_call | solution.py:323
  173.5 9.2 %turn.12 = (bf16[32,4096]{1,0:T(8,128)(2,1)S(1)}, bf16[32,4096]{1,0:T(8,128)(2,1)S(1)}, bf16[5,8,128,1024]{3,2,1,0:T(8,128)(2,1)S(1)}, bf16[5,64,1024]{2,1,0:T(8,128)(2,1)S(1)}) custom-call(s32[10,2]{1,0:T(8,128)S(1)} %copy.103.refs_4_.slots, ...), custom_call_target="tpu_custom_call", output_to_operand_aliasing={{2}: (8, {}), {3}: (9, {})} | custom-call | tf_op jit(solution)/shard_map/turn/pallas_call | solution.py:323
  186.7 9.2 %turn.13 = (bf16[32,4096]{1,0:T(8,128)(2,1)S(1)}, bf16[32,4096]{1,0:T(8,128)(2,1)S(1)}, bf16[5,8,128,1024]{3,2,1,0:T(8,128)(2,1)S(1)}, bf16[5,64,1024]{2,1,0:T(8,128)(2,1)S(1)}) custom-call(s32[10,2]{1,0:T(8,128)S(1)} %copy.103.refs_4_.slots, ...), custom_call_target="tpu_custom_call", output_to_operand_aliasing={{2}: (8, {}), {3}: (9, {})} | custom-call | tf_op jit(solution)/shard_map/turn/pallas_call | solution.py:323
  199.9 9.6 %turn.14 = (bf16[32,4096]{1,0:T(8,128)(2,1)S(1)}, bf16[32,4096]{1,0:T(8,128)(2,1)S(1)}, bf16[5,8,128,1024]{3,2,1,0:T(8,128)(2,1)S(1)}, bf16[5,64,1024]{2,1,0:T(8,128)(2,1)S(1)}) custom-call(s32[10,2]{1,0:T(8,128)S(1)} %copy.103.refs_4_.slots, ...), custom_call_target="tpu_custom_call", output_to_operand_aliasing={{2}: (8, {}), {3}: (9, {})} | custom-call | tf_op jit(solution)/shard_map/turn/pallas_call | solution.py:323
  213.5 9.2 %turn.15 = (bf16[32,4096]{1,0:T(8,128)(2,1)S(1)}, bf16[32,4096]{1,0:T(8,128)(2,1)S(1)}, bf16[5,8,128,1024]{3,2,1,0:T(8,128)(2,1)S(1)}, bf16[5,64,1024]{2,1,0:T(8,128)(2,1)S(1)}) custom-call(s32[10,2]{1,0:T(8,128)S(1)} %copy.103.refs_4_.slots, ...), custom_call_target="tpu_custom_call", output_to_operand_aliasing={{2}: (8, {}), {3}: (9, {})} | custom-call | tf_op jit(solution)/shard_map/turn/pallas_call | solution.py:323
  227.7 9.2 %turn.16 = (bf16[32,4096]{1,0:T(8,128)(2,1)S(1)}, bf16[32,4096]{1,0:T(8,128)(2,1)S(1)}, bf16[5,8,128,1024]{3,2,1,0:T(8,128)(2,1)S(1)}, bf16[5,64,1024]{2,1,0:T(8,128)(2,1)S(1)}) custom-call(s32[10,2]{1,0:T(8,128)S(1)} %copy.103.refs_4_.slots, ...), custom_call_target="tpu_custom_call", output_to_operand_aliasing={{2}: (8, {}), {3}: (9, {})} | custom-call | tf_op jit(solution)/shard_map/turn/pallas_call | solution.py:323
  241.5 9.4 %turn.17 = (bf16[32,4096]{1,0:T(8,128)(2,1)S(1)}, bf16[32,4096]{1,0:T(8,128)(2,1)S(1)}, bf16[5,8,128,1024]{3,2,1,0:T(8,128)(2,1)S(1)}, bf16[5,64,1024]{2,1,0:T(8,128)(2,1)S(1)}) custom-call(s32[10,2]{1,0:T(8,128)S(1)} %copy.103.refs_4_.slots, ...), custom_call_target="tpu_custom_call", output_to_operand_aliasing={{2}: (8, {}), {3}: (9, {})} | custom-call | tf_op jit(solution)/shard_map/turn/pallas_call | solution.py:323
  255.4 9.2 %turn.18 = (bf16[32,4096]{1,0:T(8,128)(2,1)S(1)}, bf16[32,4096]{1,0:T(8,128)(2,1)S(1)}, bf16[5,8,128,1024]{3,2,1,0:T(8,128)(2,1)S(1)}, bf16[5,64,1024]{2,1,0:T(8,128)(2,1)S(1)}) custom-call(s32[10,2]{1,0:T(8,128)S(1)} %copy.103.refs_4_.slots, ...), custom_call_target="tpu_custom_call", output_to_operand_aliasing={{2}: (8, {}), {3}: (9, {})} | custom-call | tf_op jit(solution)/shard_map/turn/pallas_call | solution.py:323
  268.8 9.2 %turn.19 = (bf16[32,4096]{1,0:T(8,128)(2,1)S(1)}, bf16[32,4096]{1,0:T(8,128)(2,1)S(1)}, bf16[5,8,128,1024]{3,2,1,0:T(8,128)(2,1)S(1)}, bf16[5,64,1024]{2,1,0:T(8,128)(2,1)S(1)}) custom-call(s32[10,2]{1,0:T(8,128)S(1)} %copy.103.refs_4_.slots, ...), custom_call_target="tpu_custom_call", output_to_operand_aliasing={{2}: (8, {}), {3}: (9, {})} | custom-call | tf_op jit(solution)/shard_map/turn/pallas_call | solution.py:323
  278.0 7.0 %grads.1 = (bf16[1024,1024]{1,0:T(8,128)(2,1)S(1)}, bf16[1024,1024]{1,0:T(8,128)(2,1)S(1)}) custom-call(bf16[5,8,128,1024]{3,2,1,0:T(8,128)(2,1)S(1)} %get-tuple-element.164.ds_ref, bf16[4,8,128,1024]{3,2,1,0:T(8,128)(2,1)S(1)} %copy-done.2, bf16[256,1024]{1,0:T(8,128)(2,1)} %copy-done.20, bf16[5,64,1024]{2,1,0:T(8,128)(2,1)S(1)} %get-tuple-element.165.ag_ref), custom_call_target="tpu_custom_call" | custom-call | tf_op jit(solution)/shard_map/grads/pallas_call | solution.py:378
  285.0 11.2 %back.5 = (bf16[128,4096]{1,0:T(8,128)(2,1)S(1)}, bf16[128,4096]{1,0:T(8,128)(2,1)S(1)}) custom-call(bf16[1024,1024]{1,0:T(8,128)(2,1)S(1)} %get-tuple-element.166.kg_ref, bf16[1024,1024]{1,0:T(8,128)(2,1)S(1)} %get-tuple-element.167.vg_ref, bf16[4096,1024]{1,0:T(8,128)(2,1)} %bitcast.39, bf16[4096,1024]{1,0:T(8,128)(2,1)} %bitcast.49), custom_call_target="tpu_custom_call" | custom-call | tf_op jit(solution)/shard_map/back/pallas_call | solution.py:400
  296.8 10.4 %back.7 = (bf16[128,4096]{1,0:T(8,128)(2,1)S(1)}, bf16[128,4096]{1,0:T(8,128)(2,1)S(1)}) custom-call(bf16[1024,1024]{1,0:T(8,128)(2,1)S(1)} %get-tuple-element.166.kg_ref, bf16[1024,1024]{1,0:T(8,128)(2,1)S(1)} %get-tuple-element.167.vg_ref, bf16[4096,1024]{1,0:T(8,128)(2,1)} %bitcast.40, bf16[4096,1024]{1,0:T(8,128)(2,1)} %bitcast.50), custom_call_target="tpu_custom_call" | custom-call | tf_op jit(solution)/shard_map/back/pallas_call | solution.py:400
  307.9 5.9 %collective-permute-start.42 = (bf16[128,4096]{1,0:T(8,128)(2,1)S(1)}, bf16[128,4096]{1,0:T(8,128)(2,1)S(1)}, u32[]{:S(2)}, u32[]{:S(2)}) collective-permute-start(bf16[128,4096]{1,0:T(8,128)(2,1)S(1)} %fusion.3), channel_id=1, source_target_pairs={{0,2},{6,4},{1,3},{7,5},{8,10},{14,12},{9,11},{15,13},{16,18},{22,... | collective-permute-start | bytes 3145736 | tf_op jit(solution)/shard_map/ppermute | solution.py:208
  313.8 11.2 %back.6 = (bf16[128,4096]{1,0:T(8,128)(2,1)S(1)}, bf16[128,4096]{1,0:T(8,128)(2,1)}) custom-call(bf16[1024,1024]{1,0:T(8,128)(2,1)S(1)} %get-tuple-element.166.kg_ref, bf16[1024,1024]{1,0:T(8,128)(2,1)S(1)} %get-tuple-element.167.vg_ref, bf16[4096,1024]{1,0:T(8,128)(2,1)} %bitcast.41, bf16[4096,1024]{1,0:T(8,128)(2,1)} %bitcast.51), custom_call_target="tpu_custom_call" | custom-call | tf_op jit(solution)/shard_map/back/pallas_call | solution.py:400
  326.0 10.6 %collective-permute-done.42 = bf16[128,4096]{1,0:T(8,128)(2,1)S(1)} collective-permute-done((bf16[128,4096]{1,0:T(8,128)(2,1)S(1)}, bf16[128,4096]{1,0:T(8,128)(2,1)S(1)}, u32[]{:S(2)}, u32[]{:S(2)}) %collective-permute-start.42) | collective-permute-done | bytes 1048608 | tf_op jit(solution)/shard_map/ppermute | solution.py:208
  338.0 5.4 %collective-permute-start.43 = (bf16[128,4096]{1,0:T(8,128)(2,1)}, bf16[128,4096]{1,0:T(8,128)(2,1)}, u32[]{:S(2)}, u32[]{:S(2)}) collective-permute-start(bf16[128,4096]{1,0:T(8,128)(2,1)} %add_convert_fusion.2), channel_id=1, source_target_pairs={{0,2},{2,4},{1,3},{3,5},{8,10},{10,12},{9,11},{11,13},{16,18},{18,... | collective-permute-start | bytes 3145736 | tf_op jit(solution)/shard_map/ppermute | solution.py:208
  346.6 10.8 %back.4 = (bf16[128,4096]{1,0:T(8,128)(2,1)S(1)}, bf16[128,4096]{1,0:T(8,128)(2,1)S(1)}) custom-call(bf16[1024,1024]{1,0:T(8,128)(2,1)S(1)} %get-tuple-element.166.kg_ref, bf16[1024,1024]{1,0:T(8,128)(2,1)S(1)} %copy-done.15, bf16[4096,1024]{1,0:T(8,128)(2,1)} %bitcast.42, bf16[4096,1024]{1,0:T(8,128)(2,1)} %bitcast.52), custom_call_target="tpu_custom_call" | custom-call | tf_op jit(solution)/shard_map/back/pallas_call | solution.py:400
  358.0 6.7 %collective-permute-done.43 = bf16[128,4096]{1,0:T(8,128)(2,1)} collective-permute-done((bf16[128,4096]{1,0:T(8,128)(2,1)}, bf16[128,4096]{1,0:T(8,128)(2,1)}, u32[]{:S(2)}, u32[]{:S(2)}) %collective-permute-start.43) | collective-permute-done | bytes 1048608 | tf_op jit(solution)/shard_map/ppermute | solution.py:208
  369.2 8.7 %collective-permute-start.44 = (bf16[128,4096]{1,0:T(8,128)(2,1)S(1)}, bf16[128,4096]{1,0:T(8,128)(2,1)S(1)}, u32[]{:S(2)}, u32[]{:S(2)}) collective-permute-start(bf16[128,4096]{1,0:T(8,128)(2,1)S(1)} %get-tuple-element.176), channel_id=1, source_target_pairs={{0,2},{2,4},{4,6},{1,3},{3,5},{5,7},{8,10},{10,12},{12,14},{9,11},... | collective-permute-start | bytes 3145736 | tf_op jit(solution)/shard_map/ppermute | solution.py:208
  380.8 16.8 %collective-permute-done.46 = bf16[128,4096]{1,0:T(8,128)(2,1)S(1)} collective-permute-done((bf16[128,4096]{1,0:T(8,128)(2,1)S(1)}, bf16[128,4096]{1,0:T(8,128)(2,1)S(1)}, u32[]{:S(2)}, u32[]{:S(2)}) %collective-permute-start.46) | collective-permute-done | bytes 1048608 | tf_op jit(solution)/shard_map/ppermute | solution.py:208
  (220 shorter events, 90.0 us)
Async XLA Ops:
  0.7 28.6 %collective-permute-start.2 = (bf16[128,4096]{1,0:T(8,128)(2,1)}, bf16[128,4096]{1,0:T(8,128)(2,1)}, u32[]{:S(2)}, u32[]{:S(2)}) collective-permute-start(bf16[128,4096]{1,0:T(8,128)(2,1)} %bitcast.73), channel_id=1, source_target_pairs={{6,4},{4,2},{2,0},{7,5},{5,3},{3,1},{14,12},{12,10},{10,8},{15,13}... | collective-permute-start | bytes 3145736 | tf_op jit(solution)/shard_map/ppermute | solution.py:208
  2.1 28.4 %collective-permute-start.4 = (bf16[128,4096]{1,0:T(8,128)(2,1)}, bf16[128,4096]{1,0:T(8,128)(2,1)}, u32[]{:S(2)}, u32[]{:S(2)}) collective-permute-start(bf16[128,4096]{1,0:T(8,128)(2,1)} %bitcast.74), channel_id=1, source_target_pairs={{0,2},{2,4},{4,6},{1,3},{3,5},{5,7},{8,10},{10,12},{12,14},{9,11},... | collective-permute-start | bytes 3145736 | tf_op jit(solution)/shard_map/ppermute | solution.py:208
  8.7 81.0 %collective-permute-start.10 = (bf16[128,4096]{1,0:T(8,128)(2,1)}, bf16[128,4096]{1,0:T(8,128)(2,1)S(1)}, u32[]{:S(2)}, u32[]{:S(2)}) collective-permute-start(bf16[128,4096]{1,0:T(8,128)(2,1)} %bitcast.75), channel_id=1, source_target_pairs={{1,0},{0,1},{3,2},{2,3},{5,4},{4,5},{7,6},{6,7},{9,8},{8,9},{11,10... | collective-permute-start | bytes 3145736 | tf_op jit(solution)/shard_map/ppermute | solution.py:205
  8.7 51.6 %collective-permute-start.1 = (bf16[128,4096]{1,0:T(8,128)(2,1)}, bf16[128,4096]{1,0:T(8,128)(2,1)S(1)}, u32[]{:S(2)}, u32[]{:S(2)}) collective-permute-start(bf16[128,4096]{1,0:T(8,128)(2,1)} %bitcast.59), channel_id=1, source_target_pairs={{1,0},{0,1},{3,2},{2,3},{5,4},{4,5},{7,6},{6,7},{9,8},{8,9},{11,10... | collective-permute-start | bytes 3145736 | tf_op jit(solution)/shard_map/ppermute | solution.py:205
  11.3 118.5 %collective-permute-start.11 = (bf16[32,4096]{1,0:T(8,128)(2,1)S(1)}, bf16[32,4096]{1,0:T(8,128)(2,1)}, u32[]{:S(2)}, u32[]{:S(2)}) collective-permute-start(bf16[32,4096]{1,0:T(8,128)(2,1)S(1)} %get-tuple-element.180.refs_0_.refs_2_), channel_id=1, source_target_pairs={{1,0},{0,1},{3,2},{2,3},{5,4},{4,5},{7,6},{6,7},{9,8},{8,9},{11,10... | collective-permute-start | bytes 786440 | tf_op jit(solution)/shard_map/ppermute | solution.py:205
  29.2 26.5 %collective-permute-start.3 = (bf16[128,4096]{1,0:T(8,128)(2,1)}, bf16[128,4096]{1,0:T(8,128)(2,1)}, u32[]{:S(2)}, u32[]{:S(2)}) collective-permute-start(bf16[128,4096]{1,0:T(8,128)(2,1)} %collective-permute-done.2), channel_id=1, source_target_pairs={{4,2},{2,0},{5,3},{3,1},{12,10},{10,8},{13,11},{11,9},{20,18},{18,... | collective-permute-start | bytes 3145736 | tf_op jit(solution)/shard_map/ppermute | solution.py:208
  30.5 25.2 %collective-permute-start.5 = (bf16[128,4096]{1,0:T(8,128)(2,1)}, bf16[128,4096]{1,0:T(8,128)(2,1)}, u32[]{:S(2)}, u32[]{:S(2)}) collective-permute-start(bf16[128,4096]{1,0:T(8,128)(2,1)} %collective-permute-done.4), channel_id=1, source_target_pairs={{2,4},{4,6},{3,5},{5,7},{10,12},{12,14},{11,13},{13,15},{18,20},{2... | collective-permute-start | bytes 3145736 | tf_op jit(solution)/shard_map/ppermute | solution.py:208
  57.1 26.2 %collective-permute-start.6 = (bf16[128,4096]{1,0:T(8,128)(2,1)S(1)}, bf16[128,4096]{1,0:T(8,128)(2,1)S(1)}, u32[]{:S(2)}, u32[]{:S(2)}) collective-permute-start(bf16[128,4096]{1,0:T(8,128)(2,1)S(1)} %broadcast_select_fusion.2.refs_0_), channel_id=1, source_target_pairs={{4,6},{2,0},{5,7},{3,1},{12,14},{10,8},{13,15},{11,9},{20,22},{18,... | collective-permute-start | bytes 3145736 | tf_op jit(solution)/shard_map/ppermute | solution.py:208
  60.2 38.8 %collective-permute-start.9 = (bf16[128,4096]{1,0:T(8,128)(2,1)S(1)}, bf16[128,4096]{1,0:T(8,128)(2,1)S(1)}, u32[]{:S(2)}, u32[]{:S(2)}) collective-permute-start(bf16[128,4096]{1,0:T(8,128)(2,1)S(1)} %get-tuple-element.178.refs_0_), channel_id=1, source_target_pairs={{1,0},{0,1},{3,2},{2,3},{5,4},{4,5},{7,6},{6,7},{9,8},{8,9},{11,10... | collective-permute-start | bytes 3145736 | tf_op jit(solution)/shard_map/ppermute | solution.py:205
  60.9 43.2 %collective-permute-start.8 = (bf16[128,4096]{1,0:T(8,128)(2,1)S(1)}, bf16[128,4096]{1,0:T(8,128)(2,1)S(1)}, u32[]{:S(2)}, u32[]{:S(2)}) collective-permute-start(bf16[128,4096]{1,0:T(8,128)(2,1)S(1)} %broadcast_select_fusion.2.refs_0_), channel_id=1, source_target_pairs={{1,0},{0,1},{3,2},{2,3},{5,4},{4,5},{7,6},{6,7},{9,8},{8,9},{11,10... | collective-permute-start | bytes 3145736 | tf_op jit(solution)/shard_map/ppermute | solution.py:205
  83.4 25.6 %collective-permute-start.7 = (bf16[128,4096]{1,0:T(8,128)(2,1)S(1)}, bf16[128,4096]{1,0:T(8,128)(2,1)S(1)}, u32[]{:S(2)}, u32[]{:S(2)}) collective-permute-start(bf16[128,4096]{1,0:T(8,128)(2,1)S(1)} %broadcast_select_fusion.3.refs_0_), channel_id=1, source_target_pairs={{1,0},{0,1},{3,2},{2,3},{5,4},{4,5},{7,6},{6,7},{9,8},{8,9},{11,10... | collective-permute-start | bytes 3145736 | tf_op jit(solution)/shard_map/ppermute | solution.py:205
  140.8 4.5 %collective-permute-start = (bf16[32,4096]{1,0:T(8,128)(2,1)}, bf16[32,4096]{1,0:T(8,128)(2,1)S(1)}, u32[]{:S(2)}, u32[]{:S(2)}) collective-permute-start(bf16[32,4096]{1,0:T(8,128)(2,1)} %get-tuple-element.183.refs_0_.refs_2_), channel_id=1, source_target_pairs={{1,0},{0,1},{3,2},{2,3},{5,4},{4,5},{7,6},{6,7},{9,8},{8,9},{11,10... | collective-permute-start | bytes 786440 | tf_op jit(solution)/shard_map/ppermute | solution.py:205
  144.0 25.0 %collective-permute-start.13 = (bf16[32,4096]{1,0:T(8,128)(2,1)S(1)}, bf16[32,4096]{1,0:T(8,128)(2,1)S(1)}, u32[]{:S(2)}, u32[]{:S(2)}) collective-permute-start(bf16[32,4096]{1,0:T(8,128)(2,1)S(1)} %get-tuple-element.113), channel_id=1, source_target_pairs={{6,4},{4,2},{2,0},{7,5},{5,3},{3,1},{14,12},{12,10},{10,8},{15,13}... | collective-permute-start | bytes 786440 | tf_op jit(solution)/shard_map/ppermute | solution.py:208
  169.0 4.5 %collective-permute-start.14 = (bf16[32,4096]{1,0:T(8,128)(2,1)S(1)}, bf16[32,4096]{1,0:T(8,128)(2,1)S(1)}, u32[]{:S(2)}, u32[]{:S(2)}) collective-permute-start(bf16[32,4096]{1,0:T(8,128)(2,1)S(1)} %broadcast_select_fusion.5.refs_0_.refs_2_), channel_id=1, source_target_pairs={{1,0},{0,1},{3,2},{2,3},{5,4},{4,5},{7,6},{6,7},{9,8},{8,9},{11,10... | collective-permute-start | bytes 786440 | tf_op jit(solution)/shard_map/ppermute | solution.py:205
  172.2 11.2 %collective-permute-start.16 = (bf16[32,4096]{1,0:T(8,128)(2,1)S(1)}, bf16[32,4096]{1,0:T(8,128)(2,1)S(1)}, u32[]{:S(2)}, u32[]{:S(2)}) collective-permute-start(bf16[32,4096]{1,0:T(8,128)(2,1)S(1)} %get-tuple-element.120), channel_id=1, source_target_pairs={{6,4},{4,2},{2,0},{7,5},{5,3},{3,1},{14,12},{12,10},{10,8},{15,13}... | collective-permute-start | bytes 786440 | tf_op jit(solution)/shard_map/ppermute | solution.py:208
  183.4 3.4 collective-permute-start.17
  185.4 11.8 %collective-permute-start.22 = (bf16[32,4096]{1,0:T(8,128)(2,1)S(1)}, bf16[32,4096]{1,0:T(8,128)(2,1)S(1)}, u32[]{:S(2)}, u32[]{:S(2)}) collective-permute-start(bf16[32,4096]{1,0:T(8,128)(2,1)S(1)} %get-tuple-element.128), channel_id=1, source_target_pairs={{6,4},{4,2},{2,0},{7,5},{5,3},{3,1},{14,12},{12,10},{10,8},{15,13}... | collective-permute-start | bytes 786440 | tf_op jit(solution)/shard_map/ppermute | solution.py:208
  198.6 12.4 %collective-permute-start.20 = (bf16[32,4096]{1,0:T(8,128)(2,1)S(1)}, bf16[32,4096]{1,0:T(8,128)(2,1)S(1)}, u32[]{:S(2)}, u32[]{:S(2)}) collective-permute-start(bf16[32,4096]{1,0:T(8,128)(2,1)S(1)} %get-tuple-element.127), channel_id=1, source_target_pairs={{6,4},{4,2},{2,0},{7,5},{5,3},{3,1},{14,12},{12,10},{10,8},{15,13}... | collective-permute-start | bytes 786440 | tf_op jit(solution)/shard_map/ppermute | solution.py:208
  212.2 13.0 %collective-permute-start.28 = (bf16[32,4096]{1,0:T(8,128)(2,1)S(1)}, bf16[32,4096]{1,0:T(8,128)(2,1)S(1)}, u32[]{:S(2)}, u32[]{:S(2)}) collective-permute-start(bf16[32,4096]{1,0:T(8,128)(2,1)S(1)} %get-tuple-element.140), channel_id=1, source_target_pairs={{6,4},{4,2},{2,0},{7,5},{5,3},{3,1},{14,12},{12,10},{10,8},{15,13}... | collective-permute-start | bytes 786440 | tf_op jit(solution)/shard_map/ppermute | solution.py:208
  226.4 12.7 %collective-permute-start.26 = (bf16[32,4096]{1,0:T(8,128)(2,1)S(1)}, bf16[32,4096]{1,0:T(8,128)(2,1)S(1)}, u32[]{:S(2)}, u32[]{:S(2)}) collective-permute-start(bf16[32,4096]{1,0:T(8,128)(2,1)S(1)} %get-tuple-element.139), channel_id=1, source_target_pairs={{6,4},{4,2},{2,0},{7,5},{5,3},{3,1},{14,12},{12,10},{10,8},{15,13}... | collective-permute-start | bytes 786440 | tf_op jit(solution)/shard_map/ppermute | solution.py:208
  240.2 12.7 %collective-permute-start.34 = (bf16[32,4096]{1,0:T(8,128)(2,1)S(1)}, bf16[32,4096]{1,0:T(8,128)(2,1)S(1)}, u32[]{:S(2)}, u32[]{:S(2)}) collective-permute-start(bf16[32,4096]{1,0:T(8,128)(2,1)S(1)} %get-tuple-element.152), channel_id=1, source_target_pairs={{6,4},{4,2},{2,0},{7,5},{5,3},{3,1},{14,12},{12,10},{10,8},{15,13}... | collective-permute-start | bytes 786440 | tf_op jit(solution)/shard_map/ppermute | solution.py:208
  254.0 12.9 %collective-permute-start.32 = (bf16[32,4096]{1,0:T(8,128)(2,1)S(1)}, bf16[32,4096]{1,0:T(8,128)(2,1)S(1)}, u32[]{:S(2)}, u32[]{:S(2)}) collective-permute-start(bf16[32,4096]{1,0:T(8,128)(2,1)S(1)} %get-tuple-element.151), channel_id=1, source_target_pairs={{6,4},{4,2},{2,0},{7,5},{5,3},{3,1},{14,12},{12,10},{10,8},{15,13}... | collective-permute-start | bytes 786440 | tf_op jit(solution)/shard_map/ppermute | solution.py:208
  296.2 11.4 %collective-permute-start.39 = (bf16[128,4096]{1,0:T(8,128)(2,1)S(1)}, bf16[128,4096]{1,0:T(8,128)(2,1)S(1)}, u32[]{:S(2)}, u32[]{:S(2)}) collective-permute-start(bf16[128,4096]{1,0:T(8,128)(2,1)S(1)} %get-tuple-element.171), channel_id=1, source_target_pairs={{1,0},{0,1},{3,2},{2,3},{5,4},{4,5},{7,6},{6,7},{9,8},{8,9},{11,10... | collective-permute-start | bytes 3145736 | tf_op jit(solution)/shard_map/ppermute | solution.py:205
  307.2 18.8 %collective-permute-start.41 = (bf16[128,4096]{1,0:T(8,128)(2,1)S(1)}, bf16[128,4096]{1,0:T(8,128)(2,1)S(1)}, u32[]{:S(2)}, u32[]{:S(2)}) collective-permute-start(bf16[128,4096]{1,0:T(8,128)(2,1)S(1)} %get-tuple-element.175), channel_id=1, source_target_pairs={{1,0},{0,1},{3,2},{2,3},{5,4},{4,5},{7,6},{6,7},{9,8},{8,9},{11,10... | collective-permute-start | bytes 3145736 | tf_op jit(solution)/shard_map/ppermute | solution.py:205
  307.9 28.7 %collective-permute-start.42 = (bf16[128,4096]{1,0:T(8,128)(2,1)S(1)}, bf16[128,4096]{1,0:T(8,128)(2,1)S(1)}, u32[]{:S(2)}, u32[]{:S(2)}) collective-permute-start(bf16[128,4096]{1,0:T(8,128)(2,1)S(1)} %fusion.3), channel_id=1, source_target_pairs={{0,2},{6,4},{1,3},{7,5},{8,10},{14,12},{9,11},{15,13},{16,18},{22,... | collective-permute-start | bytes 3145736 | tf_op jit(solution)/shard_map/ppermute | solution.py:208
  326.0 32.0 %collective-permute-start.40 = (bf16[128,4096]{1,0:T(8,128)(2,1)}, bf16[128,4096]{1,0:T(8,128)(2,1)}, u32[]{:S(2)}, u32[]{:S(2)}) collective-permute-start(bf16[128,4096]{1,0:T(8,128)(2,1)} %get-tuple-element.173), channel_id=1, source_target_pairs={{1,0},{0,1},{3,2},{2,3},{5,4},{4,5},{7,6},{6,7},{9,8},{8,9},{11,10... | collective-permute-start | bytes 3145736 | tf_op jit(solution)/shard_map/ppermute | solution.py:205
  338.0 26.7 %collective-permute-start.43 = (bf16[128,4096]{1,0:T(8,128)(2,1)}, bf16[128,4096]{1,0:T(8,128)(2,1)}, u32[]{:S(2)}, u32[]{:S(2)}) collective-permute-start(bf16[128,4096]{1,0:T(8,128)(2,1)} %add_convert_fusion.2), channel_id=1, source_target_pairs={{0,2},{2,4},{1,3},{3,5},{8,10},{10,12},{9,11},{11,13},{16,18},{18,... | collective-permute-start | bytes 3145736 | tf_op jit(solution)/shard_map/ppermute | solution.py:208
  343.4 21.4 %collective-permute-start.45 = (bf16[128,4096]{1,0:T(8,128)(2,1)}, bf16[128,4096]{1,0:T(8,128)(2,1)}, u32[]{:S(2)}, u32[]{:S(2)}) collective-permute-start(bf16[128,4096]{1,0:T(8,128)(2,1)} %add_convert_fusion.2), channel_id=1, source_target_pairs={{6,4},{4,2},{7,5},{5,3},{14,12},{12,10},{15,13},{13,11},{22,20},{2... | collective-permute-start | bytes 3145736 | tf_op jit(solution)/shard_map/ppermute | solution.py:208
  357.4 20.5 %collective-permute-start.37 = (bf16[32,4096]{1,0:T(8,128)(2,1)S(1)}, bf16[32,4096]{1,0:T(8,128)(2,1)S(1)}, u32[]{:S(2)}, u32[]{:S(2)}) collective-permute-start(bf16[32,4096]{1,0:T(8,128)(2,1)S(1)} %copy-done.31), channel_id=1, source_target_pairs={{1,0},{0,1},{3,2},{2,3},{5,4},{4,5},{7,6},{6,7},{9,8},{8,9},{11,10... | collective-permute-start | bytes 786440 | tf_op jit(solution)/shard_map/ppermute | solution.py:205
  357.5 23.3 %collective-permute-start.38 = (bf16[128,4096]{1,0:T(8,128)(2,1)S(1)}, bf16[128,4096]{1,0:T(8,128)(2,1)S(1)}, u32[]{:S(2)}, u32[]{:S(2)}) collective-permute-start(bf16[128,4096]{1,0:T(8,128)(2,1)S(1)} %get-tuple-element.169), channel_id=1, source_target_pairs={{1,0},{0,1},{3,2},{2,3},{5,4},{4,5},{7,6},{6,7},{9,8},{8,9},{11,10... | collective-permute-start | bytes 3145736 | tf_op jit(solution)/shard_map/ppermute | solution.py:205
  367.9 29.7 %collective-permute-start.46 = (bf16[128,4096]{1,0:T(8,128)(2,1)S(1)}, bf16[128,4096]{1,0:T(8,128)(2,1)S(1)}, u32[]{:S(2)}, u32[]{:S(2)}) collective-permute-start(bf16[128,4096]{1,0:T(8,128)(2,1)S(1)} %get-tuple-element.177), channel_id=1, source_target_pairs={{6,4},{4,2},{2,0},{7,5},{5,3},{3,1},{14,12},{12,10},{10,8},{15,13}... | collective-permute-start | bytes 3145736 | tf_op jit(solution)/shard_map/ppermute | solution.py:208
  369.2 29.6 %collective-permute-start.44 = (bf16[128,4096]{1,0:T(8,128)(2,1)S(1)}, bf16[128,4096]{1,0:T(8,128)(2,1)S(1)}, u32[]{:S(2)}, u32[]{:S(2)}) collective-permute-start(bf16[128,4096]{1,0:T(8,128)(2,1)S(1)} %get-tuple-element.176), channel_id=1, source_target_pairs={{0,2},{2,4},{4,6},{1,3},{3,5},{5,7},{8,10},{10,12},{12,14},{9,11},... | collective-permute-start | bytes 3145736 | tf_op jit(solution)/shard_map/ppermute | solution.py:208
  (60 other events, 650.4 us)

commit v3 on v2

--- a/solution.py
+++ b/solution.py
@@ -11,7 +11,7 @@
 PAIR = 2 * HD
 MICRO = 4
 SKEW = 2
-PIECES = 1
+PIECES = 2
 BLOCK = 512
 OUT_BLOCK = 512
 SLOTS = ((0, 1, 2, 3), (1, 2, 1, 2), (2, 3, 0, 1), (3, 0, 3, 0))
@@ -81,11 +81,11 @@
     v_ref[rows, cols] = dot(x_all[...], wv_ref[:, cols], NN).astype(bf16)
 
 
-def back_kernel(kg_ref, vg_ref, wk_ref, wv_ref, own_ref, other_ref):
+def back_kernel(kg_ref, vg_ref, wk_ref, wv_ref, *out_refs):
     out = dot(kg_ref[...], wk_ref[...], NT) + dot(vg_ref[...], wv_ref[...], NT)
-    rows = own_ref.shape[0]
-    own_ref[...] = out[:rows].astype(bf16)
-    other_ref[...] = out[rows:].astype(bf16)
+    rows = out_refs[0].shape[0]
+    for i, ref in enumerate(out_refs):
+        ref[...] = out[i * rows : (i + 1) * rows].astype(bf16)
 
 
 def turn_kernel(parts, own_rows, t, block, slots, *refs):
@@ -198,8 +198,8 @@
     m = r * n
     tokens = own * n
     params = pltpu.CompilerParams(vmem_limit_bytes=24 * 1024 * 1024)
-    small = pltpu.CompilerParams(vmem_limit_bytes=12 * 1024 * 1024)
-    least = pltpu.CompilerParams(vmem_limit_bytes=8 * 1024 * 1024)
+    small = pltpu.CompilerParams(vmem_limit_bytes=10 * 1024 * 1024)
+    least = pltpu.CompilerParams(vmem_limit_bytes=5 * 1024 * 1024)
 
     def shifted(x, by):
         return lax.ppermute(x, "mp", [((i + by) % n, i) for i in range(n)])
@@ -393,8 +393,21 @@
     out_block = min(OUT_BLOCK, model)
 
     def back(slot):
-        own_part, other = back_call(slot)
-        return summed_parts(own_part, other)
+        outs = back_call(slot)
+        swapped = []
+        for i in range(PIECES):
+            swapped.append([shifted(outs[k * PIECES + i], -k) for k in range(1, n)])
+        return list(zip(outs[:PIECES], swapped))
+
+    def total(parts):
+        out, got = parts
+        out = out.astype(f32)
+        for g in got:
+            out = out + g.astype(f32)
+        return out
+
+    def behind(x, y):
+        return lax.optimization_barrier((x, y))[0]
 
     def back_call(slot):
         return pl.pallas_call(
@@ -402,47 +415,38 @@
             grid=(model // out_block,),
             in_specs=[pl.BlockSpec((rows, width), lambda i: (slot, 0))] * 2
             + [pl.BlockSpec((out_block, width), lambda i: (i, 0))] * 2,
-            out_specs=[
-                pl.BlockSpec((share, out_block), lambda i: (0, i)),
-                pl.BlockSpec((rows - share, out_block), lambda i: (0, i)),
-            ],
-            out_shape=[
-                jax.ShapeDtypeStruct((share, model), bf16),
-                jax.ShapeDtypeStruct((rows - share, model), bf16),
-            ],
+            out_specs=[pl.BlockSpec((size, out_block), lambda i: (0, i))] * (n * PIECES),
+            out_shape=[jax.ShapeDtypeStruct((size, model), bf16)] * (n * PIECES),
             compiler_params=small,
             name="back",
         )(kg, vg, in_hbm(w_key[0]), in_hbm(w_value[0]))
 
-    def summed_parts(own_part, other):
-        totals = []
-        for i in range(PIECES):
-            total = own_part[i * size : (i + 1) * size].astype(f32)
-            for k in range(1, n):
-                first = (k - 1) * share + i * size
-                got = shifted(other[first : first + size], -k)
-                total = total + got.astype(f32)
-            totals.append(total)
-        return totals
-
     far, mid = back(3), back(2)
     got = []
-    for v in far:
-        got.append(along(v.astype(bf16), (0, 1), (3, 2)))
+    for i in range(PIECES):
+        v = far[i] if i == 0 else behind(far[i], v)
+        v = total(v).astype(bf16)
+        got.append(along(v, (0, 1), (3, 2)))
     near = back(1)
     up2, down2 = [], []
-    for v, g in zip(mid, got):
-        v = (v + g.astype(f32)).astype(bf16)
+    for i in range(PIECES):
+        held, came = (mid[i], got[i]) if i == 0 else behind((mid[i], got[i]), v)
+        v = (total(held) + came.astype(f32)).astype(bf16)
         up2.append(along(v, (0, 1), (1, 2)))
         down2.append(along(v, (3, 2), (2, 1)))
     here = back(0)
-    enc_share = []
+    up3, down3 = [], []
     for i in range(PIECES):
-        up3 = jnp.where(section == 2, far[i], near[i]) + up2[i].astype(f32)
-        down3 = jnp.where(section == 1, far[i], near[i]) + down2[i].astype(f32)
-        up3 = along(up3.astype(bf16), (0, 1), (1, 2), (2, 3))
-        down3 = along(down3.astype(bf16), (3, 2), (2, 1), (1, 0))
-        enc_share.append(here[i] + up3.astype(f32) + down3.astype(f32))
+        ends = (far[i], near[i], up2[i], down2[i])
+        a, b, u, d = ends if i == 0 else behind(ends, v)
+        a, b = total(a), total(b)
+        v = (jnp.where(section == 2, a, b) + u.astype(f32)).astype(bf16)
+        w = (jnp.where(section == 1, a, b) + d.astype(f32)).astype(bf16)
+        up3.append(along(v, (0, 1), (1, 2), (2, 3)))
+        down3.append(along(w, (3, 2), (2, 1), (1, 0)))
+    enc_share = [
+        total(h) + u.astype(f32) + d.astype(f32) for h, u, d in zip(here, up3, down3)
+    ]
     enc_share = jnp.concatenate(enc_share, axis=0)
     return dec_held[0][:own][None, None], enc_share[None]
 

time: 407 us -> 435 us (1.069)
  starting transfers between devices: 53.1 us -> 81.7 us
    ppermute x18 -> x28, starting transfers between devices: 45.6 us -> 72.3 us  [along(): return lax.ppermute(x, 'section', pairs)]
    ppermute x18 -> x28, waiting for transfers between devices: 104 us -> 108 us  [along(): return lax.ppermute(x, 'section', pairs)]
    unnamed x91 -> x83, local copies, waits for them, and re-layouts: 21 us -> 18.9 us
    ppermute x29 -> x37, starting transfers between devices: 7.52 us -> 9.42 us  [shifted(): return lax.ppermute(x, 'mp', [((i + by) % n, i) for i in range(n)])]
  transfers between devices with their start and end apart: 47 -> 65, of which waited for: 19 -> 23; matrix products, arithmetic and copies ran while one was open for 5% -> 4% of each run, Pallas kernels for 39% -> 36%
where the time goes in v3:
time: 435 us; the launch traced here: 429 us
  Pallas kernels  195 us (45%)
  waiting for transfers between devices  110 us (25%)
  starting transfers between devices  81.7 us (19%)
  local copies, waits for them, and re-layouts  24.5 us (6%)
  other arithmetic  13.4 us (3%)
    ppermute x28, waiting for transfers between devices, along(): return lax.ppermute(x, 'section', pairs)  108 us
    pallas_call x10, Pallas kernels, turn(): pl.pallas_call(functools.partial(turn_kernel, parts, r, t, block), grid_s...  94 us
    ppermute x28, starting transfers between devices, along(): return lax.ppermute(x, 'section', pairs)  72.3 us
    pallas_call x4, Pallas kernels, back_call(): pl.pallas_call(back_kernel, grid=(model // out_block,), in_specs=[pl.Bloc...  44.2 us
    pallas_call x4, Pallas kernels, all_of_it(): keys_values = project(*xs, wk, wv, *keys_values, *early)  19.5 us
    unnamed x83, local copies, waits for them, and re-layouts  18.9 us
    pallas_call x1, Pallas kernels, all_of_it(): pl.pallas_call(probs_kernel, grid=(pairs, MICRO), in_specs=[pl.BlockSpec(...  15.9 us
    pallas_call x10, Pallas kernels, norm_back(): pl.pallas_call(functools.partial(norm_kernel, k, t), grid_spec=pltpu.Pref...  14.1 us
  transfers between devices with their start and end apart: 65, of which 23 were waited for; matrix products, arithmetic and copies ran while one was open for 4% of the time, Pallas kernels for 36%

profile of v3, /device:TPU:0, one launch (start us, length us, event | category | flops | bytes accessed | tf_op | source)
XLA Modules:
  0.0 428.7 jit_solution(889145045254570467)
XLA Ops:
  3.3 6.4 %collective-permute-start.4 = (bf16[64,4096]{1,0:T(8,128)(2,1)S(1)}, bf16[64,4096]{1,0:T(8,128)(2,1)}, u32[]{:S(2)}, u32[]{:S(2)}) collective-permute-start(bf16[64,4096]{1,0:T(8,128)(2,1)S(1)} %get-tuple-element.231.refs_0_), channel_id=1, source_target_pairs={{0,2},{2,4},{4,6},{1,3},{3,5},{5,7},{8,10},{10,12},{12,14},{9,11},... | collective-permute-start | bytes 1572872 | tf_op jit(solution)/shard_map/ppermute | solution.py:208
  23.8 6.5 %collective-permute-done.8 = bf16[64,4096]{1,0:T(8,128)(2,1)} collective-permute-done((bf16[64,4096]{1,0:T(8,128)(2,1)S(1)}, bf16[64,4096]{1,0:T(8,128)(2,1)}, u32[]{:S(2)}, u32[]{:S(2)}) %collective-permute-start.8) | collective-permute-done | bytes 524320 | tf_op jit(solution)/shard_map/ppermute | solution.py:208
  41.3 4.9 %project.4 = (bf16[1024,1024]{1,0:T(8,128)(2,1)S(1)}, bf16[1024,1024]{1,0:T(8,128)(2,1)S(1)}) custom-call(bf16[64,4096]{1,0:T(8,128)(2,1)S(1)} %get-tuple-element.231.refs_0_, bf16[64,4096]{1,0:T(8,128)(2,1)S(1)} %get-tuple-element.230.refs_1_, bf16[64,4096]{1,0:T(8,128)(2,1)S(1)} %collective-permute-done.18.refs_2_, ...), custom_call_target="tpu_custom_call" | custom-call | tf_op jit(solution)/shard_map/project/pallas_call | solution.py:294
  52.2 17.5 %collective-permute-done.9 = bf16[64,4096]{1,0:T(8,128)(2,1)S(1)} collective-permute-done((bf16[64,4096]{1,0:T(8,128)(2,1)}, bf16[64,4096]{1,0:T(8,128)(2,1)S(1)}, u32[]{:S(2)}, u32[]{:S(2)}) %collective-permute-start.9) | collective-permute-done | bytes 524320 | tf_op jit(solution)/shard_map/ppermute | solution.py:208
  71.2 13.2 %collective-permute-done.6 = bf16[64,4096]{1,0:T(8,128)(2,1)S(1)} collective-permute-done((bf16[64,4096]{1,0:T(8,128)(2,1)S(1)}, bf16[64,4096]{1,0:T(8,128)(2,1)S(1)}, u32[]{:S(2)}, u32[]{:S(2)}) %collective-permute-start.6) | collective-permute-done | bytes 524320 | tf_op jit(solution)/shard_map/ppermute | solution.py:208
  86.0 12.3 %collective-permute-done.11 = bf16[64,4096]{1,0:T(8,128)(2,1)S(1)} collective-permute-done((bf16[64,4096]{1,0:T(8,128)(2,1)S(1)}, bf16[64,4096]{1,0:T(8,128)(2,1)S(1)}, u32[]{:S(2)}, u32[]{:S(2)}) %collective-permute-start.11) | collective-permute-done | bytes 524320 | tf_op jit(solution)/shard_map/ppermute | solution.py:208
  105.0 4.9 %project.5 = (bf16[1024,1024]{1,0:T(8,128)(2,1)S(1)}, bf16[1024,1024]{1,0:T(8,128)(2,1)S(1)}) custom-call(bf16[64,4096]{1,0:T(8,128)(2,1)S(1)} %get-tuple-element.228.refs_0_, bf16[64,4096]{1,0:T(8,128)(2,1)S(1)} %get-tuple-element.226.refs_1_, bf16[64,4096]{1,0:T(8,128)(2,1)S(1)} %collective-permute-done.16.refs_2_, ...), custom_call_target="tpu_custom_call", output_to_operand_aliasing={{0}: (6, {}), {1}: (7, {})} | custom-call | tf_op jit(solution)/shard_map/project/pallas_call | solution.py:294
  109.9 4.9 %project.6 = (bf16[1024,1024]{1,0:T(8,128)(2,1)S(1)}, bf16[1024,1024]{1,0:T(8,128)(2,1)S(1)}) custom-call(bf16[64,4096]{1,0:T(8,128)(2,1)S(1)} %broadcast_select_fusion.5.refs_0_, bf16[64,4096]{1,0:T(8,128)(2,1)S(1)} %broadcast_select_fusion.2.refs_1_, ...), custom_call_target="tpu_custom_call", output_to_operand_aliasing={{0}: (6, {}), {1}: (7, {})} | custom-call | tf_op jit(solution)/shard_map/project/pallas_call | solution.py:294
  114.8 4.9 %project.7 = (bf16[1024,1024]{1,0:T(8,128)(2,1)S(1)}, bf16[1024,1024]{1,0:T(8,128)(2,1)S(1)}) custom-call(bf16[64,4096]{1,0:T(8,128)(2,1)S(1)} %broadcast_select_fusion.7.refs_0_, bf16[64,4096]{1,0:T(8,128)(2,1)S(1)} %broadcast_select_fusion.6.refs_1_, ...), custom_call_target="tpu_custom_call", output_to_operand_aliasing={{0}: (6, {}), {1}: (7, {})} | custom-call | tf_op jit(solution)/shard_map/project/pallas_call | solution.py:294
  119.8 15.9 %probs.1 = (bf16[4,8,128,1024]{3,2,1,0:T(8,128)(2,1)S(1)}, bf16[1024,4096]{1,0:T(8,128)(2,1)S(1)}, bf16[4096,1024]{1,0:T(8,128)(2,1)S(1)}) custom-call(bf16[256,1024]{1,0:T(8,128)(2,1)S(1)} %convolution_convert_fusion.q_ref, bf16[1024,1024]{1,0:T(8,128)(2,1)S(1)} %get-tuple-element.124.k_ref.refs_4_, s32[4,128,1]{2,1,0:T(8,128)S(1)} %copy-done.18, ...), custom_call_target="tpu_custom_call" | custom-call | tf_op jit(solution)/shard_map/probs/pallas_call | solution.py:297
  138.9 10.5 %turn.10 = (bf16[32,4096]{1,0:T(8,128)(2,1)S(1)}, bf16[32,4096]{1,0:T(8,128)(2,1)S(1)}, bf16[5,8,128,1024]{3,2,1,0:T(8,128)(2,1)S(1)}, bf16[5,64,1024]{2,1,0:T(8,128)(2,1)S(1)}) custom-call(s32[10,2]{1,0:T(8,128)S(1)} %copy.103.refs_6_.slots, bf16[32,4096]{1,0:T(8,128)(2,1)} %get-tuple-element.222.refs_0_.refs_2_, ...), custom_call_target="tpu_custom_call" | custom-call | tf_op jit(solution)/shard_map/turn/pallas_call | solution.py:323
  154.8 9.2 %turn.11 = (bf16[32,4096]{1,0:T(8,128)(2,1)S(1)}, bf16[32,4096]{1,0:T(8,128)(2,1)S(1)}, bf16[5,8,128,1024]{3,2,1,0:T(8,128)(2,1)S(1)}, bf16[5,64,1024]{2,1,0:T(8,128)(2,1)S(1)}) custom-call(s32[10,2]{1,0:T(8,128)S(1)} %copy.103.refs_6_.slots, bf16[32,4096]{1,0:T(8,128)(2,1)S(1)} %copy-done.19, ...), custom_call_target="tpu_custom_call", output_to_operand_aliasing={{2}: (8, {}), {3}: (9, {})} | custom-call | tf_op jit(solution)/shard_map/turn/pallas_call | solution.py:323
  168.1 9.2 %turn.12 = (bf16[32,4096]{1,0:T(8,128)(2,1)S(1)}, bf16[32,4096]{1,0:T(8,128)(2,1)S(1)}, bf16[5,8,128,1024]{3,2,1,0:T(8,128)(2,1)S(1)}, bf16[5,64,1024]{2,1,0:T(8,128)(2,1)S(1)}) custom-call(s32[10,2]{1,0:T(8,128)S(1)} %copy.103.refs_6_.slots, ...), custom_call_target="tpu_custom_call", output_to_operand_aliasing={{2}: (8, {}), {3}: (9, {})} | custom-call | tf_op jit(solution)/shard_map/turn/pallas_call | solution.py:323
  182.1 9.2 %turn.13 = (bf16[32,4096]{1,0:T(8,128)(2,1)S(1)}, bf16[32,4096]{1,0:T(8,128)(2,1)S(1)}, bf16[5,8,128,1024]{3,2,1,0:T(8,128)(2,1)S(1)}, bf16[5,64,1024]{2,1,0:T(8,128)(2,1)S(1)}) custom-call(s32[10,2]{1,0:T(8,128)S(1)} %copy.103.refs_6_.slots, ...), custom_call_target="tpu_custom_call", output_to_operand_aliasing={{2}: (8, {}), {3}: (9, {})} | custom-call | tf_op jit(solution)/shard_map/turn/pallas_call | solution.py:323
  196.4 9.2 %turn.14 = (bf16[32,4096]{1,0:T(8,128)(2,1)S(1)}, bf16[32,4096]{1,0:T(8,128)(2,1)S(1)}, bf16[5,8,128,1024]{3,2,1,0:T(8,128)(2,1)S(1)}, bf16[5,64,1024]{2,1,0:T(8,128)(2,1)S(1)}) custom-call(s32[10,2]{1,0:T(8,128)S(1)} %copy.103.refs_6_.slots, ...), custom_call_target="tpu_custom_call", output_to_operand_aliasing={{2}: (8, {}), {3}: (9, {})} | custom-call | tf_op jit(solution)/shard_map/turn/pallas_call | solution.py:323
  210.1 9.2 %turn.15 = (bf16[32,4096]{1,0:T(8,128)(2,1)S(1)}, bf16[32,4096]{1,0:T(8,128)(2,1)S(1)}, bf16[5,8,128,1024]{3,2,1,0:T(8,128)(2,1)S(1)}, bf16[5,64,1024]{2,1,0:T(8,128)(2,1)S(1)}) custom-call(s32[10,2]{1,0:T(8,128)S(1)} %copy.103.refs_6_.slots, ...), custom_call_target="tpu_custom_call", output_to_operand_aliasing={{2}: (8, {}), {3}: (9, {})} | custom-call | tf_op jit(solution)/shard_map/turn/pallas_call | solution.py:323
  224.1 9.2 %turn.16 = (bf16[32,4096]{1,0:T(8,128)(2,1)S(1)}, bf16[32,4096]{1,0:T(8,128)(2,1)S(1)}, bf16[5,8,128,1024]{3,2,1,0:T(8,128)(2,1)S(1)}, bf16[5,64,1024]{2,1,0:T(8,128)(2,1)S(1)}) custom-call(s32[10,2]{1,0:T(8,128)S(1)} %copy.103.refs_6_.slots, ...), custom_call_target="tpu_custom_call", output_to_operand_aliasing={{2}: (8, {}), {3}: (9, {})} | custom-call | tf_op jit(solution)/shard_map/turn/pallas_call | solution.py:323
  237.9 9.2 %turn.17 = (bf16[32,4096]{1,0:T(8,128)(2,1)S(1)}, bf16[32,4096]{1,0:T(8,128)(2,1)S(1)}, bf16[5,8,128,1024]{3,2,1,0:T(8,128)(2,1)S(1)}, bf16[5,64,1024]{2,1,0:T(8,128)(2,1)S(1)}) custom-call(s32[10,2]{1,0:T(8,128)S(1)} %copy.103.refs_6_.slots, ...), custom_call_target="tpu_custom_call", output_to_operand_aliasing={{2}: (8, {}), {3}: (9, {})} | custom-call | tf_op jit(solution)/shard_map/turn/pallas_call | solution.py:323
  252.0 9.2 %turn.18 = (bf16[32,4096]{1,0:T(8,128)(2,1)S(1)}, bf16[32,4096]{1,0:T(8,128)(2,1)S(1)}, bf16[5,8,128,1024]{3,2,1,0:T(8,128)(2,1)S(1)}, bf16[5,64,1024]{2,1,0:T(8,128)(2,1)S(1)}) custom-call(s32[10,2]{1,0:T(8,128)S(1)} %copy.103.refs_6_.slots, ...), custom_call_target="tpu_custom_call", output_to_operand_aliasing={{2}: (8, {}), {3}: (9, {})} | custom-call | tf_op jit(solution)/shard_map/turn/pallas_call | solution.py:323
  265.0 9.9 %turn.19 = (bf16[32,4096]{1,0:T(8,128)(2,1)S(1)}, bf16[32,4096]{1,0:T(8,128)(2,1)}, bf16[5,8,128,1024]{3,2,1,0:T(8,128)(2,1)S(1)}, bf16[5,64,1024]{2,1,0:T(8,128)(2,1)S(1)}) custom-call(s32[10,2]{1,0:T(8,128)S(1)} %copy.103.refs_6_.slots, bf16[32,4096]{1,0:T(8,128)(2,1)S(1)} %collective-permute-done.41.refs_0_.refs_2_, ...), custom_call_target="tpu_custom_call", output_to_operand_aliasing={{2}: (8, {}), {3}: (9, {})} | custom-call | tf_op jit(solution)/shard_map/turn/pallas_call | solution.py:323
  275.6 6.9 %grads.1 = (bf16[1024,1024]{1,0:T(8,128)(2,1)S(1)}, bf16[1024,1024]{1,0:T(8,128)(2,1)S(1)}) custom-call(bf16[5,8,128,1024]{3,2,1,0:T(8,128)(2,1)S(1)} %get-tuple-element.187.ds_ref, bf16[4,8,128,1024]{3,2,1,0:T(8,128)(2,1)S(1)} %get-tuple-element.128.refs_6_.p_ref, bf16[256,1024]{1,0:T(8,128)(2,1)} %copy-done.20, ...), custom_call_target="tpu_custom_call" | custom-call | tf_op jit(solution)/shard_map/grads/pallas_call | solution.py:378
  282.5 12.6 %back.5 = (bf16[64,4096]{1,0:T(8,128)(2,1)S(1)}, bf16[64,4096]{1,0:T(8,128)(2,1)S(1)}, bf16[64,4096]{1,0:T(8,128)(2,1)}, bf16[64,4096]{1,0:T(8,128)(2,1)S(1)}) custom-call(bf16[1024,1024]{1,0:T(8,128)(2,1)S(1)} %get-tuple-element.189.kg_ref, bf16[1024,1024]{1,0:T(8,128)(2,1)S(1)} %get-tuple-element.190.vg_ref, bf16[4096,1024]{1,0:T(8,128)(2,1)} %bitcast.42, ...), custom_call_target="tpu_custom_call" | custom-call | tf_op jit(solution)/shard_map/back/pallas_call | solution.py:413
  299.7 10.4 %back.6 = (bf16[64,4096]{1,0:T(8,128)(2,1)S(1)}, bf16[64,4096]{1,0:T(8,128)(2,1)S(1)}, bf16[64,4096]{1,0:T(8,128)(2,1)S(1)}, bf16[64,4096]{1,0:T(8,128)(2,1)S(1)}) custom-call(bf16[1024,1024]{1,0:T(8,128)(2,1)S(1)} %copy-done.14, bf16[1024,1024]{1,0:T(8,128)(2,1)S(1)} %copy-done.16, bf16[4096,1024]{1,0:T(8,128)(2,1)} %bitcast.43, bf16[4096,1024]{1,0:T(8,128)(2,1)} %bitcast.53), custom_call_target="tpu_custom_call" | custom-call | tf_op jit(solution)/shard_map/back/pallas_call | solution.py:413
  310.1 10.5 %back.7 = (bf16[64,4096]{1,0:T(8,128)(2,1)S(1)}, bf16[64,4096]{1,0:T(8,128)(2,1)S(1)}, bf16[64,4096]{1,0:T(8,128)(2,1)S(1)}, bf16[64,4096]{1,0:T(8,128)(2,1)S(1)}) custom-call(bf16[1024,1024]{1,0:T(8,128)(2,1)S(1)} %copy-done.14, bf16[1024,1024]{1,0:T(8,128)(2,1)S(1)} %copy-done.16, bf16[4096,1024]{1,0:T(8,128)(2,1)} %bitcast.44, bf16[4096,1024]{1,0:T(8,128)(2,1)} %bitcast.54), custom_call_target="tpu_custom_call" | custom-call | tf_op jit(solution)/shard_map/back/pallas_call | solution.py:413
  320.7 10.6 %back.4 = (bf16[64,4096]{1,0:T(8,128)(2,1)S(1)}, bf16[64,4096]{1,0:T(8,128)(2,1)S(1)}, bf16[64,4096]{1,0:T(8,128)(2,1)S(1)}, bf16[64,4096]{1,0:T(8,128)(2,1)S(1)}) custom-call(bf16[1024,1024]{1,0:T(8,128)(2,1)S(1)} %copy-done.14, bf16[1024,1024]{1,0:T(8,128)(2,1)S(1)} %copy-done.16, bf16[4096,1024]{1,0:T(8,128)(2,1)} %bitcast.45, bf16[4096,1024]{1,0:T(8,128)(2,1)} %bitcast.55), custom_call_target="tpu_custom_call" | custom-call | tf_op jit(solution)/shard_map/back/pallas_call | solution.py:413
  336.8 6.0 %collective-permute-start.51 = (bf16[64,4096]{1,0:T(8,128)(2,1)S(1)}, bf16[64,4096]{1,0:T(8,128)(2,1)S(1)}, u32[]{:S(2)}, u32[]{:S(2)}) collective-permute-start(bf16[64,4096]{1,0:T(8,128)(2,1)S(1)} %fusion.3), channel_id=1, source_target_pairs={{0,2},{6,4},{1,3},{7,5},{8,10},{14,12},{9,11},{15,13},{16,18},{22,... | collective-permute-start | bytes 1572872 | tf_op jit(solution)/shard_map/ppermute | solution.py:208
  343.1 11.2 %collective-permute-done.51 = bf16[64,4096]{1,0:T(8,128)(2,1)S(1)} collective-permute-done((bf16[64,4096]{1,0:T(8,128)(2,1)S(1)}, bf16[64,4096]{1,0:T(8,128)(2,1)S(1)}, u32[]{:S(2)}, u32[]{:S(2)}) %collective-permute-start.51) | collective-permute-done | bytes 524320 | tf_op jit(solution)/shard_map/ppermute | solution.py:208
  359.6 9.7 %collective-permute-done.60 = bf16[64,4096]{1,0:T(8,128)(2,1)S(1)} collective-permute-done((bf16[64,4096]{1,0:T(8,128)(2,1)S(1)}, bf16[64,4096]{1,0:T(8,128)(2,1)S(1)}, u32[]{:S(2)}, u32[]{:S(2)}) %collective-permute-start.60) | collective-permute-done | bytes 524320 | tf_op jit(solution)/shard_map/ppermute | solution.py:208
  374.0 7.4 %collective-permute-start.61 = (bf16[64,4096]{1,0:T(8,128)(2,1)S(1)}, bf16[64,4096]{1,0:T(8,128)(2,1)S(1)}, u32[]{:S(2)}, u32[]{:S(2)}) collective-permute-start(bf16[64,4096]{1,0:T(8,128)(2,1)S(1)} %add_convert_fusion.2), channel_id=1, source_target_pairs={{0,2},{2,4},{1,3},{3,5},{8,10},{10,12},{9,11},{11,13},{16,18},{18,... | collective-permute-start | bytes 1572872 | tf_op jit(solution)/shard_map/ppermute | solution.py:208
  387.4 7.2 %collective-permute-done.61 = bf16[64,4096]{1,0:T(8,128)(2,1)S(1)} collective-permute-done((bf16[64,4096]{1,0:T(8,128)(2,1)S(1)}, bf16[64,4096]{1,0:T(8,128)(2,1)S(1)}, u32[]{:S(2)}, u32[]{:S(2)}) %collective-permute-start.61) | collective-permute-done | bytes 524320 | tf_op jit(solution)/shard_map/ppermute | solution.py:208
  396.4 10.5 %collective-permute-start.63 = (bf16[64,4096]{1,0:T(8,128)(2,1)S(1)}, bf16[64,4096]{1,0:T(8,128)(2,1)S(1)}, u32[]{:S(2)}, u32[]{:S(2)}) collective-permute-start(bf16[64,4096]{1,0:T(8,128)(2,1)S(1)} %get-tuple-element.220), channel_id=1, source_target_pairs={{0,2},{2,4},{4,6},{1,3},{3,5},{5,7},{8,10},{10,12},{12,14},{9,11},... | collective-permute-start | bytes 1572872 | tf_op jit(solution)/shard_map/ppermute | solution.py:208
  419.4 6.1 %collective-permute-done.55 = bf16[64,4096]{1,0:T(8,128)(2,1)S(1)} collective-permute-done((bf16[64,4096]{1,0:T(8,128)(2,1)S(1)}, bf16[64,4096]{1,0:T(8,128)(2,1)S(1)}, u32[]{:S(2)}, u32[]{:S(2)}) %collective-permute-start.55) | collective-permute-done | bytes 524320 | tf_op jit(solution)/shard_map/ppermute | solution.py:208
  (257 shorter events, 132.2 us)
Async XLA Ops:
  2.0 19.8 %collective-permute-start.2 = (bf16[64,4096]{1,0:T(8,128)(2,1)S(1)}, bf16[64,4096]{1,0:T(8,128)(2,1)}, u32[]{:S(2)}, u32[]{:S(2)}) collective-permute-start(bf16[64,4096]{1,0:T(8,128)(2,1)S(1)} %get-tuple-element.231.refs_0_), channel_id=1, source_target_pairs={{6,4},{4,2},{2,0},{7,5},{5,3},{3,1},{14,12},{12,10},{10,8},{15,13}... | collective-permute-start | bytes 1572872 | tf_op jit(solution)/shard_map/ppermute | solution.py:208
  3.3 19.1 %collective-permute-start.4 = (bf16[64,4096]{1,0:T(8,128)(2,1)S(1)}, bf16[64,4096]{1,0:T(8,128)(2,1)}, u32[]{:S(2)}, u32[]{:S(2)}) collective-permute-start(bf16[64,4096]{1,0:T(8,128)(2,1)S(1)} %get-tuple-element.231.refs_0_), channel_id=1, source_target_pairs={{0,2},{2,4},{4,6},{1,3},{3,5},{5,7},{8,10},{10,12},{12,14},{9,11},... | collective-permute-start | bytes 1572872 | tf_op jit(solution)/shard_map/ppermute | solution.py:208
  9.7 20.5 %collective-permute-start.8 = (bf16[64,4096]{1,0:T(8,128)(2,1)S(1)}, bf16[64,4096]{1,0:T(8,128)(2,1)}, u32[]{:S(2)}, u32[]{:S(2)}) collective-permute-start(bf16[64,4096]{1,0:T(8,128)(2,1)S(1)} %get-tuple-element.230.refs_1_), channel_id=1, source_target_pairs={{6,4},{4,2},{2,0},{7,5},{5,3},{3,1},{14,12},{12,10},{10,8},{15,13}... | collective-permute-start | bytes 1572872 | tf_op jit(solution)/shard_map/ppermute | solution.py:208
  11.0 20.3 %collective-permute-start.7 = (bf16[64,4096]{1,0:T(8,128)(2,1)S(1)}, bf16[64,4096]{1,0:T(8,128)(2,1)S(1)}, u32[]{:S(2)}, u32[]{:S(2)}) collective-permute-start(bf16[64,4096]{1,0:T(8,128)(2,1)S(1)} %get-tuple-element.230.refs_1_), channel_id=1, source_target_pairs={{0,2},{2,4},{4,6},{1,3},{3,5},{5,7},{8,10},{10,12},{12,14},{9,11},... | collective-permute-start | bytes 1572872 | tf_op jit(solution)/shard_map/ppermute | solution.py:208
  15.6 17.1 %collective-permute-start.18 = (bf16[64,4096]{1,0:T(8,128)(2,1)S(1)}, bf16[64,4096]{1,0:T(8,128)(2,1)S(1)}, u32[]{:S(2)}, u32[]{:S(2)}) collective-permute-start(bf16[64,4096]{1,0:T(8,128)(2,1)S(1)} %get-tuple-element.231.refs_0_), channel_id=1, source_target_pairs={{1,0},{0,1},{3,2},{2,3},{5,4},{4,5},{7,6},{6,7},{9,8},{8,9},{11,10... | collective-permute-start | bytes 1572872 | tf_op jit(solution)/shard_map/ppermute | solution.py:205
  22.4 23.8 %collective-permute-start.1 = (bf16[128,4096]{1,0:T(8,128)(2,1)S(1)}, bf16[128,4096]{1,0:T(8,128)(2,1)S(1)}, u32[]{:S(2)}, u32[]{:S(2)}) collective-permute-start(bf16[128,4096]{1,0:T(8,128)(2,1)S(1)} %bitcast.62), channel_id=1, source_target_pairs={{1,0},{0,1},{3,2},{2,3},{5,4},{4,5},{7,6},{6,7},{9,8},{8,9},{11,10... | collective-permute-start | bytes 3145736 | tf_op jit(solution)/shard_map/ppermute | solution.py:205
  30.3 105.4 %collective-permute-start.20 = (bf16[32,4096]{1,0:T(8,128)(2,1)}, bf16[32,4096]{1,0:T(8,128)(2,1)S(1)}, u32[]{:S(2)}, u32[]{:S(2)}) collective-permute-start(bf16[32,4096]{1,0:T(8,128)(2,1)} %get-tuple-element.222.refs_0_.refs_2_), channel_id=1, source_target_pairs={{1,0},{0,1},{3,2},{2,3},{5,4},{4,5},{7,6},{6,7},{9,8},{8,9},{11,10... | collective-permute-start | bytes 786440 | tf_op jit(solution)/shard_map/ppermute | solution.py:205
  32.7 65.6 %collective-permute-start.16 = (bf16[64,4096]{1,0:T(8,128)(2,1)S(1)}, bf16[64,4096]{1,0:T(8,128)(2,1)S(1)}, u32[]{:S(2)}, u32[]{:S(2)}) collective-permute-start(bf16[64,4096]{1,0:T(8,128)(2,1)S(1)} %get-tuple-element.228.refs_0_), channel_id=1, source_target_pairs={{1,0},{0,1},{3,2},{2,3},{5,4},{4,5},{7,6},{6,7},{9,8},{8,9},{11,10... | collective-permute-start | bytes 1572872 | tf_op jit(solution)/shard_map/ppermute | solution.py:205
  32.7 66.1 %collective-permute-start.17 = (bf16[64,4096]{1,0:T(8,128)(2,1)S(1)}, bf16[64,4096]{1,0:T(8,128)(2,1)S(1)}, u32[]{:S(2)}, u32[]{:S(2)}) collective-permute-start(bf16[64,4096]{1,0:T(8,128)(2,1)S(1)} %get-tuple-element.226.refs_1_), channel_id=1, source_target_pairs={{1,0},{0,1},{3,2},{2,3},{5,4},{4,5},{7,6},{6,7},{9,8},{8,9},{11,10... | collective-permute-start | bytes 1572872 | tf_op jit(solution)/shard_map/ppermute | solution.py:205
  33.2 16.8 %collective-permute-start.3 = (bf16[64,4096]{1,0:T(8,128)(2,1)}, bf16[64,4096]{1,0:T(8,128)(2,1)S(1)}, u32[]{:S(2)}, u32[]{:S(2)}) collective-permute-start(bf16[64,4096]{1,0:T(8,128)(2,1)} %collective-permute-done.2), channel_id=1, source_target_pairs={{4,2},{2,0},{5,3},{3,1},{12,10},{10,8},{13,11},{11,9},{20,18},{18,... | collective-permute-start | bytes 1572872 | tf_op jit(solution)/shard_map/ppermute | solution.py:208
  50.0 19.8 %collective-permute-start.9 = (bf16[64,4096]{1,0:T(8,128)(2,1)}, bf16[64,4096]{1,0:T(8,128)(2,1)S(1)}, u32[]{:S(2)}, u32[]{:S(2)}) collective-permute-start(bf16[64,4096]{1,0:T(8,128)(2,1)} %collective-permute-done.8), channel_id=1, source_target_pairs={{4,2},{2,0},{5,3},{3,1},{12,10},{10,8},{13,11},{11,9},{20,18},{18,... | collective-permute-start | bytes 1572872 | tf_op jit(solution)/shard_map/ppermute | solution.py:208
  51.4 19.6 %collective-permute-start.10 = (bf16[64,4096]{1,0:T(8,128)(2,1)S(1)}, bf16[64,4096]{1,0:T(8,128)(2,1)S(1)}, u32[]{:S(2)}, u32[]{:S(2)}) collective-permute-start(bf16[64,4096]{1,0:T(8,128)(2,1)S(1)} %copy-done.32), channel_id=1, source_target_pairs={{2,4},{4,6},{3,5},{5,7},{10,12},{12,14},{11,13},{13,15},{18,20},{2... | collective-permute-start | bytes 1572872 | tf_op jit(solution)/shard_map/ppermute | solution.py:208
  69.8 14.7 %collective-permute-start.6 = (bf16[64,4096]{1,0:T(8,128)(2,1)S(1)}, bf16[64,4096]{1,0:T(8,128)(2,1)S(1)}, u32[]{:S(2)}, u32[]{:S(2)}) collective-permute-start(bf16[64,4096]{1,0:T(8,128)(2,1)S(1)} %broadcast_select_fusion.5.refs_0_), channel_id=1, source_target_pairs={{4,6},{2,0},{5,7},{3,1},{12,14},{10,8},{13,15},{11,9},{20,22},{18,... | collective-permute-start | bytes 1572872 | tf_op jit(solution)/shard_map/ppermute | solution.py:208
  71.1 38.8 %collective-permute-start.14 = (bf16[64,4096]{1,0:T(8,128)(2,1)S(1)}, bf16[64,4096]{1,0:T(8,128)(2,1)S(1)}, u32[]{:S(2)}, u32[]{:S(2)}) collective-permute-start(bf16[64,4096]{1,0:T(8,128)(2,1)S(1)} %broadcast_select_fusion.5.refs_0_), channel_id=1, source_target_pairs={{1,0},{0,1},{3,2},{2,3},{5,4},{4,5},{7,6},{6,7},{9,8},{8,9},{11,10... | collective-permute-start | bytes 1572872 | tf_op jit(solution)/shard_map/ppermute | solution.py:205
  84.4 13.8 %collective-permute-start.11 = (bf16[64,4096]{1,0:T(8,128)(2,1)S(1)}, bf16[64,4096]{1,0:T(8,128)(2,1)S(1)}, u32[]{:S(2)}, u32[]{:S(2)}) collective-permute-start(bf16[64,4096]{1,0:T(8,128)(2,1)S(1)} %broadcast_select_fusion.2.refs_1_), channel_id=1, source_target_pairs={{4,6},{2,0},{5,7},{3,1},{12,14},{10,8},{13,15},{11,9},{20,22},{18,... | collective-permute-start | bytes 1572872 | tf_op jit(solution)/shard_map/ppermute | solution.py:208
  98.3 16.5 %collective-permute-start.12 = (bf16[64,4096]{1,0:T(8,128)(2,1)S(1)}, bf16[64,4096]{1,0:T(8,128)(2,1)S(1)}, u32[]{:S(2)}, u32[]{:S(2)}) collective-permute-start(bf16[64,4096]{1,0:T(8,128)(2,1)S(1)} %broadcast_select_fusion.7.refs_0_), channel_id=1, source_target_pairs={{1,0},{0,1},{3,2},{2,3},{5,4},{4,5},{7,6},{6,7},{9,8},{8,9},{11,10... | collective-permute-start | bytes 1572872 | tf_op jit(solution)/shard_map/ppermute | solution.py:205
  98.9 15.9 %collective-permute-start.13 = (bf16[64,4096]{1,0:T(8,128)(2,1)S(1)}, bf16[64,4096]{1,0:T(8,128)(2,1)S(1)}, u32[]{:S(2)}, u32[]{:S(2)}) collective-permute-start(bf16[64,4096]{1,0:T(8,128)(2,1)S(1)} %broadcast_select_fusion.6.refs_1_), channel_id=1, source_target_pairs={{1,0},{0,1},{3,2},{2,3},{5,4},{4,5},{7,6},{6,7},{9,8},{8,9},{11,10... | collective-permute-start | bytes 1572872 | tf_op jit(solution)/shard_map/ppermute | solution.py:205
  296.0 39.2 %collective-permute-start.48 = (bf16[64,4096]{1,0:T(8,128)(2,1)}, bf16[64,4096]{1,0:T(8,128)(2,1)}, u32[]{:S(2)}, u32[]{:S(2)}) collective-permute-start(bf16[64,4096]{1,0:T(8,128)(2,1)} %get-tuple-element.194), channel_id=1, source_target_pairs={{1,0},{0,1},{3,2},{2,3},{5,4},{4,5},{7,6},{6,7},{9,8},{8,9},{11,10... | collective-permute-start | bytes 1572872 | tf_op jit(solution)/shard_map/ppermute | solution.py:205
  296.5 35.9 %collective-permute-start.46 = (bf16[32,4096]{1,0:T(8,128)(2,1)}, bf16[32,4096]{1,0:T(8,128)(2,1)}, u32[]{:S(2)}, u32[]{:S(2)}) collective-permute-start(bf16[32,4096]{1,0:T(8,128)(2,1)} %get-tuple-element.184), channel_id=1, source_target_pairs={{1,0},{0,1},{3,2},{2,3},{5,4},{4,5},{7,6},{6,7},{9,8},{8,9},{11,10... | collective-permute-start | bytes 786440 | tf_op jit(solution)/shard_map/ppermute | solution.py:205
  331.9 55.5 %collective-permute-start.58 = (bf16[64,4096]{1,0:T(8,128)(2,1)S(1)}, bf16[64,4096]{1,0:T(8,128)(2,1)S(1)}, u32[]{:S(2)}, u32[]{:S(2)}) collective-permute-start(bf16[64,4096]{1,0:T(8,128)(2,1)S(1)} %get-tuple-element.204), channel_id=1, source_target_pairs={{1,0},{0,1},{3,2},{2,3},{5,4},{4,5},{7,6},{6,7},{9,8},{8,9},{11,10... | collective-permute-start | bytes 1572872 | tf_op jit(solution)/shard_map/ppermute | solution.py:205
  332.0 26.9 %collective-permute-start.59 = (bf16[64,4096]{1,0:T(8,128)(2,1)S(1)}, bf16[64,4096]{1,0:T(8,128)(2,1)S(1)}, u32[]{:S(2)}, u32[]{:S(2)}) collective-permute-start(bf16[64,4096]{1,0:T(8,128)(2,1)S(1)} %get-tuple-element.206), channel_id=1, source_target_pairs={{1,0},{0,1},{3,2},{2,3},{5,4},{4,5},{7,6},{6,7},{9,8},{8,9},{11,10... | collective-permute-start | bytes 1572872 | tf_op jit(solution)/shard_map/ppermute | solution.py:205
  335.2 38.7 %collective-permute-start.49 = (bf16[64,4096]{1,0:T(8,128)(2,1)S(1)}, bf16[64,4096]{1,0:T(8,128)(2,1)S(1)}, u32[]{:S(2)}, u32[]{:S(2)}) collective-permute-start(bf16[64,4096]{1,0:T(8,128)(2,1)S(1)} %get-tuple-element.196), channel_id=1, source_target_pairs={{1,0},{0,1},{3,2},{2,3},{5,4},{4,5},{7,6},{6,7},{9,8},{8,9},{11,10... | collective-permute-start | bytes 1572872 | tf_op jit(solution)/shard_map/ppermute | solution.py:205
  336.8 17.5 %collective-permute-start.51 = (bf16[64,4096]{1,0:T(8,128)(2,1)S(1)}, bf16[64,4096]{1,0:T(8,128)(2,1)S(1)}, u32[]{:S(2)}, u32[]{:S(2)}) collective-permute-start(bf16[64,4096]{1,0:T(8,128)(2,1)S(1)} %fusion.3), channel_id=1, source_target_pairs={{0,2},{6,4},{1,3},{7,5},{8,10},{14,12},{9,11},{15,13},{16,18},{22,... | collective-permute-start | bytes 1572872 | tf_op jit(solution)/shard_map/ppermute | solution.py:208
  343.0 68.9 %collective-permute-start.56 = (bf16[64,4096]{1,0:T(8,128)(2,1)S(1)}, bf16[64,4096]{1,0:T(8,128)(2,1)S(1)}, u32[]{:S(2)}, u32[]{:S(2)}) collective-permute-start(bf16[64,4096]{1,0:T(8,128)(2,1)S(1)} %get-tuple-element.200), channel_id=1, source_target_pairs={{1,0},{0,1},{3,2},{2,3},{5,4},{4,5},{7,6},{6,7},{9,8},{8,9},{11,10... | collective-permute-start | bytes 1572872 | tf_op jit(solution)/shard_map/ppermute | solution.py:205
  354.3 15.0 %collective-permute-start.60 = (bf16[64,4096]{1,0:T(8,128)(2,1)S(1)}, bf16[64,4096]{1,0:T(8,128)(2,1)S(1)}, u32[]{:S(2)}, u32[]{:S(2)}) collective-permute-start(bf16[64,4096]{1,0:T(8,128)(2,1)S(1)} %add_convert_fusion.3), channel_id=1, source_target_pairs={{0,2},{6,4},{1,3},{7,5},{8,10},{14,12},{9,11},{15,13},{16,18},{22,... | collective-permute-start | bytes 1572872 | tf_op jit(solution)/shard_map/ppermute | solution.py:208
  358.9 15.1 %collective-permute-start.54 = (bf16[64,4096]{1,0:T(8,128)(2,1)S(1)}, bf16[64,4096]{1,0:T(8,128)(2,1)S(1)}, u32[]{:S(2)}, u32[]{:S(2)}) collective-permute-start(bf16[64,4096]{1,0:T(8,128)(2,1)S(1)} %add_convert_fusion.6), channel_id=1, source_target_pairs={{6,4},{4,2},{7,5},{5,3},{14,12},{12,10},{15,13},{13,11},{22,20},{2... | collective-permute-start | bytes 1572872 | tf_op jit(solution)/shard_map/ppermute | solution.py:208
  369.3 15.6 %collective-permute-start.52 = (bf16[64,4096]{1,0:T(8,128)(2,1)S(1)}, bf16[64,4096]{1,0:T(8,128)(2,1)S(1)}, u32[]{:S(2)}, u32[]{:S(2)}) collective-permute-start(bf16[64,4096]{1,0:T(8,128)(2,1)S(1)} %add_convert_fusion.6), channel_id=1, source_target_pairs={{0,2},{2,4},{1,3},{3,5},{8,10},{10,12},{9,11},{11,13},{16,18},{18,... | collective-permute-start | bytes 1572872 | tf_op jit(solution)/shard_map/ppermute | solution.py:208
  373.9 45.5 %collective-permute-start.47 = (bf16[64,4096]{1,0:T(8,128)(2,1)S(1)}, bf16[64,4096]{1,0:T(8,128)(2,1)S(1)}, u32[]{:S(2)}, u32[]{:S(2)}) collective-permute-start(bf16[64,4096]{1,0:T(8,128)(2,1)S(1)} %get-tuple-element.192), channel_id=1, source_target_pairs={{1,0},{0,1},{3,2},{2,3},{5,4},{4,5},{7,6},{6,7},{9,8},{8,9},{11,10... | collective-permute-start | bytes 1572872 | tf_op jit(solution)/shard_map/ppermute | solution.py:205
  374.0 20.7 %collective-permute-start.61 = (bf16[64,4096]{1,0:T(8,128)(2,1)S(1)}, bf16[64,4096]{1,0:T(8,128)(2,1)S(1)}, u32[]{:S(2)}, u32[]{:S(2)}) collective-permute-start(bf16[64,4096]{1,0:T(8,128)(2,1)S(1)} %add_convert_fusion.2), channel_id=1, source_target_pairs={{0,2},{2,4},{1,3},{3,5},{8,10},{10,12},{9,11},{11,13},{16,18},{18,... | collective-permute-start | bytes 1572872 | tf_op jit(solution)/shard_map/ppermute | solution.py:208
  395.1 20.7 %collective-permute-start.64 = (bf16[64,4096]{1,0:T(8,128)(2,1)S(1)}, bf16[64,4096]{1,0:T(8,128)(2,1)S(1)}, u32[]{:S(2)}, u32[]{:S(2)}) collective-permute-start(bf16[64,4096]{1,0:T(8,128)(2,1)S(1)} %get-tuple-element.221), channel_id=1, source_target_pairs={{6,4},{4,2},{2,0},{7,5},{5,3},{3,1},{14,12},{12,10},{10,8},{15,13}... | collective-permute-start | bytes 1572872 | tf_op jit(solution)/shard_map/ppermute | solution.py:208
  396.4 22.7 %collective-permute-start.63 = (bf16[64,4096]{1,0:T(8,128)(2,1)S(1)}, bf16[64,4096]{1,0:T(8,128)(2,1)S(1)}, u32[]{:S(2)}, u32[]{:S(2)}) collective-permute-start(bf16[64,4096]{1,0:T(8,128)(2,1)S(1)} %get-tuple-element.220), channel_id=1, source_target_pairs={{0,2},{2,4},{4,6},{1,3},{3,5},{5,7},{8,10},{10,12},{12,14},{9,11},... | collective-permute-start | bytes 1572872 | tf_op jit(solution)/shard_map/ppermute | solution.py:208
  408.0 18.8 %collective-permute-start.53 = (bf16[64,4096]{1,0:T(8,128)(2,1)S(1)}, bf16[64,4096]{1,0:T(8,128)(2,1)S(1)}, u32[]{:S(2)}, u32[]{:S(2)}) collective-permute-start(bf16[64,4096]{1,0:T(8,128)(2,1)S(1)} %get-tuple-element.219), channel_id=1, source_target_pairs={{0,2},{2,4},{4,6},{1,3},{3,5},{5,7},{8,10},{10,12},{12,14},{9,11},... | collective-permute-start | bytes 1572872 | tf_op jit(solution)/shard_map/ppermute | solution.py:208
  (74 other events, 697.1 us)

commit v4 on v3

--- a/solution.py
+++ b/solution.py
@@ -82,7 +82,9 @@
 
 
 def back_kernel(kg_ref, vg_ref, wk_ref, wv_ref, *out_refs):
-    out = dot(kg_ref[...], wk_ref[...], NT) + dot(vg_ref[...], wv_ref[...], NT)
+    block = out_refs[0].shape[1]
+    place = pl.ds(pl.multiple_of(pl.program_id(0) * block, block), block)
+    out = dot(kg_ref[...], wk_ref[place, :], NT) + dot(vg_ref[...], wv_ref[place, :], NT)
     rows = out_refs[0].shape[0]
     for i, ref in enumerate(out_refs):
         ref[...] = out[i * rows : (i + 1) * rows].astype(bf16)
@@ -151,7 +153,19 @@
     all_ref[pl.ds(pl.multiple_of(slots[t, 1] * rows, rows), rows), :] = out
 
 
-def grads_kernel(micro, ds_ref, p_ref, q_ref, ag_ref, kg_ref, vg_ref):
+def grads_kernel(
+    micro, ds_ref, p_ref, q_ref, ag_ref, wk_ref, wv_ref, kg_ref, vg_ref, wk_out, wv_out, sems
+):
+    copies = [
+        pltpu.make_async_copy(wk_ref, wk_out, sems.at[0]),
+        pltpu.make_async_copy(wv_ref, wv_out, sems.at[1]),
+    ]
+
+    @pl.when(pl.program_id(0) == 0)
+    def _():
+        for copy in copies:
+            copy.start()
+
     rows = ag_ref.shape[1]
     pair = pl.program_id(0)
     cols = pl.ds(pl.multiple_of(pair * PAIR, PAIR), PAIR)
@@ -167,6 +181,11 @@
     vg = dot(ag.T.astype(bf16), p, NN)
     kg_ref[...] = kg.T.astype(bf16)
     vg_ref[...] = vg.T.astype(bf16)
+
+    @pl.when(pl.program_id(0) == pl.num_programs(0) - 1)
+    def _():
+        for copy in copies:
+            copy.wait()
 
 
 def all_of_it(
@@ -247,8 +266,9 @@
     slots = jnp.stack([read, jnp.where(micro == read, read, MICRO)], axis=1)
     outer = (section == 0) | (section == 3)
     is_last = section == sections - 1
-    wk, wv, low, outer, is_last, slots = lax.optimization_barrier(
-        (wk, wv, low, outer, is_last, slots)
+    is_first, is_second = section == 1, section == 2
+    wk, wv, low, outer, is_last, is_first, is_second, slots = lax.optimization_barrier(
+        (wk, wv, low, outer, is_last, is_first, is_second, slots)
     )
     size = share // PIECES
     mine = [enc_rows[0, i * size : (i + 1) * size] for i in range(PIECES)]
@@ -375,7 +395,7 @@
         if t + SKEW < turns:
             hops[t] = along(mine, (3, 2), (2, 1), (1, 0))
 
-    kg, vg = pl.pallas_call(
+    kg, vg, wk_back, wv_back = pl.pallas_call(
         functools.partial(grads_kernel, MICRO),
         grid=(pairs,),
         in_specs=[
@@ -383,12 +403,18 @@
             resident,
             pl.BlockSpec((tokens, PAIR), lambda p: (0, p)),
             resident,
+            any_spec,
+            any_spec,
         ],
-        out_specs=[pl.BlockSpec((enc, PAIR), lambda p: (0, p))] * 2,
-        out_shape=[jax.ShapeDtypeStruct((enc, width), bf16)] * 2,
-        compiler_params=small,
+        out_specs=[pl.BlockSpec((enc, PAIR), lambda p: (0, p))] * 2 + [resident] * 2,
+        out_shape=[jax.ShapeDtypeStruct((enc, width), bf16)] * 2
+        + [in_vmem(wk.shape), in_vmem(wv.shape)],
+        scratch_shapes=[pltpu.SemaphoreType.DMA((2,))],
+        compiler_params=least,
         name="grads",
-    )(held[0], probs, in_hbm(queries), held[1])
+    )(
+        held[0], probs, in_hbm(queries), held[1], in_hbm(w_key[0]), in_hbm(w_value[0])
+    )
 
     out_block = min(OUT_BLOCK, model)
 
@@ -414,12 +440,12 @@
             back_kernel,
             grid=(model // out_block,),
             in_specs=[pl.BlockSpec((rows, width), lambda i: (slot, 0))] * 2
-            + [pl.BlockSpec((out_block, width), lambda i: (i, 0))] * 2,
+            + [resident] * 2,
             out_specs=[pl.BlockSpec((size, out_block), lambda i: (0, i))] * (n * PIECES),
             out_shape=[jax.ShapeDtypeStruct((size, model), bf16)] * (n * PIECES),
-            compiler_params=small,
+            compiler_params=least,
             name="back",
-        )(kg, vg, in_hbm(w_key[0]), in_hbm(w_value[0]))
+        )(kg, vg, wk_back, wv_back)
 
     far, mid = back(3), back(2)
     got = []
@@ -440,8 +466,8 @@
         ends = (far[i], near[i], up2[i], down2[i])
         a, b, u, d = ends if i == 0 else behind(ends, v)
         a, b = total(a), total(b)
-        v = (jnp.where(section == 2, a, b) + u.astype(f32)).astype(bf16)
-        w = (jnp.where(section == 1, a, b) + d.astype(f32)).astype(bf16)
+        v = (jnp.where(is_second, a, b) + u.astype(f32)).astype(bf16)
+        w = (jnp.where(is_first, a, b) + d.astype(f32)).astype(bf16)
         up3.append(along(v, (0, 1), (1, 2), (2, 3)))
         down3.append(along(w, (3, 2), (2, 1), (1, 0)))
     enc_share = [

time: 435 us -> 418 us (0.961)
  Pallas kernels: 195 us -> 178 us
  waiting for transfers between devices: 110 us -> 118 us
    pallas_call x4, Pallas kernels: 44.2 us -> 24.5 us  [back_call(): pl.pallas_call(back_kernel, grid=(model // out_block,), in_specs=[pl.Bloc...]
    pallas_call x1, Pallas kernels: 6.91 us -> 11.3 us  [all_of_it(): pl.pallas_call(functools.partial(grads_kernel, MICRO), grid=(pairs,), in_...]
    ppermute x28, waiting for transfers between devices: 108 us -> 112 us  [along(): return lax.ppermute(x, 'section', pairs)]
    unnamed x83 -> x61, local copies, waits for them, and re-layouts: 18.9 us -> 17.5 us
  transfers between devices with their start and end apart: 65 -> 65, of which waited for: 23 -> 24; matrix products, arithmetic and copies ran while one was open for 4% -> 4% of each run, Pallas kernels for 36% -> 38%
where the time goes in v4:
time: 418 us; the launch traced here: 413 us
  Pallas kernels  178 us (43%)
  waiting for transfers between devices  118 us (28%)
  starting transfers between devices  79.5 us (19%)
  local copies, waits for them, and re-layouts  23.1 us (6%)
  other arithmetic  9.88 us (2%)
    ppermute x28, waiting for transfers between devices, along(): return lax.ppermute(x, 'section', pairs)  112 us
    pallas_call x10, Pallas kernels, turn(): pl.pallas_call(functools.partial(turn_kernel, parts, r, t, block), grid_s...  93.3 us
    ppermute x28, starting transfers between devices, along(): return lax.ppermute(x, 'section', pairs)  70.2 us
    pallas_call x4, Pallas kernels, back_call(): pl.pallas_call(back_kernel, grid=(model // out_block,), in_specs=[pl.Bloc...  24.5 us
    pallas_call x4, Pallas kernels, all_of_it(): keys_values = project(*xs, wk, wv, *keys_values, *early)  19.5 us
    unnamed x61, local copies, waits for them, and re-layouts  17.5 us
    pallas_call x1, Pallas kernels, all_of_it(): pl.pallas_call(probs_kernel, grid=(pairs, MICRO), in_specs=[pl.BlockSpec(...  15.9 us
    pallas_call x10, Pallas kernels, norm_back(): pl.pallas_call(functools.partial(norm_kernel, k, t), grid_spec=pltpu.Pref...  13.1 us
  transfers between devices with their start and end apart: 65, of which 24 were waited for; matrix products, arithmetic and copies ran while one was open for 4% of the time, Pallas kernels for 38%

profile of v4, /device:TPU:0, one launch (start us, length us, event | category | flops | bytes accessed | tf_op | source)
XLA Modules:
  0.0 412.8 jit_solution(12497355545019007494)
XLA Ops:
  3.9 5.9 %collective-permute-start.7 = (bf16[64,4096]{1,0:T(8,128)(2,1)S(1)}, bf16[64,4096]{1,0:T(8,128)(2,1)}, u32[]{:S(2)}, u32[]{:S(2)}) collective-permute-start(bf16[64,4096]{1,0:T(8,128)(2,1)S(1)} %get-tuple-element.238.refs_1_), channel_id=1, source_target_pairs={{0,2},{2,4},{4,6},{1,3},{3,5},{5,7},{8,10},{10,12},{12,14},{9,11},... | collective-permute-start | bytes 1572872 | tf_op jit(solution)/shard_map/ppermute | solution.py:227
  22.9 9.2 %collective-permute-done.4 = bf16[64,4096]{1,0:T(8,128)(2,1)} collective-permute-done((bf16[64,4096]{1,0:T(8,128)(2,1)S(1)}, bf16[64,4096]{1,0:T(8,128)(2,1)}, u32[]{:S(2)}, u32[]{:S(2)}) %collective-permute-start.4) | collective-permute-done | bytes 524320 | tf_op jit(solution)/shard_map/ppermute | solution.py:227
  45.7 4.9 %project.4 = (bf16[1024,1024]{1,0:T(8,128)(2,1)S(1)}, bf16[1024,1024]{1,0:T(8,128)(2,1)S(1)}) custom-call(bf16[64,4096]{1,0:T(8,128)(2,1)S(1)} %get-tuple-element.239.refs_0_, bf16[64,4096]{1,0:T(8,128)(2,1)S(1)} %get-tuple-element.238.refs_1_, bf16[64,4096]{1,0:T(8,128)(2,1)S(1)} %collective-permute-done.18.refs_2_, ...), custom_call_target="tpu_custom_call" | custom-call | tf_op jit(solution)/shard_map/project/pallas_call | solution.py:314
  55.9 25.2 %collective-permute-done.3 = bf16[64,4096]{1,0:T(8,128)(2,1)S(1)} collective-permute-done((bf16[64,4096]{1,0:T(8,128)(2,1)S(1)}, bf16[64,4096]{1,0:T(8,128)(2,1)S(1)}, u32[]{:S(2)}, u32[]{:S(2)}) %collective-permute-start.3) | collective-permute-done | bytes 524320 | tf_op jit(solution)/shard_map/ppermute | solution.py:227
  82.4 11.4 %collective-permute-done.11 = bf16[64,4096]{1,0:T(8,128)(2,1)S(1)} collective-permute-done((bf16[64,4096]{1,0:T(8,128)(2,1)S(1)}, bf16[64,4096]{1,0:T(8,128)(2,1)S(1)}, u32[]{:S(2)}, u32[]{:S(2)}) %collective-permute-start.11) | collective-permute-done | bytes 524320 | tf_op jit(solution)/shard_map/ppermute | solution.py:227
  95.4 10.4 %collective-permute-done.6 = bf16[64,4096]{1,0:T(8,128)(2,1)S(1)} collective-permute-done((bf16[64,4096]{1,0:T(8,128)(2,1)S(1)}, bf16[64,4096]{1,0:T(8,128)(2,1)S(1)}, u32[]{:S(2)}, u32[]{:S(2)}) %collective-permute-start.6) | collective-permute-done | bytes 524320 | tf_op jit(solution)/shard_map/ppermute | solution.py:227
  112.6 4.9 %project.5 = (bf16[1024,1024]{1,0:T(8,128)(2,1)S(1)}, bf16[1024,1024]{1,0:T(8,128)(2,1)S(1)}) custom-call(bf16[64,4096]{1,0:T(8,128)(2,1)S(1)} %get-tuple-element.236.refs_0_, bf16[64,4096]{1,0:T(8,128)(2,1)S(1)} %get-tuple-element.234.refs_1_, bf16[64,4096]{1,0:T(8,128)(2,1)S(1)} %collective-permute-done.16.refs_2_, ...), custom_call_target="tpu_custom_call", output_to_operand_aliasing={{0}: (6, {}), {1}: (7, {})} | custom-call | tf_op jit(solution)/shard_map/project/pallas_call | solution.py:314
  117.5 4.9 %project.6 = (bf16[1024,1024]{1,0:T(8,128)(2,1)S(1)}, bf16[1024,1024]{1,0:T(8,128)(2,1)S(1)}) custom-call(bf16[64,4096]{1,0:T(8,128)(2,1)S(1)} %broadcast_select_fusion.5.refs_0_, bf16[64,4096]{1,0:T(8,128)(2,1)S(1)} %broadcast_select_fusion.2.refs_1_, ...), custom_call_target="tpu_custom_call", output_to_operand_aliasing={{0}: (6, {}), {1}: (7, {})} | custom-call | tf_op jit(solution)/shard_map/project/pallas_call | solution.py:314
  122.4 4.9 %project.7 = (bf16[1024,1024]{1,0:T(8,128)(2,1)S(1)}, bf16[1024,1024]{1,0:T(8,128)(2,1)S(1)}) custom-call(bf16[64,4096]{1,0:T(8,128)(2,1)S(1)} %broadcast_select_fusion.7.refs_0_, bf16[64,4096]{1,0:T(8,128)(2,1)S(1)} %broadcast_select_fusion.6.refs_1_, ...), custom_call_target="tpu_custom_call", output_to_operand_aliasing={{0}: (6, {}), {1}: (7, {})} | custom-call | tf_op jit(solution)/shard_map/project/pallas_call | solution.py:314
  127.3 15.9 %probs.1 = (bf16[4,8,128,1024]{3,2,1,0:T(8,128)(2,1)S(1)}, bf16[1024,4096]{1,0:T(8,128)(2,1)S(1)}, bf16[4096,1024]{1,0:T(8,128)(2,1)S(1)}) custom-call(bf16[256,1024]{1,0:T(8,128)(2,1)S(1)} %convolution_convert_fusion.q_ref, bf16[1024,1024]{1,0:T(8,128)(2,1)S(1)} %get-tuple-element.128.k_ref.refs_4_, s32[4,128,1]{2,1,0:T(8,128)S(1)} %copy-done.16, ...), custom_call_target="tpu_custom_call" | custom-call | tf_op jit(solution)/shard_map/probs/pallas_call | solution.py:317
  144.8 10.5 %turn.10 = (bf16[32,4096]{1,0:T(8,128)(2,1)S(1)}, bf16[32,4096]{1,0:T(8,128)(2,1)S(1)}, bf16[5,8,128,1024]{3,2,1,0:T(8,128)(2,1)S(1)}, bf16[5,64,1024]{2,1,0:T(8,128)(2,1)S(1)}) custom-call(s32[10,2]{1,0:T(8,128)S(1)} %copy.103.refs_6_.slots, bf16[32,4096]{1,0:T(8,128)(2,1)} %get-tuple-element.230.refs_0_.refs_2_, ...), custom_call_target="tpu_custom_call" | custom-call | tf_op jit(solution)/shard_map/turn/pallas_call | solution.py:343
  162.3 9.2 %turn.11 = (bf16[32,4096]{1,0:T(8,128)(2,1)S(1)}, bf16[32,4096]{1,0:T(8,128)(2,1)S(1)}, bf16[5,8,128,1024]{3,2,1,0:T(8,128)(2,1)S(1)}, bf16[5,64,1024]{2,1,0:T(8,128)(2,1)S(1)}) custom-call(s32[10,2]{1,0:T(8,128)S(1)} %copy.103.refs_6_.slots, bf16[32,4096]{1,0:T(8,128)(2,1)S(1)} %copy-done.17, ...), custom_call_target="tpu_custom_call", output_to_operand_aliasing={{2}: (8, {}), {3}: (9, {})} | custom-call | tf_op jit(solution)/shard_map/turn/pallas_call | solution.py:343
  175.6 9.2 %turn.12 = (bf16[32,4096]{1,0:T(8,128)(2,1)S(1)}, bf16[32,4096]{1,0:T(8,128)(2,1)S(1)}, bf16[5,8,128,1024]{3,2,1,0:T(8,128)(2,1)S(1)}, bf16[5,64,1024]{2,1,0:T(8,128)(2,1)S(1)}) custom-call(s32[10,2]{1,0:T(8,128)S(1)} %copy.103.refs_6_.slots, ...), custom_call_target="tpu_custom_call", output_to_operand_aliasing={{2}: (8, {}), {3}: (9, {})} | custom-call | tf_op jit(solution)/shard_map/turn/pallas_call | solution.py:343
  188.8 9.2 %turn.13 = (bf16[32,4096]{1,0:T(8,128)(2,1)S(1)}, bf16[32,4096]{1,0:T(8,128)(2,1)S(1)}, bf16[5,8,128,1024]{3,2,1,0:T(8,128)(2,1)S(1)}, bf16[5,64,1024]{2,1,0:T(8,128)(2,1)S(1)}) custom-call(s32[10,2]{1,0:T(8,128)S(1)} %copy.103.refs_6_.slots, ...), custom_call_target="tpu_custom_call", output_to_operand_aliasing={{2}: (8, {}), {3}: (9, {})} | custom-call | tf_op jit(solution)/shard_map/turn/pallas_call | solution.py:343
  202.2 9.2 %turn.14 = (bf16[32,4096]{1,0:T(8,128)(2,1)S(1)}, bf16[32,4096]{1,0:T(8,128)(2,1)S(1)}, bf16[5,8,128,1024]{3,2,1,0:T(8,128)(2,1)S(1)}, bf16[5,64,1024]{2,1,0:T(8,128)(2,1)S(1)}) custom-call(s32[10,2]{1,0:T(8,128)S(1)} %copy.103.refs_6_.slots, ...), custom_call_target="tpu_custom_call", output_to_operand_aliasing={{2}: (8, {}), {3}: (9, {})} | custom-call | tf_op jit(solution)/shard_map/turn/pallas_call | solution.py:343
  215.5 9.2 %turn.15 = (bf16[32,4096]{1,0:T(8,128)(2,1)S(1)}, bf16[32,4096]{1,0:T(8,128)(2,1)S(1)}, bf16[5,8,128,1024]{3,2,1,0:T(8,128)(2,1)S(1)}, bf16[5,64,1024]{2,1,0:T(8,128)(2,1)S(1)}) custom-call(s32[10,2]{1,0:T(8,128)S(1)} %copy.103.refs_6_.slots, ...), custom_call_target="tpu_custom_call", output_to_operand_aliasing={{2}: (8, {}), {3}: (9, {})} | custom-call | tf_op jit(solution)/shard_map/turn/pallas_call | solution.py:343
  229.5 9.2 %turn.16 = (bf16[32,4096]{1,0:T(8,128)(2,1)S(1)}, bf16[32,4096]{1,0:T(8,128)(2,1)S(1)}, bf16[5,8,128,1024]{3,2,1,0:T(8,128)(2,1)S(1)}, bf16[5,64,1024]{2,1,0:T(8,128)(2,1)S(1)}) custom-call(s32[10,2]{1,0:T(8,128)S(1)} %copy.103.refs_6_.slots, ...), custom_call_target="tpu_custom_call", output_to_operand_aliasing={{2}: (8, {}), {3}: (9, {})} | custom-call | tf_op jit(solution)/shard_map/turn/pallas_call | solution.py:343
  243.3 9.2 %turn.17 = (bf16[32,4096]{1,0:T(8,128)(2,1)S(1)}, bf16[32,4096]{1,0:T(8,128)(2,1)S(1)}, bf16[5,8,128,1024]{3,2,1,0:T(8,128)(2,1)S(1)}, bf16[5,64,1024]{2,1,0:T(8,128)(2,1)S(1)}) custom-call(s32[10,2]{1,0:T(8,128)S(1)} %copy.103.refs_6_.slots, ...), custom_call_target="tpu_custom_call", output_to_operand_aliasing={{2}: (8, {}), {3}: (9, {})} | custom-call | tf_op jit(solution)/shard_map/turn/pallas_call | solution.py:343
  257.4 9.2 %turn.18 = (bf16[32,4096]{1,0:T(8,128)(2,1)S(1)}, bf16[32,4096]{1,0:T(8,128)(2,1)S(1)}, bf16[5,8,128,1024]{3,2,1,0:T(8,128)(2,1)S(1)}, bf16[5,64,1024]{2,1,0:T(8,128)(2,1)S(1)}) custom-call(s32[10,2]{1,0:T(8,128)S(1)} %copy.103.refs_6_.slots, ...), custom_call_target="tpu_custom_call", output_to_operand_aliasing={{2}: (8, {}), {3}: (9, {})} | custom-call | tf_op jit(solution)/shard_map/turn/pallas_call | solution.py:343
  270.4 9.2 %turn.19 = (bf16[32,4096]{1,0:T(8,128)(2,1)S(1)}, bf16[32,4096]{1,0:T(8,128)(2,1)S(1)}, bf16[5,8,128,1024]{3,2,1,0:T(8,128)(2,1)S(1)}, bf16[5,64,1024]{2,1,0:T(8,128)(2,1)S(1)}) custom-call(s32[10,2]{1,0:T(8,128)S(1)} %copy.103.refs_6_.slots, ...), custom_call_target="tpu_custom_call", output_to_operand_aliasing={{2}: (8, {}), {3}: (9, {})} | custom-call | tf_op jit(solution)/shard_map/turn/pallas_call | solution.py:343
  280.2 11.3 %grads.1 = (bf16[1024,1024]{1,0:T(8,128)(2,1)S(1)}, bf16[1024,1024]{1,0:T(8,128)(2,1)S(1)}, bf16[4096,1024]{1,0:T(8,128)(2,1)S(1)}, bf16[4096,1024]{1,0:T(8,128)(2,1)S(1)}) custom-call(bf16[5,8,128,1024]{3,2,1,0:T(8,128)(2,1)S(1)} %get-tuple-element.191.ds_ref, bf16[4,8,128,1024]{3,2,1,0:T(8,128)(2,1)S(1)} %get-tuple-element.132.refs_6_.p_ref, ...), custom_call_target="tpu_custom_call" | custom-call | tf_op jit(solution)/shard_map/grads/pallas_call | solution.py:398
  291.5 6.1 %back.7 = (bf16[64,4096]{1,0:T(8,128)(2,1)S(1)}, bf16[64,4096]{1,0:T(8,128)(2,1)S(1)}, bf16[64,4096]{1,0:T(8,128)(2,1)S(1)}, bf16[64,4096]{1,0:T(8,128)(2,1)S(1)}) custom-call(bf16[1024,1024]{1,0:T(8,128)(2,1)S(1)} %get-tuple-element.193.kg_ref, bf16[1024,1024]{1,0:T(8,128)(2,1)S(1)} %get-tuple-element.194.vg_ref, ...), custom_call_target="tpu_custom_call" | custom-call | tf_op jit(solution)/shard_map/back/pallas_call | solution.py:439
  297.7 6.1 %back.6 = (bf16[64,4096]{1,0:T(8,128)(2,1)S(1)}, bf16[64,4096]{1,0:T(8,128)(2,1)S(1)}, bf16[64,4096]{1,0:T(8,128)(2,1)S(1)}, bf16[64,4096]{1,0:T(8,128)(2,1)S(1)}) custom-call(bf16[1024,1024]{1,0:T(8,128)(2,1)S(1)} %get-tuple-element.193.kg_ref, bf16[1024,1024]{1,0:T(8,128)(2,1)S(1)} %get-tuple-element.194.vg_ref, ...), custom_call_target="tpu_custom_call" | custom-call | tf_op jit(solution)/shard_map/back/pallas_call | solution.py:439
  303.8 6.1 %back.5 = (bf16[64,4096]{1,0:T(8,128)(2,1)S(1)}, bf16[64,4096]{1,0:T(8,128)(2,1)S(1)}, bf16[64,4096]{1,0:T(8,128)(2,1)S(1)}, bf16[64,4096]{1,0:T(8,128)(2,1)S(1)}) custom-call(bf16[1024,1024]{1,0:T(8,128)(2,1)S(1)} %get-tuple-element.193.kg_ref, bf16[1024,1024]{1,0:T(8,128)(2,1)S(1)} %get-tuple-element.194.vg_ref, ...), custom_call_target="tpu_custom_call" | custom-call | tf_op jit(solution)/shard_map/back/pallas_call | solution.py:439
  313.4 6.1 %back.4 = (bf16[64,4096]{1,0:T(8,128)(2,1)S(1)}, bf16[64,4096]{1,0:T(8,128)(2,1)S(1)}, bf16[64,4096]{1,0:T(8,128)(2,1)S(1)}, bf16[64,4096]{1,0:T(8,128)(2,1)S(1)}) custom-call(bf16[1024,1024]{1,0:T(8,128)(2,1)S(1)} %get-tuple-element.193.kg_ref, bf16[1024,1024]{1,0:T(8,128)(2,1)S(1)} %get-tuple-element.194.vg_ref, bf16[4096,1024]{1,0:T(8,128)(2,1)S(1)} %copy-done.14, ...), custom_call_target="tpu_custom_call" | custom-call | tf_op jit(solution)/shard_map/back/pallas_call | solution.py:439
  326.4 6.0 %collective-permute-start.51 = (bf16[64,4096]{1,0:T(8,128)(2,1)S(1)}, bf16[64,4096]{1,0:T(8,128)(2,1)S(1)}, u32[]{:S(2)}, u32[]{:S(2)}) collective-permute-start(bf16[64,4096]{1,0:T(8,128)(2,1)S(1)} %fusion.3), channel_id=1, source_target_pairs={{0,2},{6,4},{1,3},{7,5},{8,10},{14,12},{9,11},{15,13},{16,18},{22,... | collective-permute-start | bytes 1572872 | tf_op jit(solution)/shard_map/ppermute | solution.py:227
  332.7 11.4 %collective-permute-done.51 = bf16[64,4096]{1,0:T(8,128)(2,1)S(1)} collective-permute-done((bf16[64,4096]{1,0:T(8,128)(2,1)S(1)}, bf16[64,4096]{1,0:T(8,128)(2,1)S(1)}, u32[]{:S(2)}, u32[]{:S(2)}) %collective-permute-start.51) | collective-permute-done | bytes 524320 | tf_op jit(solution)/shard_map/ppermute | solution.py:227
  349.4 9.9 %collective-permute-done.60 = bf16[64,4096]{1,0:T(8,128)(2,1)S(1)} collective-permute-done((bf16[64,4096]{1,0:T(8,128)(2,1)S(1)}, bf16[64,4096]{1,0:T(8,128)(2,1)S(1)}, u32[]{:S(2)}, u32[]{:S(2)}) %collective-permute-start.60) | collective-permute-done | bytes 524320 | tf_op jit(solution)/shard_map/ppermute | solution.py:227
  364.7 8.9 %collective-permute-done.52 = bf16[64,4096]{1,0:T(8,128)(2,1)S(1)} collective-permute-done((bf16[64,4096]{1,0:T(8,128)(2,1)S(1)}, bf16[64,4096]{1,0:T(8,128)(2,1)S(1)}, u32[]{:S(2)}, u32[]{:S(2)}) %collective-permute-start.52) | collective-permute-done | bytes 524320 | tf_op jit(solution)/shard_map/ppermute | solution.py:227
  380.3 12.4 %collective-permute-start.53 = (bf16[64,4096]{1,0:T(8,128)(2,1)S(1)}, bf16[64,4096]{1,0:T(8,128)(2,1)S(1)}, u32[]{:S(2)}, u32[]{:S(2)}) collective-permute-start(bf16[64,4096]{1,0:T(8,128)(2,1)S(1)} %get-tuple-element.227), channel_id=1, source_target_pairs={{0,2},{2,4},{4,6},{1,3},{3,5},{5,7},{8,10},{10,12},{12,14},{9,11},... | collective-permute-start | bytes 1572872 | tf_op jit(solution)/shard_map/ppermute | solution.py:227
  398.5 6.5 %collective-permute-done.53 = bf16[64,4096]{1,0:T(8,128)(2,1)S(1)} collective-permute-done((bf16[64,4096]{1,0:T(8,128)(2,1)S(1)}, bf16[64,4096]{1,0:T(8,128)(2,1)S(1)}, u32[]{:S(2)}, u32[]{:S(2)}) %collective-permute-start.53) | collective-permute-done | bytes 524320 | tf_op jit(solution)/shard_map/ppermute | solution.py:227
  405.2 5.6 %collective-permute-done.63 = bf16[64,4096]{1,0:T(8,128)(2,1)S(1)} collective-permute-done((bf16[64,4096]{1,0:T(8,128)(2,1)S(1)}, bf16[64,4096]{1,0:T(8,128)(2,1)S(1)}, u32[]{:S(2)}, u32[]{:S(2)}) %collective-permute-start.63) | collective-permute-done | bytes 524320 | tf_op jit(solution)/shard_map/ppermute | solution.py:227
  (235 shorter events, 123.4 us)
Async XLA Ops:
  2.0 35.0 %collective-permute-start.19 = (bf16[64,4096]{1,0:T(8,128)(2,1)S(1)}, bf16[64,4096]{1,0:T(8,128)(2,1)S(1)}, u32[]{:S(2)}, u32[]{:S(2)}) collective-permute-start(bf16[64,4096]{1,0:T(8,128)(2,1)S(1)} %get-tuple-element.238.refs_1_), channel_id=1, source_target_pairs={{1,0},{0,1},{3,2},{2,3},{5,4},{4,5},{7,6},{6,7},{9,8},{8,9},{11,10... | collective-permute-start | bytes 1572872 | tf_op jit(solution)/shard_map/ppermute | solution.py:224
  2.6 17.4 %collective-permute-start.8 = (bf16[64,4096]{1,0:T(8,128)(2,1)S(1)}, bf16[64,4096]{1,0:T(8,128)(2,1)}, u32[]{:S(2)}, u32[]{:S(2)}) collective-permute-start(bf16[64,4096]{1,0:T(8,128)(2,1)S(1)} %get-tuple-element.238.refs_1_), channel_id=1, source_target_pairs={{6,4},{4,2},{2,0},{7,5},{5,3},{3,1},{14,12},{12,10},{10,8},{15,13}... | collective-permute-start | bytes 1572872 | tf_op jit(solution)/shard_map/ppermute | solution.py:227
  3.9 17.4 %collective-permute-start.7 = (bf16[64,4096]{1,0:T(8,128)(2,1)S(1)}, bf16[64,4096]{1,0:T(8,128)(2,1)}, u32[]{:S(2)}, u32[]{:S(2)}) collective-permute-start(bf16[64,4096]{1,0:T(8,128)(2,1)S(1)} %get-tuple-element.238.refs_1_), channel_id=1, source_target_pairs={{0,2},{2,4},{4,6},{1,3},{3,5},{5,7},{8,10},{10,12},{12,14},{9,11},... | collective-permute-start | bytes 1572872 | tf_op jit(solution)/shard_map/ppermute | solution.py:227
  9.8 27.8 %collective-permute-start.18 = (bf16[64,4096]{1,0:T(8,128)(2,1)S(1)}, bf16[64,4096]{1,0:T(8,128)(2,1)S(1)}, u32[]{:S(2)}, u32[]{:S(2)}) collective-permute-start(bf16[64,4096]{1,0:T(8,128)(2,1)S(1)} %get-tuple-element.239.refs_0_), channel_id=1, source_target_pairs={{1,0},{0,1},{3,2},{2,3},{5,4},{4,5},{7,6},{6,7},{9,8},{8,9},{11,10... | collective-permute-start | bytes 1572872 | tf_op jit(solution)/shard_map/ppermute | solution.py:224
  10.0 22.1 %collective-permute-start.4 = (bf16[64,4096]{1,0:T(8,128)(2,1)S(1)}, bf16[64,4096]{1,0:T(8,128)(2,1)}, u32[]{:S(2)}, u32[]{:S(2)}) collective-permute-start(bf16[64,4096]{1,0:T(8,128)(2,1)S(1)} %get-tuple-element.239.refs_0_), channel_id=1, source_target_pairs={{0,2},{2,4},{4,6},{1,3},{3,5},{5,7},{8,10},{10,12},{12,14},{9,11},... | collective-permute-start | bytes 1572872 | tf_op jit(solution)/shard_map/ppermute | solution.py:227
  20.0 15.9 %collective-permute-start.2 = (bf16[64,4096]{1,0:T(8,128)(2,1)S(1)}, bf16[64,4096]{1,0:T(8,128)(2,1)S(1)}, u32[]{:S(2)}, u32[]{:S(2)}) collective-permute-start(bf16[64,4096]{1,0:T(8,128)(2,1)S(1)} %get-tuple-element.239.refs_0_), channel_id=1, source_target_pairs={{6,4},{4,2},{2,0},{7,5},{5,3},{3,1},{14,12},{12,10},{10,8},{15,13}... | collective-permute-start | bytes 1572872 | tf_op jit(solution)/shard_map/ppermute | solution.py:227
  21.3 29.2 %collective-permute-start.1 = (bf16[128,4096]{1,0:T(8,128)(2,1)S(1)}, bf16[128,4096]{1,0:T(8,128)(2,1)S(1)}, u32[]{:S(2)}, u32[]{:S(2)}) collective-permute-start(bf16[128,4096]{1,0:T(8,128)(2,1)S(1)} %bitcast.56), channel_id=1, source_target_pairs={{1,0},{0,1},{3,2},{2,3},{5,4},{4,5},{7,6},{6,7},{9,8},{8,9},{11,10... | collective-permute-start | bytes 3145736 | tf_op jit(solution)/shard_map/ppermute | solution.py:224
  32.1 111.1 %collective-permute-start.20 = (bf16[32,4096]{1,0:T(8,128)(2,1)}, bf16[32,4096]{1,0:T(8,128)(2,1)S(1)}, u32[]{:S(2)}, u32[]{:S(2)}) collective-permute-start(bf16[32,4096]{1,0:T(8,128)(2,1)} %get-tuple-element.230.refs_0_.refs_2_), channel_id=1, source_target_pairs={{1,0},{0,1},{3,2},{2,3},{5,4},{4,5},{7,6},{6,7},{9,8},{8,9},{11,10... | collective-permute-start | bytes 786440 | tf_op jit(solution)/shard_map/ppermute | solution.py:224
  35.9 69.9 %collective-permute-start.17 = (bf16[64,4096]{1,0:T(8,128)(2,1)S(1)}, bf16[64,4096]{1,0:T(8,128)(2,1)S(1)}, u32[]{:S(2)}, u32[]{:S(2)}) collective-permute-start(bf16[64,4096]{1,0:T(8,128)(2,1)S(1)} %get-tuple-element.234.refs_1_), channel_id=1, source_target_pairs={{1,0},{0,1},{3,2},{2,3},{5,4},{4,5},{7,6},{6,7},{9,8},{8,9},{11,10... | collective-permute-start | bytes 1572872 | tf_op jit(solution)/shard_map/ppermute | solution.py:224
  37.0 69.4 %collective-permute-start.16 = (bf16[64,4096]{1,0:T(8,128)(2,1)S(1)}, bf16[64,4096]{1,0:T(8,128)(2,1)S(1)}, u32[]{:S(2)}, u32[]{:S(2)}) collective-permute-start(bf16[64,4096]{1,0:T(8,128)(2,1)S(1)} %get-tuple-element.236.refs_0_), channel_id=1, source_target_pairs={{1,0},{0,1},{3,2},{2,3},{5,4},{4,5},{7,6},{6,7},{9,8},{8,9},{11,10... | collective-permute-start | bytes 1572872 | tf_op jit(solution)/shard_map/ppermute | solution.py:224
  37.6 16.0 %collective-permute-start.9 = (bf16[64,4096]{1,0:T(8,128)(2,1)}, bf16[64,4096]{1,0:T(8,128)(2,1)S(1)}, u32[]{:S(2)}, u32[]{:S(2)}) collective-permute-start(bf16[64,4096]{1,0:T(8,128)(2,1)} %collective-permute-done.8), channel_id=1, source_target_pairs={{4,2},{2,0},{5,3},{3,1},{12,10},{10,8},{13,11},{11,9},{20,18},{18,... | collective-permute-start | bytes 1572872 | tf_op jit(solution)/shard_map/ppermute | solution.py:227
  54.4 26.6 %collective-permute-start.3 = (bf16[64,4096]{1,0:T(8,128)(2,1)S(1)}, bf16[64,4096]{1,0:T(8,128)(2,1)S(1)}, u32[]{:S(2)}, u32[]{:S(2)}) collective-permute-start(bf16[64,4096]{1,0:T(8,128)(2,1)S(1)} %collective-permute-done.2), channel_id=1, source_target_pairs={{4,2},{2,0},{5,3},{3,1},{12,10},{10,8},{13,11},{11,9},{20,18},{18,... | collective-permute-start | bytes 1572872 | tf_op jit(solution)/shard_map/ppermute | solution.py:227
  55.8 61.7 %collective-permute-start.15 = (bf16[64,4096]{1,0:T(8,128)(2,1)S(1)}, bf16[64,4096]{1,0:T(8,128)(2,1)S(1)}, u32[]{:S(2)}, u32[]{:S(2)}) collective-permute-start(bf16[64,4096]{1,0:T(8,128)(2,1)S(1)} %broadcast_select_fusion.2.refs_1_), channel_id=1, source_target_pairs={{1,0},{0,1},{3,2},{2,3},{5,4},{4,5},{7,6},{6,7},{9,8},{8,9},{11,10... | collective-permute-start | bytes 1572872 | tf_op jit(solution)/shard_map/ppermute | solution.py:224
  105.9 16.5 %collective-permute-start.13 = (bf16[64,4096]{1,0:T(8,128)(2,1)S(1)}, bf16[64,4096]{1,0:T(8,128)(2,1)S(1)}, u32[]{:S(2)}, u32[]{:S(2)}) collective-permute-start(bf16[64,4096]{1,0:T(8,128)(2,1)S(1)} %broadcast_select_fusion.6.refs_1_), channel_id=1, source_target_pairs={{1,0},{0,1},{3,2},{2,3},{5,4},{4,5},{7,6},{6,7},{9,8},{8,9},{11,10... | collective-permute-start | bytes 1572872 | tf_op jit(solution)/shard_map/ppermute | solution.py:224
  106.4 15.9 %collective-permute-start.12 = (bf16[64,4096]{1,0:T(8,128)(2,1)S(1)}, bf16[64,4096]{1,0:T(8,128)(2,1)S(1)}, u32[]{:S(2)}, u32[]{:S(2)}) collective-permute-start(bf16[64,4096]{1,0:T(8,128)(2,1)S(1)} %broadcast_select_fusion.7.refs_0_), channel_id=1, source_target_pairs={{1,0},{0,1},{3,2},{2,3},{5,4},{4,5},{7,6},{6,7},{9,8},{8,9},{11,10... | collective-permute-start | bytes 1572872 | tf_op jit(solution)/shard_map/ppermute | solution.py:224
  279.6 41.0 %collective-permute-start.46 = (bf16[32,4096]{1,0:T(8,128)(2,1)S(1)}, bf16[32,4096]{1,0:T(8,128)(2,1)S(1)}, u32[]{:S(2)}, u32[]{:S(2)}) collective-permute-start(bf16[32,4096]{1,0:T(8,128)(2,1)S(1)} %get-tuple-element.188), channel_id=1, source_target_pairs={{1,0},{0,1},{3,2},{2,3},{5,4},{4,5},{7,6},{6,7},{9,8},{8,9},{11,10... | collective-permute-start | bytes 786440 | tf_op jit(solution)/shard_map/ppermute | solution.py:224
  319.5 13.0 %collective-permute-start.50 = (bf16[64,4096]{1,0:T(8,128)(2,1)S(1)}, bf16[64,4096]{1,0:T(8,128)(2,1)S(1)}, u32[]{:S(2)}, u32[]{:S(2)}) collective-permute-start(bf16[64,4096]{1,0:T(8,128)(2,1)S(1)} %get-tuple-element.205), channel_id=1, source_target_pairs={{1,0},{0,1},{3,2},{2,3},{5,4},{4,5},{7,6},{6,7},{9,8},{8,9},{11,10... | collective-permute-start | bytes 1572872 | tf_op jit(solution)/shard_map/ppermute | solution.py:224
  319.6 29.1 %collective-permute-start.59 = (bf16[64,4096]{1,0:T(8,128)(2,1)S(1)}, bf16[64,4096]{1,0:T(8,128)(2,1)S(1)}, u32[]{:S(2)}, u32[]{:S(2)}) collective-permute-start(bf16[64,4096]{1,0:T(8,128)(2,1)S(1)} %get-tuple-element.214), channel_id=1, source_target_pairs={{1,0},{0,1},{3,2},{2,3},{5,4},{4,5},{7,6},{6,7},{9,8},{8,9},{11,10... | collective-permute-start | bytes 1572872 | tf_op jit(solution)/shard_map/ppermute | solution.py:224
  320.1 43.8 %collective-permute-start.49 = (bf16[64,4096]{1,0:T(8,128)(2,1)S(1)}, bf16[64,4096]{1,0:T(8,128)(2,1)S(1)}, u32[]{:S(2)}, u32[]{:S(2)}) collective-permute-start(bf16[64,4096]{1,0:T(8,128)(2,1)S(1)} %get-tuple-element.203), channel_id=1, source_target_pairs={{1,0},{0,1},{3,2},{2,3},{5,4},{4,5},{7,6},{6,7},{9,8},{8,9},{11,10... | collective-permute-start | bytes 1572872 | tf_op jit(solution)/shard_map/ppermute | solution.py:224
  320.1 58.8 %collective-permute-start.58 = (bf16[64,4096]{1,0:T(8,128)(2,1)S(1)}, bf16[64,4096]{1,0:T(8,128)(2,1)S(1)}, u32[]{:S(2)}, u32[]{:S(2)}) collective-permute-start(bf16[64,4096]{1,0:T(8,128)(2,1)S(1)} %get-tuple-element.212), channel_id=1, source_target_pairs={{1,0},{0,1},{3,2},{2,3},{5,4},{4,5},{7,6},{6,7},{9,8},{8,9},{11,10... | collective-permute-start | bytes 1572872 | tf_op jit(solution)/shard_map/ppermute | solution.py:224
  326.4 17.7 %collective-permute-start.51 = (bf16[64,4096]{1,0:T(8,128)(2,1)S(1)}, bf16[64,4096]{1,0:T(8,128)(2,1)S(1)}, u32[]{:S(2)}, u32[]{:S(2)}) collective-permute-start(bf16[64,4096]{1,0:T(8,128)(2,1)S(1)} %fusion.3), channel_id=1, source_target_pairs={{0,2},{6,4},{1,3},{7,5},{8,10},{14,12},{9,11},{15,13},{16,18},{22,... | collective-permute-start | bytes 1572872 | tf_op jit(solution)/shard_map/ppermute | solution.py:227
  332.5 64.6 %collective-permute-start.47 = (bf16[64,4096]{1,0:T(8,128)(2,1)S(1)}, bf16[64,4096]{1,0:T(8,128)(2,1)S(1)}, u32[]{:S(2)}, u32[]{:S(2)}) collective-permute-start(bf16[64,4096]{1,0:T(8,128)(2,1)S(1)} %get-tuple-element.198), channel_id=1, source_target_pairs={{1,0},{0,1},{3,2},{2,3},{5,4},{4,5},{7,6},{6,7},{9,8},{8,9},{11,10... | collective-permute-start | bytes 1572872 | tf_op jit(solution)/shard_map/ppermute | solution.py:224
  344.0 15.2 %collective-permute-start.60 = (bf16[64,4096]{1,0:T(8,128)(2,1)S(1)}, bf16[64,4096]{1,0:T(8,128)(2,1)S(1)}, u32[]{:S(2)}, u32[]{:S(2)}) collective-permute-start(bf16[64,4096]{1,0:T(8,128)(2,1)S(1)} %add_convert_fusion.3), channel_id=1, source_target_pairs={{0,2},{6,4},{1,3},{7,5},{8,10},{14,12},{9,11},{15,13},{16,18},{22,... | collective-permute-start | bytes 1572872 | tf_op jit(solution)/shard_map/ppermute | solution.py:227
  348.7 15.3 %collective-permute-start.54 = (bf16[64,4096]{1,0:T(8,128)(2,1)S(1)}, bf16[64,4096]{1,0:T(8,128)(2,1)S(1)}, u32[]{:S(2)}, u32[]{:S(2)}) collective-permute-start(bf16[64,4096]{1,0:T(8,128)(2,1)S(1)} %add_convert_fusion.6), channel_id=1, source_target_pairs={{6,4},{4,2},{7,5},{5,3},{14,12},{12,10},{15,13},{13,11},{22,20},{2... | collective-permute-start | bytes 1572872 | tf_op jit(solution)/shard_map/ppermute | solution.py:227
  359.3 14.4 %collective-permute-start.52 = (bf16[64,4096]{1,0:T(8,128)(2,1)S(1)}, bf16[64,4096]{1,0:T(8,128)(2,1)S(1)}, u32[]{:S(2)}, u32[]{:S(2)}) collective-permute-start(bf16[64,4096]{1,0:T(8,128)(2,1)S(1)} %add_convert_fusion.6), channel_id=1, source_target_pairs={{0,2},{2,4},{1,3},{3,5},{8,10},{10,12},{9,11},{11,13},{16,18},{18,... | collective-permute-start | bytes 1572872 | tf_op jit(solution)/shard_map/ppermute | solution.py:227
  363.9 41.3 %collective-permute-start.56 = (bf16[64,4096]{1,0:T(8,128)(2,1)S(1)}, bf16[64,4096]{1,0:T(8,128)(2,1)S(1)}, u32[]{:S(2)}, u32[]{:S(2)}) collective-permute-start(bf16[64,4096]{1,0:T(8,128)(2,1)S(1)} %get-tuple-element.208), channel_id=1, source_target_pairs={{1,0},{0,1},{3,2},{2,3},{5,4},{4,5},{7,6},{6,7},{9,8},{8,9},{11,10... | collective-permute-start | bytes 1572872 | tf_op jit(solution)/shard_map/ppermute | solution.py:224
  364.0 16.3 %collective-permute-start.62 = (bf16[64,4096]{1,0:T(8,128)(2,1)S(1)}, bf16[64,4096]{1,0:T(8,128)(2,1)S(1)}, u32[]{:S(2)}, u32[]{:S(2)}) collective-permute-start(bf16[64,4096]{1,0:T(8,128)(2,1)S(1)} %add_convert_fusion.2), channel_id=1, source_target_pairs={{6,4},{4,2},{7,5},{5,3},{14,12},{12,10},{15,13},{13,11},{22,20},{2... | collective-permute-start | bytes 1572872 | tf_op jit(solution)/shard_map/ppermute | solution.py:227
  373.6 19.1 %collective-permute-start.61 = (bf16[64,4096]{1,0:T(8,128)(2,1)S(1)}, bf16[64,4096]{1,0:T(8,128)(2,1)S(1)}, u32[]{:S(2)}, u32[]{:S(2)}) collective-permute-start(bf16[64,4096]{1,0:T(8,128)(2,1)S(1)} %add_convert_fusion.2), channel_id=1, source_target_pairs={{0,2},{2,4},{1,3},{3,5},{8,10},{10,12},{9,11},{11,13},{16,18},{18,... | collective-permute-start | bytes 1572872 | tf_op jit(solution)/shard_map/ppermute | solution.py:227
  379.0 19.5 %collective-permute-start.55 = (bf16[64,4096]{1,0:T(8,128)(2,1)S(1)}, bf16[64,4096]{1,0:T(8,128)(2,1)S(1)}, u32[]{:S(2)}, u32[]{:S(2)}) collective-permute-start(bf16[64,4096]{1,0:T(8,128)(2,1)S(1)} %get-tuple-element.226), channel_id=1, source_target_pairs={{6,4},{4,2},{2,0},{7,5},{5,3},{3,1},{14,12},{12,10},{10,8},{15,13}... | collective-permute-start | bytes 1572872 | tf_op jit(solution)/shard_map/ppermute | solution.py:227
  380.3 24.7 %collective-permute-start.53 = (bf16[64,4096]{1,0:T(8,128)(2,1)S(1)}, bf16[64,4096]{1,0:T(8,128)(2,1)S(1)}, u32[]{:S(2)}, u32[]{:S(2)}) collective-permute-start(bf16[64,4096]{1,0:T(8,128)(2,1)S(1)} %get-tuple-element.227), channel_id=1, source_target_pairs={{0,2},{2,4},{4,6},{1,3},{3,5},{5,7},{8,10},{10,12},{12,14},{9,11},... | collective-permute-start | bytes 1572872 | tf_op jit(solution)/shard_map/ppermute | solution.py:227
  393.2 17.6 %collective-permute-start.63 = (bf16[64,4096]{1,0:T(8,128)(2,1)S(1)}, bf16[64,4096]{1,0:T(8,128)(2,1)S(1)}, u32[]{:S(2)}, u32[]{:S(2)}) collective-permute-start(bf16[64,4096]{1,0:T(8,128)(2,1)S(1)} %get-tuple-element.228), channel_id=1, source_target_pairs={{0,2},{2,4},{4,6},{1,3},{3,5},{5,7},{8,10},{10,12},{12,14},{9,11},... | collective-permute-start | bytes 1572872 | tf_op jit(solution)/shard_map/ppermute | solution.py:227
  397.2 13.7 %collective-permute-start.64 = (bf16[64,4096]{1,0:T(8,128)(2,1)S(1)}, bf16[64,4096]{1,0:T(8,128)(2,1)S(1)}, u32[]{:S(2)}, u32[]{:S(2)}) collective-permute-start(bf16[64,4096]{1,0:T(8,128)(2,1)S(1)} %get-tuple-element.229), channel_id=1, source_target_pairs={{6,4},{4,2},{2,0},{7,5},{5,3},{3,1},{14,12},{12,10},{10,8},{15,13}... | collective-permute-start | bytes 1572872 | tf_op jit(solution)/shard_map/ppermute | solution.py:227
  (63 other events, 536.5 us)
